TPU v7x, 512 devices: a whole 4x8x8 slice. The times are simulated.
512 devices in a mesh: group: 64 (over x, y_lo, z), member: 8 (over y_hi, core).
Axes of the slice: x: 4, y: 8 (y_hi: 4, y_lo: 2; y = y_hi * 2 + y_lo), z: 8, core: 2. Of those that a mesh axis runs over, the one named last changes fastest.
Arguments:
- load: float32 [512, 16, 768], P(('group', 'member')), may hold values from -6 to 6
- stiffness: bfloat16 [512, 768, 1024], P(('group', 'member')), as said below
- block_inverse: bfloat16 [512, 768, 1024], P(('group', 'member')), as said below
- deflation: bfloat16 [512, 32, 1024], P(('group', 'member')), may hold values from -0.375 to 0.375
- margin_rows: int32 [512, 4, 64], P(('group', 'member')), may hold values from 0 to 767
- coarse_inverse: bfloat16 [256, 64, 16384], P('member', None, 'group'), as said below
Outputs:
- solution: float32 [512, 16, 768], P(('group', 'member'))
- residual: float32 [512, 16, 768], P(('group', 'member'))
Inputs may be any that keep to these rules, and one draw needn't show every extreme that they name: `margin_rows`: row numbers may repeat within a list. `stiffness`: each row's entry in the column of its own unknown (column i for row i) is the largest entry of the row in magnitude. `block_inverse`: each row's entry in the column of its own unknown is the largest entry of the row in magnitude. `coarse_inverse`: entry [l, h, j] with h * 256 + l == j is the largest entry of its row in magnitude.
All inputs are finite; a program needn't handle non-finite values.
Results may differ from a plain program's by a relative error of at most 0.0085.
Values may be sent and summed in bfloat16 or wider, within the bound.
No kernel may reach another device: no remote copies, remote signals or barrier semaphores. Data moves between devices by JAX's collectives and lax.ppermute only.
A program may use at most 64 MiB of HBM per device.

v0:
```python
import jax
import jax.numpy as jnp
from jax import lax
from jax.sharding import PartitionSpec as P

ITERS = 2


def from_behind(shard, axis, by):
    peers = lax.axis_size(axis)
    return lax.ppermute(shard, axis, [(i, (i + by) % peers) for i in range(peers)])


def local(load, stiffness, block_inverse, deflation, margin_rows, coarse_inverse):
    own_load = load[0]
    stiff_rows = stiffness[0]
    inverse_rows = block_inverse[0]
    basis_rows = deflation[0]
    own_lists = margin_rows[0]
    owned_count = own_load.shape[1]

    def extend(values):
        from_group_lower = from_behind(values, "group", 1)
        from_group_upper = from_behind(values, "group", -1)
        from_member_lower = from_behind(values, "member", 1)
        from_member_upper = from_behind(values, "member", -1)
        pieces = [
            jnp.take(from_group_lower, own_lists[0], axis=1),
            jnp.take(from_group_upper, own_lists[1], axis=1),
            jnp.take(from_member_lower, own_lists[2], axis=1),
            jnp.take(from_member_upper, own_lists[3], axis=1),
        ]
        return jnp.concatenate([values] + pieces, axis=1)

    solution = jnp.zeros_like(own_load)
    residual = own_load
    for step_index in range(ITERS):
        block_values = extend(residual.astype(jnp.bfloat16))
        own_coef = jnp.einsum(
            "cn,kn->ck", block_values, basis_rows, preferred_element_type=jnp.float32
        ).astype(jnp.bfloat16)
        gathered = lax.all_gather(own_coef, "member", axis=1, tiled=True)
        summed = lax.psum_scatter(
            jnp.einsum("lhj,cj->hcl", coarse_inverse, gathered, preferred_element_type=jnp.float32),
            "group",
            scatter_dimension=0,
            tiled=True,
        )
        prolong = summed[0].astype(jnp.bfloat16)
        local_fix = jnp.einsum(
            "cn,un->cu", block_values, inverse_rows, preferred_element_type=jnp.float32
        )
        correction = local_fix + jnp.dot(
            prolong, basis_rows[:, :owned_count], preferred_element_type=jnp.float32
        )
        solution = solution + correction
        solution_block = extend(solution.astype(jnp.bfloat16))
        applied = jnp.einsum(
            "cn,un->cu", solution_block, stiff_rows, preferred_element_type=jnp.float32
        )
        residual = own_load - applied
    return (solution[None], residual[None])


def solution(mesh):
    placed = (
        P(("group", "member"), None, None),
        P(("group", "member"), None, None),
        P(("group", "member"), None, None),
        P(("group", "member"), None, None),
        P(("group", "member"), None, None),
        P("member", None, "group"),
    )
    return jax.shard_map(
        local,
        mesh=mesh,
        in_specs=placed,
        out_specs=(P(("group", "member"), None, None), P(("group", "member"), None, None)),
        check_vma=False,
    )
```

profile of v0, /device:TPU:1, one launch (start us, length us, event | category | flops | bytes accessed | tf_op | source)
XLA Modules:
  0.0 793.8 jit_solution(12968325357086244460)
XLA Ops:
  7.2 1.0 bitcast_convert_fusion
  8.2 8.7 %collective-permute-start.3 = (bf16[16,768]{1,0:T(8,128)(2,1)S(1)}, bf16[16,768]{1,0:T(8,128)(2,1)S(1)}, u32[]{:S(2)}, u32[]{:S(2)}) collective-permute-start(bf16[16,768]{1,0:T(8,128)(2,1)S(1)} %bitcast_convert_fusion), channel_id=1, source_target_pairs={{0,7},{1,0},{2,1},{3,2},{4,3},{5,4},{6,5},{7,6},{8,15},{9,8},{10,9... | collective-permute-start | bytes 73736 | tf_op jit(solution)/shard_map/ppermute | solution.py:11
  16.9 1.9 collective-permute-start.2
  18.9 10.7 %collective-permute-start.1 = (bf16[16,768]{1,0:T(8,128)(2,1)S(1)}, bf16[16,768]{1,0:T(8,128)(2,1)S(1)}, u32[]{:S(2)}, u32[]{:S(2)}) collective-permute-start(bf16[16,768]{1,0:T(8,128)(2,1)S(1)} %bitcast_convert_fusion), channel_id=1, source_target_pairs={{0,504},{8,0},{16,8},{24,16},{32,24},{40,32},{48,40},{56,48},{64,5... | collective-permute-start | bytes 73736 | tf_op jit(solution)/shard_map/ppermute | solution.py:11
  29.6 1.9 collective-permute-start
  31.5 0.8 compare_and_fusion
  32.5 5.9 collective-permute-done
  42.1 1.0 fusion.29
  43.1 16.6 %all-gather = bf16[8,32,16]{1,2,0:T(8,128)(2,1)S(1)} all-gather(bf16[1,32,16]{1,2,0:T(8,128)(2,1)S(1)} %fusion.29), channel_id=1, replica_groups=mesh['group'=64,'member'=8] {'member'}, dimensions={0}, use_global_device_ids=true | all-gather | bytes 9216 | tf_op jit(solution)/shard_map/all_gather | solution.py:42
  60.3 1.1 copy.85
  61.5 260.5 %reduce-scatter.3.cloned.1.call-done = f32[1,16,32]{2,1,0:T(8,128)} async-done(((f32[64,16,32]{2,1,0:T(8,128)}), f32[1,16,32]{2,1,0:T(8,128)}) %reduce-scatter.3.cloned.1.call-update) | async-done | bytes 2064 | tf_op jit(solution)/shard_map/reduce_scatter | solution.py:43
  322.0 0.8 fusion.33
  322.8 1.1 fusion.41
  324.0 1.9 collective-permute-start.4
  325.9 54.7 %collective-permute-start.7 = (bf16[16,768]{1,0:T(8,128)(2,1)S(1)}, bf16[16,768]{1,0:T(8,128)(2,1)S(1)}, u32[]{:S(2)}, u32[]{:S(2)}) collective-permute-start(bf16[16,768]{1,0:T(8,128)(2,1)S(1)} %get-tuple-element.17), channel_id=1, source_target_pairs={{0,7},{1,0},{2,1},{3,2},{4,3},{5,4},{6,5},{7,6},{8,15},{9,8},{10,9... | collective-permute-start | bytes 73736 | tf_op jit(solution)/shard_map/ppermute | solution.py:11
  380.6 3.9 collective-permute-start.6
  384.6 7.9 collective-permute-start.5
  392.4 0.9 copy.86
  394.1 0.9 copy.88
  395.0 0.8 gather_fusion.5
  396.7 0.8 gather_fusion.6
  398.4 0.8 gather_fusion.7
  400.5 1.9 collective-permute-start.8
  402.4 1.9 collective-permute-start.11
  404.3 4.5 collective-permute-start.10
  408.9 7.6 collective-permute-start.9
  416.5 0.9 copy.94
  417.4 0.8 gather_fusion.8
  418.3 0.9 copy.96
  419.2 0.8 gather_fusion.9
  420.9 0.8 gather_fusion.10
  422.6 0.8 gather_fusion.11
  424.2 15.0 %all-gather.1 = bf16[8,32,16]{1,2,0:T(8,128)(2,1)S(1)} all-gather(bf16[1,32,16]{1,2,0:T(8,128)(2,1)S(1)} %fusion.30), channel_id=1, replica_groups=mesh['group'=64,'member'=8] {'member'}, dimensions={0}, use_global_device_ids=true | all-gather | bytes 9216 | tf_op jit(solution)/shard_map/all_gather | solution.py:42
  440.0 1.7 convolution_bitcast_fusion
  441.7 1.1 copy.103
  442.9 266.1 %reduce-scatter.5.cloned.1.call-done = f32[1,16,32]{2,1,0:T(8,128)} async-done(((f32[64,16,32]{2,1,0:T(8,128)}), f32[1,16,32]{2,1,0:T(8,128)}) %reduce-scatter.5.cloned.1.call-update) | async-done | bytes 2064 | tf_op jit(solution)/shard_map/reduce_scatter | solution.py:43
  709.0 0.8 fusion.31
  709.8 1.9 fusion.42
  711.7 1.9 collective-permute-start.12
  713.7 7.6 collective-permute-start.13
  721.2 57.4 %collective-permute-start.14 = (bf16[16,768]{1,0:T(8,128)(2,1)S(1)}, bf16[16,768]{1,0:T(8,128)(2,1)S(1)}, u32[]{:S(2)}, u32[]{:S(2)}) collective-permute-start(bf16[16,768]{1,0:T(8,128)(2,1)S(1)} %get-tuple-element.19), channel_id=1, source_target_pairs={{0,1},{1,2},{2,3},{3,4},{4,5},{5,6},{6,7},{7,0},{8,9},{9,10},{10,1... | collective-permute-start | bytes 73736 | tf_op jit(solution)/shard_map/ppermute | solution.py:11
  778.7 1.9 collective-permute-start.15
  780.8 0.8 gather_fusion.12
  781.8 0.8 gather_fusion.13
  782.8 0.8 gather_fusion.14
  783.6 1.1 collective-permute-done.15
  784.9 0.8 gather_fusion.15
  785.9 1.1 fusion.23
  (116 shorter events, 13.1 us)
Async XLA Ops:
  7.2 315.6 %copy-start = (bf16[1,768,1024]{2,1,0:T(8,128)(2,1)S(1)}, bf16[1,768,1024]{2,1,0:T(8,128)(2,1)}, u32[]{:S(2)}) copy-start(bf16[1,768,1024]{2,1,0:T(8,128)(2,1)} %param.10) | copy-start | bytes 4718596
  7.2 52.6 %copy-start.2 = (bf16[32,64,256]{2,1,0:T(8,128)(2,1)S(1)}, bf16[32,64,256]{2,1,0:T(8,128)(2,1)}, u32[]{:S(2)}) copy-start(bf16[32,64,256]{2,1,0:T(8,128)(2,1)} %param.13) | copy-start | bytes 3145732
  7.2 314.8 %reduce-scatter.3.cloned.1.call-start = ((), (), s32[]{:S(2)}) async-start(), calls=%async_computation.2 | async-start | bytes 532480 | tf_op jit(solution)/shard_map/reduce_scatter | solution.py:43
  8.2 32.9 %collective-permute-start.3 = (bf16[16,768]{1,0:T(8,128)(2,1)S(1)}, bf16[16,768]{1,0:T(8,128)(2,1)S(1)}, u32[]{:S(2)}, u32[]{:S(2)}) collective-permute-start(bf16[16,768]{1,0:T(8,128)(2,1)S(1)} %bitcast_convert_fusion), channel_id=1, source_target_pairs={{0,7},{1,0},{2,1},{3,2},{4,3},{5,4},{6,5},{7,6},{8,15},{9,8},{10,9... | collective-permute-start | bytes 73736 | tf_op jit(solution)/shard_map/ppermute | solution.py:11
  16.9 23.2 %collective-permute-start.2 = (bf16[16,768]{1,0:T(8,128)(2,1)S(1)}, bf16[16,768]{1,0:T(8,128)(2,1)S(1)}, u32[]{:S(2)}, u32[]{:S(2)}) collective-permute-start(bf16[16,768]{1,0:T(8,128)(2,1)S(1)} %bitcast_convert_fusion), channel_id=1, source_target_pairs={{0,1},{1,2},{2,3},{3,4},{4,5},{5,6},{6,7},{7,0},{8,9},{9,10},{10,1... | collective-permute-start | bytes 73736 | tf_op jit(solution)/shard_map/ppermute | solution.py:11
  18.9 20.4 %collective-permute-start.1 = (bf16[16,768]{1,0:T(8,128)(2,1)S(1)}, bf16[16,768]{1,0:T(8,128)(2,1)S(1)}, u32[]{:S(2)}, u32[]{:S(2)}) collective-permute-start(bf16[16,768]{1,0:T(8,128)(2,1)S(1)} %bitcast_convert_fusion), channel_id=1, source_target_pairs={{0,504},{8,0},{16,8},{24,16},{32,24},{40,32},{48,40},{56,48},{64,5... | collective-permute-start | bytes 73736 | tf_op jit(solution)/shard_map/ppermute | solution.py:11
  29.6 8.8 %collective-permute-start = (bf16[16,768]{1,0:T(8,128)(2,1)S(1)}, bf16[16,768]{1,0:T(8,128)(2,1)S(1)}, u32[]{:S(2)}, u32[]{:S(2)}) collective-permute-start(bf16[16,768]{1,0:T(8,128)(2,1)S(1)} %bitcast_convert_fusion), channel_id=1, source_target_pairs={{0,8},{8,16},{16,24},{24,32},{32,40},{40,48},{48,56},{56,64},{64,7... | collective-permute-start | bytes 73736 | tf_op jit(solution)/shard_map/ppermute | solution.py:11
  32.4 29.0 %copy-start.7 = (pred[64]{0:T(512)(128)(4,1)}, pred[64]{0:T(512)(128)(4,1)S(1)}, u32[]{:S(2)}) copy-start(pred[64]{0:T(512)(128)(4,1)S(1)} %get-tuple-element.15) | copy-start | bytes 196
  32.4 29.0 %copy-start.9 = (pred[64]{0:T(512)(128)(4,1)}, pred[64]{0:T(512)(128)(4,1)S(1)}, u32[]{:S(2)}) copy-start(pred[64]{0:T(512)(128)(4,1)S(1)} %get-tuple-element.11) | copy-start | bytes 196
  32.4 29.0 %copy-start.5 = (pred[64]{0:T(512)(128)(4,1)}, pred[64]{0:T(512)(128)(4,1)S(1)}, u32[]{:S(2)}) copy-start(pred[64]{0:T(512)(128)(4,1)S(1)} %get-tuple-element.3) | copy-start | bytes 196
  32.4 361.7 %copy-start.11 = (pred[64]{0:T(512)(128)(4,1)}, pred[64]{0:T(512)(128)(4,1)S(1)}, u32[]{:S(2)}) copy-start(pred[64]{0:T(512)(128)(4,1)S(1)} %get-tuple-element.13) | copy-start | bytes 196
  32.4 28.9 %copy-start.14 = (s32[1024]{0:T(1024)}, s32[1024]{0:T(1024)S(1)}, u32[]{:S(2)}) copy-start(s32[1024]{0:T(1024)S(1)} %pad_clamp_fusion) | copy-start | bytes 12292
  32.4 28.9 %copy-start.16 = (s32[1024]{0:T(1024)}, s32[1024]{0:T(1024)S(1)}, u32[]{:S(2)}) copy-start(s32[1024]{0:T(1024)S(1)} %pad_clamp_fusion.2) | copy-start | bytes 12292
  32.5 360.9 %copy-start.17 = (s32[1024]{0:T(1024)}, s32[1024]{0:T(1024)S(1)}, u32[]{:S(2)}) copy-start(s32[1024]{0:T(1024)S(1)} %pad_clamp_fusion.3) | copy-start | bytes 12292
  32.5 28.9 %copy-start.15 = (s32[1024]{0:T(1024)}, s32[1024]{0:T(1024)S(1)}, u32[]{:S(2)}) copy-start(s32[1024]{0:T(1024)S(1)} %pad_clamp_fusion.1) | copy-start | bytes 12292
  41.3 280.7 %copy-start.3 = (bf16[1,32,1024]{2,1,0:T(8,128)(2,1)S(1)}, bf16[1,32,1024]{2,1,0:T(8,128)(2,1)}, u32[]{:S(2)}) copy-start(bf16[1,32,1024]{2,1,0:T(8,128)(2,1)} %param.11) | copy-start | bytes 196612
  61.4 338.5 %copy-start.1 = (bf16[1,768,1024]{2,1,0:T(8,128)(2,1)S(1)}, bf16[1,768,1024]{2,1,0:T(8,128)(2,1)}, u32[]{:S(2)}) copy-start(bf16[1,768,1024]{2,1,0:T(8,128)(2,1)} %param.9) | copy-start | bytes 4718596
  61.4 338.5 %copy-start.4 = (f32[1,16,768]{2,1,0:T(8,128)S(1)}, f32[1,16,768]{2,1,0:T(8,128)}, u32[]{:S(2)}) copy-start(f32[1,16,768]{2,1,0:T(8,128)} %param.8) | copy-start | bytes 147460
  61.4 647.5 %reduce-scatter.5.cloned.1.call-start = ((), (), s32[]{:S(2)}) async-start(), calls=%async_computation.3 | async-start | bytes 532480 | tf_op jit(solution)/shard_map/reduce_scatter | solution.py:43
  324.0 68.5 %collective-permute-start.4 = (bf16[16,768]{1,0:T(8,128)(2,1)S(1)}, bf16[16,768]{1,0:T(8,128)(2,1)}, u32[]{:S(2)}, u32[]{:S(2)}) collective-permute-start(bf16[16,768]{1,0:T(8,128)(2,1)S(1)} %get-tuple-element.17), channel_id=1, source_target_pairs={{0,8},{8,16},{16,24},{24,32},{32,40},{40,48},{48,56},{56,64},{64,7... | collective-permute-start | bytes 73736 | tf_op jit(solution)/shard_map/ppermute | solution.py:11
  325.9 72.4 %collective-permute-start.7 = (bf16[16,768]{1,0:T(8,128)(2,1)S(1)}, bf16[16,768]{1,0:T(8,128)(2,1)S(1)}, u32[]{:S(2)}, u32[]{:S(2)}) collective-permute-start(bf16[16,768]{1,0:T(8,128)(2,1)S(1)} %get-tuple-element.17), channel_id=1, source_target_pairs={{0,7},{1,0},{2,1},{3,2},{4,3},{5,4},{6,5},{7,6},{8,15},{9,8},{10,9... | collective-permute-start | bytes 73736 | tf_op jit(solution)/shard_map/ppermute | solution.py:11
  380.6 15.9 %collective-permute-start.6 = (bf16[16,768]{1,0:T(8,128)(2,1)S(1)}, bf16[16,768]{1,0:T(8,128)(2,1)S(1)}, u32[]{:S(2)}, u32[]{:S(2)}) collective-permute-start(bf16[16,768]{1,0:T(8,128)(2,1)S(1)} %get-tuple-element.17), channel_id=1, source_target_pairs={{0,1},{1,2},{2,3},{3,4},{4,5},{5,6},{6,7},{7,0},{8,9},{9,10},{10,1... | collective-permute-start | bytes 73736 | tf_op jit(solution)/shard_map/ppermute | solution.py:11
  384.6 9.5 %collective-permute-start.5 = (bf16[16,768]{1,0:T(8,128)(2,1)S(1)}, bf16[16,768]{1,0:T(8,128)(2,1)}, u32[]{:S(2)}, u32[]{:S(2)}) collective-permute-start(bf16[16,768]{1,0:T(8,128)(2,1)S(1)} %get-tuple-element.17), channel_id=1, source_target_pairs={{0,504},{8,0},{16,8},{24,16},{32,24},{40,32},{48,40},{56,48},{64,5... | collective-permute-start | bytes 73736 | tf_op jit(solution)/shard_map/ppermute | solution.py:11
  399.9 18.3 %copy-start.12 = (pred[64]{0:T(512)(128)(4,1)S(1)}, pred[64]{0:T(512)(128)(4,1)}, u32[]{:S(2)}) copy-start(pred[64]{0:T(512)(128)(4,1)} %copy-done.11) | copy-start | bytes 196
  400.5 16.0 %collective-permute-start.8 = (bf16[16,768]{1,0:T(8,128)(2,1)S(1)}, bf16[16,768]{1,0:T(8,128)(2,1)}, u32[]{:S(2)}, u32[]{:S(2)}) collective-permute-start(bf16[16,768]{1,0:T(8,128)(2,1)S(1)} %fusion.26), channel_id=1, source_target_pairs={{0,8},{8,16},{16,24},{24,32},{32,40},{40,48},{48,56},{56,64},{64,7... | collective-permute-start | bytes 73736 | tf_op jit(solution)/shard_map/ppermute | solution.py:11
  402.4 20.0 %collective-permute-start.11 = (bf16[16,768]{1,0:T(8,128)(2,1)S(1)}, bf16[16,768]{1,0:T(8,128)(2,1)S(1)}, u32[]{:S(2)}, u32[]{:S(2)}) collective-permute-start(bf16[16,768]{1,0:T(8,128)(2,1)S(1)} %fusion.26), channel_id=1, source_target_pairs={{0,7},{1,0},{2,1},{3,2},{4,3},{5,4},{6,5},{7,6},{8,15},{9,8},{10,9... | collective-permute-start | bytes 73736 | tf_op jit(solution)/shard_map/ppermute | solution.py:11
  404.3 16.4 %collective-permute-start.10 = (bf16[16,768]{1,0:T(8,128)(2,1)S(1)}, bf16[16,768]{1,0:T(8,128)(2,1)S(1)}, u32[]{:S(2)}, u32[]{:S(2)}) collective-permute-start(bf16[16,768]{1,0:T(8,128)(2,1)S(1)} %fusion.26), channel_id=1, source_target_pairs={{0,1},{1,2},{2,3},{3,4},{4,5},{5,6},{6,7},{7,0},{8,9},{9,10},{10,1... | collective-permute-start | bytes 73736 | tf_op jit(solution)/shard_map/ppermute | solution.py:11
  408.9 9.4 %collective-permute-start.9 = (bf16[16,768]{1,0:T(8,128)(2,1)S(1)}, bf16[16,768]{1,0:T(8,128)(2,1)}, u32[]{:S(2)}, u32[]{:S(2)}) collective-permute-start(bf16[16,768]{1,0:T(8,128)(2,1)S(1)} %fusion.26), channel_id=1, source_target_pairs={{0,504},{8,0},{16,8},{24,16},{32,24},{40,32},{48,40},{56,48},{64,5... | collective-permute-start | bytes 73736 | tf_op jit(solution)/shard_map/ppermute | solution.py:11
  442.8 342.9 %copy-start.10 = (pred[64]{0:T(512)(128)(4,1)S(1)}, pred[64]{0:T(512)(128)(4,1)}, u32[]{:S(2)}) copy-start(pred[64]{0:T(512)(128)(4,1)} %copy-done.9) | copy-start | bytes 196
  442.8 342.9 %copy-start.13 = (pred[64]{0:T(512)(128)(4,1)S(1)}, pred[64]{0:T(512)(128)(4,1)}, u32[]{:S(2)}) copy-start(pred[64]{0:T(512)(128)(4,1)} %copy-done.11) | copy-start | bytes 196
  442.8 342.9 %copy-start.6 = (pred[64]{0:T(512)(128)(4,1)S(1)}, pred[64]{0:T(512)(128)(4,1)}, u32[]{:S(2)}) copy-start(pred[64]{0:T(512)(128)(4,1)} %copy-done.5) | copy-start | bytes 196
  442.9 342.9 %copy-start.8 = (pred[64]{0:T(512)(128)(4,1)S(1)}, pred[64]{0:T(512)(128)(4,1)}, u32[]{:S(2)}) copy-start(pred[64]{0:T(512)(128)(4,1)} %copy-done.7) | copy-start | bytes 196
  711.7 68.8 %collective-permute-start.12 = (bf16[16,768]{1,0:T(8,128)(2,1)S(1)}, bf16[16,768]{1,0:T(8,128)(2,1)S(1)}, u32[]{:S(2)}, u32[]{:S(2)}) collective-permute-start(bf16[16,768]{1,0:T(8,128)(2,1)S(1)} %get-tuple-element.19), channel_id=1, source_target_pairs={{0,8},{8,16},{16,24},{24,32},{32,40},{40,48},{48,56},{56,64},{64,7... | collective-permute-start | bytes 73736 | tf_op jit(solution)/shard_map/ppermute | solution.py:11
  713.7 67.9 %collective-permute-start.13 = (bf16[16,768]{1,0:T(8,128)(2,1)S(1)}, bf16[16,768]{1,0:T(8,128)(2,1)S(1)}, u32[]{:S(2)}, u32[]{:S(2)}) collective-permute-start(bf16[16,768]{1,0:T(8,128)(2,1)S(1)} %get-tuple-element.19), channel_id=1, source_target_pairs={{0,504},{8,0},{16,8},{24,16},{32,24},{40,32},{48,40},{56,48},{64,5... | collective-permute-start | bytes 73736 | tf_op jit(solution)/shard_map/ppermute | solution.py:11
  721.2 61.4 %collective-permute-start.14 = (bf16[16,768]{1,0:T(8,128)(2,1)S(1)}, bf16[16,768]{1,0:T(8,128)(2,1)S(1)}, u32[]{:S(2)}, u32[]{:S(2)}) collective-permute-start(bf16[16,768]{1,0:T(8,128)(2,1)S(1)} %get-tuple-element.19), channel_id=1, source_target_pairs={{0,1},{1,2},{2,3},{3,4},{4,5},{5,6},{6,7},{7,0},{8,9},{9,10},{10,1... | collective-permute-start | bytes 73736 | tf_op jit(solution)/shard_map/ppermute | solution.py:11
  778.7 6.0 collective-permute-start.15
Sparse Core Ops, SparseCore 0:
  61.5 260.4 reduce-scatter.2
  442.9 265.9 reduce-scatter.4
where the time goes:
time: 796 us; the launch traced here: 794 us
  waiting for transfers between devices  534 us (67%)
  starting transfers between devices  177 us (22%)
  blocking collectives  31.6 us (4%)
  local copies, waits for them, and re-layouts  21.8 us (3%)
  between operations  14.6 us (2%)
  matrix products  9.74 us (1%)
    reduce_scatter x2, waiting for transfers between devices, local(): lax.psum_scatter(jnp.einsum('lhj,cj->hcl', coarse_inverse, gathered, pref...  527 us
    ppermute x16, starting transfers between devices, from_behind(): lax.ppermute(shard, axis, [(i, (i + by) % peers) for i in range(peers)])  177 us
    all_gather x2, blocking collectives, local(): gathered = lax.all_gather(own_coef, 'member', axis=1, tiled=True)  31.6 us
  transfers between devices with their start and end apart: 18, of which 4 were waited for; matrix products, arithmetic and copies ran while one was open for 2% of the time, Pallas kernels for 0%

commit v1 on v0

--- a/solution.py
+++ b/solution.py
@@ -40,13 +40,9 @@
             "cn,kn->ck", block_values, basis_rows, preferred_element_type=jnp.float32
         ).astype(jnp.bfloat16)
         gathered = lax.all_gather(own_coef, "member", axis=1, tiled=True)
-        summed = lax.psum_scatter(
-            jnp.einsum("lhj,cj->hcl", coarse_inverse, gathered, preferred_element_type=jnp.float32),
-            "group",
-            scatter_dimension=0,
-            tiled=True,
-        )
-        prolong = summed[0].astype(jnp.bfloat16)
+        shares = jnp.einsum("lhj,cj->hcl", coarse_inverse, gathered, preferred_element_type=jnp.float32)
+        arrived = lax.all_to_all(shares, "group", 0, 0, tiled=True)
+        prolong = jnp.sum(arrived, axis=0).astype(jnp.bfloat16)
         local_fix = jnp.einsum(
             "cn,un->cu", block_values, inverse_rows, preferred_element_type=jnp.float32
         )

time: 796 us -> 186 us (0.23)
  waiting for transfers between devices: 534 us -> 6.2 us
  starting transfers between devices: 177 us -> 71.2 us
  blocking collectives: 31.6 us -> 63.5 us
  between operations: 14.6 us -> 1.23 us
    reduce_scatter x2 -> x0, waiting for transfers between devices: 527 us -> none  [local(): lax.psum_scatter(jnp.einsum('lhj,cj->hcl', coarse_inverse, gathered, pref...]
    ppermute x16, starting transfers between devices: 177 us -> 71.2 us  [from_behind(): lax.ppermute(shard, axis, [(i, (i + by) % peers) for i in range(peers)])]
    all_to_all x0 -> x2, blocking collectives: none -> 31.4 us  [local(): arrived = lax.all_to_all(shares, 'group', 0, 0, tiled=True)]
  transfers between devices with their start and end apart: 18 -> 16, of which waited for: 4 -> 2; matrix products, arithmetic and copies ran while one was open for 2% -> 10% of each run, Pallas kernels for 0% -> 0%
where the time goes in v1:
time: 186 us; the launch traced here: 184 us
  starting transfers between devices  71.2 us (38%)
  blocking collectives  63.5 us (34%)
  local copies, waits for them, and re-layouts  24.3 us (13%)
  other arithmetic  8.75 us (5%)
  matrix products  8.35 us (4%)
  waiting for transfers between devices  6.2 us (3%)
    ppermute x16, starting transfers between devices, from_behind(): lax.ppermute(shard, axis, [(i, (i + by) % peers) for i in range(peers)])  71.2 us
    all_gather x2, blocking collectives, local(): gathered = lax.all_gather(own_coef, 'member', axis=1, tiled=True)  32.1 us
    all_to_all x2, blocking collectives, local(): arrived = lax.all_to_all(shares, 'group', 0, 0, tiled=True)  31.4 us
    ppermute x16, waiting for transfers between devices, from_behind(): lax.ppermute(shard, axis, [(i, (i + by) % peers) for i in range(peers)])  6.2 us
    ppermute x16, local copies, waits for them, and re-layouts, from_behind(): lax.ppermute(shard, axis, [(i, (i + by) % peers) for i in range(peers)])  5.63 us
  transfers between devices with their start and end apart: 16, of which 2 were waited for; matrix products, arithmetic and copies ran while one was open for 10% of the time, Pallas kernels for 0%

profile of v1, /device:TPU:1, one launch (start us, length us, event | category | flops | bytes accessed | tf_op | source)
XLA Modules:
  0.0 183.5 jit_solution(14538968554219266176)
XLA Ops:
  0.7 1.0 bitcast_convert_fusion
  1.6 8.7 %collective-permute-start.3 = (bf16[16,768]{1,0:T(8,128)(2,1)S(1)}, bf16[16,768]{1,0:T(8,128)(2,1)S(1)}, u32[]{:S(2)}, u32[]{:S(2)}) collective-permute-start(bf16[16,768]{1,0:T(8,128)(2,1)S(1)} %bitcast_convert_fusion), channel_id=1, source_target_pairs={{0,7},{1,0},{2,1},{3,2},{4,3},{5,4},{6,5},{7,6},{8,15},{9,8},{10,9... | collective-permute-start | bytes 73736 | tf_op jit(solution)/shard_map/ppermute | solution.py:11
  10.4 1.9 %collective-permute-start.2 = (bf16[16,768]{1,0:T(8,128)(2,1)S(1)}, bf16[16,768]{1,0:T(8,128)(2,1)S(1)}, u32[]{:S(2)}, u32[]{:S(2)}) collective-permute-start(bf16[16,768]{1,0:T(8,128)(2,1)S(1)} %bitcast_convert_fusion), channel_id=1, source_target_pairs={{0,1},{1,2},{2,3},{3,4},{4,5},{5,6},{6,7},{7,0},{8,9},{9,10},{10,1... | collective-permute-start | bytes 73736 | tf_op jit(solution)/shard_map/ppermute | solution.py:11
  12.3 10.7 %collective-permute-start.1 = (bf16[16,768]{1,0:T(8,128)(2,1)S(1)}, bf16[16,768]{1,0:T(8,128)(2,1)S(1)}, u32[]{:S(2)}, u32[]{:S(2)}) collective-permute-start(bf16[16,768]{1,0:T(8,128)(2,1)S(1)} %bitcast_convert_fusion), channel_id=1, source_target_pairs={{0,504},{8,0},{16,8},{24,16},{32,24},{40,32},{48,40},{56,48},{64,5... | collective-permute-start | bytes 73736 | tf_op jit(solution)/shard_map/ppermute | solution.py:11
  23.0 1.9 %collective-permute-start = (bf16[16,768]{1,0:T(8,128)(2,1)S(1)}, bf16[16,768]{1,0:T(8,128)(2,1)S(1)}, u32[]{:S(2)}, u32[]{:S(2)}) collective-permute-start(bf16[16,768]{1,0:T(8,128)(2,1)S(1)} %bitcast_convert_fusion), channel_id=1, source_target_pairs={{0,8},{8,16},{16,24},{24,32},{32,40},{40,48},{48,56},{56,64},{64,7... | collective-permute-start | bytes 73736 | tf_op jit(solution)/shard_map/ppermute | solution.py:11
  24.9 0.8 compare_and_fusion
  25.9 5.9 %collective-permute-done = bf16[16,768]{1,0:T(8,128)(2,1)S(1)} collective-permute-done((bf16[16,768]{1,0:T(8,128)(2,1)S(1)}, bf16[16,768]{1,0:T(8,128)(2,1)S(1)}, u32[]{:S(2)}, u32[]{:S(2)}) %collective-permute-start) | collective-permute-done | bytes 24608 | tf_op jit(solution)/shard_map/ppermute | solution.py:11
  35.5 1.0 fusion.29
  36.5 16.6 %all-gather = bf16[8,32,16]{1,2,0:T(8,128)(2,1)S(1)} all-gather(bf16[1,32,16]{1,2,0:T(8,128)(2,1)S(1)} %fusion.29), channel_id=1, replica_groups=mesh['group'=64,'member'=8] {'member'}, dimensions={0}, use_global_device_ids=true | all-gather | bytes 9216 | tf_op jit(solution)/shard_map/all_gather | solution.py:42
  54.3 13.7 %all_to_all.10 = f32[64,1,512]{2,1,0:T(1,128)S(1)} all-to-all(f32[64,1,512]{2,1,0:T(1,128)S(1)} %reshape.201), channel_id=1, replica_groups=mesh['group'=64,'member'=8] {'group'}, dimensions={0} | all-to-all | bytes 262144 | tf_op jit(solution)/shard_map/all_to_all | solution.py:44
  68.5 0.9 reduce
  69.8 1.1 fusion.39
  70.9 2.2 %collective-permute-start.4 = (bf16[16,768]{1,0:T(8,128)(2,1)S(1)}, bf16[16,768]{1,0:T(8,128)(2,1)}, u32[]{:S(2)}, u32[]{:S(2)}) collective-permute-start(bf16[16,768]{1,0:T(8,128)(2,1)S(1)} %get-tuple-element.17), channel_id=1, source_target_pairs={{0,8},{8,16},{16,24},{24,32},{32,40},{40,48},{48,56},{56,64},{64,7... | collective-permute-start | bytes 73736 | tf_op jit(solution)/shard_map/ppermute | solution.py:11
  73.2 3.9 %collective-permute-start.7 = (bf16[16,768]{1,0:T(8,128)(2,1)S(1)}, bf16[16,768]{1,0:T(8,128)(2,1)S(1)}, u32[]{:S(2)}, u32[]{:S(2)}) collective-permute-start(bf16[16,768]{1,0:T(8,128)(2,1)S(1)} %get-tuple-element.17), channel_id=1, source_target_pairs={{0,7},{1,0},{2,1},{3,2},{4,3},{5,4},{6,5},{7,6},{8,15},{9,8},{10,9... | collective-permute-start | bytes 73736 | tf_op jit(solution)/shard_map/ppermute | solution.py:11
  77.1 2.6 %collective-permute-start.6 = (bf16[16,768]{1,0:T(8,128)(2,1)S(1)}, bf16[16,768]{1,0:T(8,128)(2,1)S(1)}, u32[]{:S(2)}, u32[]{:S(2)}) collective-permute-start(bf16[16,768]{1,0:T(8,128)(2,1)S(1)} %get-tuple-element.17), channel_id=1, source_target_pairs={{0,1},{1,2},{2,3},{3,4},{4,5},{5,6},{6,7},{7,0},{8,9},{9,10},{10,1... | collective-permute-start | bytes 73736 | tf_op jit(solution)/shard_map/ppermute | solution.py:11
  79.6 7.2 %collective-permute-start.5 = (bf16[16,768]{1,0:T(8,128)(2,1)S(1)}, bf16[16,768]{1,0:T(8,128)(2,1)}, u32[]{:S(2)}, u32[]{:S(2)}) collective-permute-start(bf16[16,768]{1,0:T(8,128)(2,1)S(1)} %get-tuple-element.17), channel_id=1, source_target_pairs={{0,504},{8,0},{16,8},{24,16},{32,24},{40,32},{48,40},{56,48},{64,5... | collective-permute-start | bytes 73736 | tf_op jit(solution)/shard_map/ppermute | solution.py:11
  86.9 0.9 copy.84
  88.6 0.9 copy.86
  89.5 0.8 gather_fusion.5
  91.1 0.8 gather_fusion.6
  92.8 0.8 gather_fusion.7
  94.9 1.9 %collective-permute-start.8 = (bf16[16,768]{1,0:T(8,128)(2,1)S(1)}, bf16[16,768]{1,0:T(8,128)(2,1)}, u32[]{:S(2)}, u32[]{:S(2)}) collective-permute-start(bf16[16,768]{1,0:T(8,128)(2,1)S(1)} %fusion.26), channel_id=1, source_target_pairs={{0,8},{8,16},{16,24},{24,32},{32,40},{40,48},{48,56},{56,64},{64,7... | collective-permute-start | bytes 73736 | tf_op jit(solution)/shard_map/ppermute | solution.py:11
  96.8 1.9 %collective-permute-start.11 = (bf16[16,768]{1,0:T(8,128)(2,1)S(1)}, bf16[16,768]{1,0:T(8,128)(2,1)S(1)}, u32[]{:S(2)}, u32[]{:S(2)}) collective-permute-start(bf16[16,768]{1,0:T(8,128)(2,1)S(1)} %fusion.26), channel_id=1, source_target_pairs={{0,7},{1,0},{2,1},{3,2},{4,3},{5,4},{6,5},{7,6},{8,15},{9,8},{10,9... | collective-permute-start | bytes 73736 | tf_op jit(solution)/shard_map/ppermute | solution.py:11
  98.8 4.5 %collective-permute-start.10 = (bf16[16,768]{1,0:T(8,128)(2,1)S(1)}, bf16[16,768]{1,0:T(8,128)(2,1)S(1)}, u32[]{:S(2)}, u32[]{:S(2)}) collective-permute-start(bf16[16,768]{1,0:T(8,128)(2,1)S(1)} %fusion.26), channel_id=1, source_target_pairs={{0,1},{1,2},{2,3},{3,4},{4,5},{5,6},{6,7},{7,0},{8,9},{9,10},{10,1... | collective-permute-start | bytes 73736 | tf_op jit(solution)/shard_map/ppermute | solution.py:11
  103.3 7.6 %collective-permute-start.9 = (bf16[16,768]{1,0:T(8,128)(2,1)S(1)}, bf16[16,768]{1,0:T(8,128)(2,1)}, u32[]{:S(2)}, u32[]{:S(2)}) collective-permute-start(bf16[16,768]{1,0:T(8,128)(2,1)S(1)} %fusion.26), channel_id=1, source_target_pairs={{0,504},{8,0},{16,8},{24,16},{32,24},{40,32},{48,40},{56,48},{64,5... | collective-permute-start | bytes 73736 | tf_op jit(solution)/shard_map/ppermute | solution.py:11
  110.9 0.9 copy.92
  111.8 0.8 gather_fusion.8
  112.7 0.9 copy.94
  113.6 0.8 gather_fusion.9
  115.3 0.8 gather_fusion.10
  117.0 0.8 gather_fusion.11
  118.7 15.6 %all-gather.1 = bf16[8,32,16]{1,2,0:T(8,128)(2,1)S(1)} all-gather(bf16[1,32,16]{1,2,0:T(8,128)(2,1)S(1)} %fusion.30), channel_id=1, replica_groups=mesh['group'=64,'member'=8] {'member'}, dimensions={0}, use_global_device_ids=true | all-gather | bytes 9216 | tf_op jit(solution)/shard_map/all_gather | solution.py:42
  134.9 1.7 convolution_bitcast_fusion
  136.7 1.1 copy.101
  137.8 1.3 reshape.203
  139.1 17.8 %all_to_all.11 = f32[64,1,512]{2,1,0:T(1,128)S(1)} all-to-all(f32[64,1,512]{2,1,0:T(1,128)S(1)} %reshape.203), channel_id=1, replica_groups=mesh['group'=64,'member'=8] {'group'}, dimensions={0} | all-to-all | bytes 262144 | tf_op jit(solution)/shard_map/all_to_all | solution.py:44
  156.8 0.9 reduce.1
  157.7 1.0 reshape.204
  158.7 1.1 reduce_sum.19
  160.0 1.9 %fusion.40 = (bf16[16,768]{1,0:T(8,128)(2,1)S(1)}, f32[16,768]{1,0:T(8,128)}) fusion(f32[16,768]{1,0:T(8,128)} %get-tuple-element.18, f32[16,768]{1,0:T(8,128)S(1)} %fusion.31, bf16[16,1024]{1,0:T(8,128)(2,1)S(1)} %concatenate.14, bf16[1,768,1024]{2,1,0:T(8,128)(2,1)S(1)} %copy-done), kind=kOutput, calls=%fused_computation.75 | convolution fusion | flops 25202688 | bytes 1777664 | tf_op jit(solution)/shard_map/cn,un->cu/dot_general | solution.py:46
  161.9 2.5 %collective-permute-start.12 = (bf16[16,768]{1,0:T(8,128)(2,1)S(1)}, bf16[16,768]{1,0:T(8,128)(2,1)S(1)}, u32[]{:S(2)}, u32[]{:S(2)}) collective-permute-start(bf16[16,768]{1,0:T(8,128)(2,1)S(1)} %get-tuple-element.19), channel_id=1, source_target_pairs={{0,8},{8,16},{16,24},{24,32},{32,40},{40,48},{48,56},{56,64},{64,7... | collective-permute-start | bytes 73736 | tf_op jit(solution)/shard_map/ppermute | solution.py:11
  164.4 7.0 %collective-permute-start.13 = (bf16[16,768]{1,0:T(8,128)(2,1)S(1)}, bf16[16,768]{1,0:T(8,128)(2,1)S(1)}, u32[]{:S(2)}, u32[]{:S(2)}) collective-permute-start(bf16[16,768]{1,0:T(8,128)(2,1)S(1)} %get-tuple-element.19), channel_id=1, source_target_pairs={{0,504},{8,0},{16,8},{24,16},{32,24},{40,32},{48,40},{56,48},{64,5... | collective-permute-start | bytes 73736 | tf_op jit(solution)/shard_map/ppermute | solution.py:11
  171.4 3.7 %collective-permute-start.14 = (bf16[16,768]{1,0:T(8,128)(2,1)S(1)}, bf16[16,768]{1,0:T(8,128)(2,1)S(1)}, u32[]{:S(2)}, u32[]{:S(2)}) collective-permute-start(bf16[16,768]{1,0:T(8,128)(2,1)S(1)} %get-tuple-element.19), channel_id=1, source_target_pairs={{0,1},{1,2},{2,3},{3,4},{4,5},{5,6},{6,7},{7,0},{8,9},{9,10},{10,1... | collective-permute-start | bytes 73736 | tf_op jit(solution)/shard_map/ppermute | solution.py:11
  175.2 2.7 %collective-permute-start.15 = (bf16[16,768]{1,0:T(8,128)(2,1)S(1)}, bf16[16,768]{1,0:T(8,128)(2,1)S(1)}, u32[]{:S(2)}, u32[]{:S(2)}) collective-permute-start(bf16[16,768]{1,0:T(8,128)(2,1)S(1)} %get-tuple-element.19), channel_id=1, source_target_pairs={{0,7},{1,0},{2,1},{3,2},{4,3},{5,4},{6,5},{7,6},{8,15},{9,8},{10,9... | collective-permute-start | bytes 73736 | tf_op jit(solution)/shard_map/ppermute | solution.py:11
  178.0 0.8 gather_fusion.12
  180.1 0.8 gather_fusion.14
  181.4 0.8 gather_fusion.15
  182.4 1.1 fusion.23
  (121 shorter events, 15.5 us)
Async XLA Ops:
  0.6 69.1 %copy-start = (bf16[1,768,1024]{2,1,0:T(8,128)(2,1)S(1)}, bf16[1,768,1024]{2,1,0:T(8,128)(2,1)}, u32[]{:S(2)}) copy-start(bf16[1,768,1024]{2,1,0:T(8,128)(2,1)} %param.10) | copy-start | bytes 4718596
  0.6 52.5 %copy-start.2 = (bf16[32,64,256]{2,1,0:T(8,128)(2,1)S(1)}, bf16[32,64,256]{2,1,0:T(8,128)(2,1)}, u32[]{:S(2)}) copy-start(bf16[32,64,256]{2,1,0:T(8,128)(2,1)} %param.13) | copy-start | bytes 3145732
  1.6 32.9 %collective-permute-start.3 = (bf16[16,768]{1,0:T(8,128)(2,1)S(1)}, bf16[16,768]{1,0:T(8,128)(2,1)S(1)}, u32[]{:S(2)}, u32[]{:S(2)}) collective-permute-start(bf16[16,768]{1,0:T(8,128)(2,1)S(1)} %bitcast_convert_fusion), channel_id=1, source_target_pairs={{0,7},{1,0},{2,1},{3,2},{4,3},{5,4},{6,5},{7,6},{8,15},{9,8},{10,9... | collective-permute-start | bytes 73736 | tf_op jit(solution)/shard_map/ppermute | solution.py:11
  10.4 23.2 %collective-permute-start.2 = (bf16[16,768]{1,0:T(8,128)(2,1)S(1)}, bf16[16,768]{1,0:T(8,128)(2,1)S(1)}, u32[]{:S(2)}, u32[]{:S(2)}) collective-permute-start(bf16[16,768]{1,0:T(8,128)(2,1)S(1)} %bitcast_convert_fusion), channel_id=1, source_target_pairs={{0,1},{1,2},{2,3},{3,4},{4,5},{5,6},{6,7},{7,0},{8,9},{9,10},{10,1... | collective-permute-start | bytes 73736 | tf_op jit(solution)/shard_map/ppermute | solution.py:11
  12.3 20.4 %collective-permute-start.1 = (bf16[16,768]{1,0:T(8,128)(2,1)S(1)}, bf16[16,768]{1,0:T(8,128)(2,1)S(1)}, u32[]{:S(2)}, u32[]{:S(2)}) collective-permute-start(bf16[16,768]{1,0:T(8,128)(2,1)S(1)} %bitcast_convert_fusion), channel_id=1, source_target_pairs={{0,504},{8,0},{16,8},{24,16},{32,24},{40,32},{48,40},{56,48},{64,5... | collective-permute-start | bytes 73736 | tf_op jit(solution)/shard_map/ppermute | solution.py:11
  23.0 8.8 %collective-permute-start = (bf16[16,768]{1,0:T(8,128)(2,1)S(1)}, bf16[16,768]{1,0:T(8,128)(2,1)S(1)}, u32[]{:S(2)}, u32[]{:S(2)}) collective-permute-start(bf16[16,768]{1,0:T(8,128)(2,1)S(1)} %bitcast_convert_fusion), channel_id=1, source_target_pairs={{0,8},{8,16},{16,24},{24,32},{32,40},{40,48},{48,56},{56,64},{64,7... | collective-permute-start | bytes 73736 | tf_op jit(solution)/shard_map/ppermute | solution.py:11
  25.8 28.2 %copy-start.5 = (pred[64]{0:T(512)(128)(4,1)}, pred[64]{0:T(512)(128)(4,1)S(1)}, u32[]{:S(2)}) copy-start(pred[64]{0:T(512)(128)(4,1)S(1)} %get-tuple-element.3) | copy-start | bytes 196
  25.8 28.2 %copy-start.7 = (pred[64]{0:T(512)(128)(4,1)}, pred[64]{0:T(512)(128)(4,1)S(1)}, u32[]{:S(2)}) copy-start(pred[64]{0:T(512)(128)(4,1)S(1)} %get-tuple-element.15) | copy-start | bytes 196
  25.8 28.2 %copy-start.9 = (pred[64]{0:T(512)(128)(4,1)}, pred[64]{0:T(512)(128)(4,1)S(1)}, u32[]{:S(2)}) copy-start(pred[64]{0:T(512)(128)(4,1)S(1)} %get-tuple-element.11) | copy-start | bytes 196
  25.8 62.7 %copy-start.11 = (pred[64]{0:T(512)(128)(4,1)}, pred[64]{0:T(512)(128)(4,1)S(1)}, u32[]{:S(2)}) copy-start(pred[64]{0:T(512)(128)(4,1)S(1)} %get-tuple-element.13) | copy-start | bytes 196
  25.8 28.2 %copy-start.14 = (s32[1024]{0:T(1024)}, s32[1024]{0:T(1024)S(1)}, u32[]{:S(2)}) copy-start(s32[1024]{0:T(1024)S(1)} %pad_clamp_fusion) | copy-start | bytes 12292
  25.9 28.2 %copy-start.16 = (s32[1024]{0:T(1024)}, s32[1024]{0:T(1024)S(1)}, u32[]{:S(2)}) copy-start(s32[1024]{0:T(1024)S(1)} %pad_clamp_fusion.2) | copy-start | bytes 12292
  25.9 61.9 %copy-start.17 = (s32[1024]{0:T(1024)}, s32[1024]{0:T(1024)S(1)}, u32[]{:S(2)}) copy-start(s32[1024]{0:T(1024)S(1)} %pad_clamp_fusion.3) | copy-start | bytes 12292
  25.9 28.2 %copy-start.15 = (s32[1024]{0:T(1024)}, s32[1024]{0:T(1024)S(1)}, u32[]{:S(2)}) copy-start(s32[1024]{0:T(1024)S(1)} %pad_clamp_fusion.1) | copy-start | bytes 12292
  53.7 15.9 %copy-start.3 = (bf16[1,32,1024]{2,1,0:T(8,128)(2,1)S(1)}, bf16[1,32,1024]{2,1,0:T(8,128)(2,1)}, u32[]{:S(2)}) copy-start(bf16[1,32,1024]{2,1,0:T(8,128)(2,1)} %param.11) | copy-start | bytes 196612
  69.6 24.8 %copy-start.1 = (bf16[1,768,1024]{2,1,0:T(8,128)(2,1)S(1)}, bf16[1,768,1024]{2,1,0:T(8,128)(2,1)}, u32[]{:S(2)}) copy-start(bf16[1,768,1024]{2,1,0:T(8,128)(2,1)} %param.9) | copy-start | bytes 4718596
  69.6 24.8 %copy-start.4 = (f32[1,16,768]{2,1,0:T(8,128)S(1)}, f32[1,16,768]{2,1,0:T(8,128)}, u32[]{:S(2)}) copy-start(f32[1,16,768]{2,1,0:T(8,128)} %param.8) | copy-start | bytes 147460
  70.9 16.0 %collective-permute-start.4 = (bf16[16,768]{1,0:T(8,128)(2,1)S(1)}, bf16[16,768]{1,0:T(8,128)(2,1)}, u32[]{:S(2)}, u32[]{:S(2)}) collective-permute-start(bf16[16,768]{1,0:T(8,128)(2,1)S(1)} %get-tuple-element.17), channel_id=1, source_target_pairs={{0,8},{8,16},{16,24},{24,32},{32,40},{40,48},{48,56},{56,64},{64,7... | collective-permute-start | bytes 73736 | tf_op jit(solution)/shard_map/ppermute | solution.py:11
  73.2 19.5 %collective-permute-start.7 = (bf16[16,768]{1,0:T(8,128)(2,1)S(1)}, bf16[16,768]{1,0:T(8,128)(2,1)S(1)}, u32[]{:S(2)}, u32[]{:S(2)}) collective-permute-start(bf16[16,768]{1,0:T(8,128)(2,1)S(1)} %get-tuple-element.17), channel_id=1, source_target_pairs={{0,7},{1,0},{2,1},{3,2},{4,3},{5,4},{6,5},{7,6},{8,15},{9,8},{10,9... | collective-permute-start | bytes 73736 | tf_op jit(solution)/shard_map/ppermute | solution.py:11
  77.1 13.9 %collective-permute-start.6 = (bf16[16,768]{1,0:T(8,128)(2,1)S(1)}, bf16[16,768]{1,0:T(8,128)(2,1)S(1)}, u32[]{:S(2)}, u32[]{:S(2)}) collective-permute-start(bf16[16,768]{1,0:T(8,128)(2,1)S(1)} %get-tuple-element.17), channel_id=1, source_target_pairs={{0,1},{1,2},{2,3},{3,4},{4,5},{5,6},{6,7},{7,0},{8,9},{9,10},{10,1... | collective-permute-start | bytes 73736 | tf_op jit(solution)/shard_map/ppermute | solution.py:11
  79.6 8.9 %collective-permute-start.5 = (bf16[16,768]{1,0:T(8,128)(2,1)S(1)}, bf16[16,768]{1,0:T(8,128)(2,1)}, u32[]{:S(2)}, u32[]{:S(2)}) collective-permute-start(bf16[16,768]{1,0:T(8,128)(2,1)S(1)} %get-tuple-element.17), channel_id=1, source_target_pairs={{0,504},{8,0},{16,8},{24,16},{32,24},{40,32},{48,40},{56,48},{64,5... | collective-permute-start | bytes 73736 | tf_op jit(solution)/shard_map/ppermute | solution.py:11
  94.4 18.3 %copy-start.12 = (pred[64]{0:T(512)(128)(4,1)S(1)}, pred[64]{0:T(512)(128)(4,1)}, u32[]{:S(2)}) copy-start(pred[64]{0:T(512)(128)(4,1)} %copy-done.11) | copy-start | bytes 196
  94.9 16.0 %collective-permute-start.8 = (bf16[16,768]{1,0:T(8,128)(2,1)S(1)}, bf16[16,768]{1,0:T(8,128)(2,1)}, u32[]{:S(2)}, u32[]{:S(2)}) collective-permute-start(bf16[16,768]{1,0:T(8,128)(2,1)S(1)} %fusion.26), channel_id=1, source_target_pairs={{0,8},{8,16},{16,24},{24,32},{32,40},{40,48},{48,56},{56,64},{64,7... | collective-permute-start | bytes 73736 | tf_op jit(solution)/shard_map/ppermute | solution.py:11
  96.8 20.0 %collective-permute-start.11 = (bf16[16,768]{1,0:T(8,128)(2,1)S(1)}, bf16[16,768]{1,0:T(8,128)(2,1)S(1)}, u32[]{:S(2)}, u32[]{:S(2)}) collective-permute-start(bf16[16,768]{1,0:T(8,128)(2,1)S(1)} %fusion.26), channel_id=1, source_target_pairs={{0,7},{1,0},{2,1},{3,2},{4,3},{5,4},{6,5},{7,6},{8,15},{9,8},{10,9... | collective-permute-start | bytes 73736 | tf_op jit(solution)/shard_map/ppermute | solution.py:11
  98.8 16.3 %collective-permute-start.10 = (bf16[16,768]{1,0:T(8,128)(2,1)S(1)}, bf16[16,768]{1,0:T(8,128)(2,1)S(1)}, u32[]{:S(2)}, u32[]{:S(2)}) collective-permute-start(bf16[16,768]{1,0:T(8,128)(2,1)S(1)} %fusion.26), channel_id=1, source_target_pairs={{0,1},{1,2},{2,3},{3,4},{4,5},{5,6},{6,7},{7,0},{8,9},{9,10},{10,1... | collective-permute-start | bytes 73736 | tf_op jit(solution)/shard_map/ppermute | solution.py:11
  103.3 9.4 %collective-permute-start.9 = (bf16[16,768]{1,0:T(8,128)(2,1)S(1)}, bf16[16,768]{1,0:T(8,128)(2,1)}, u32[]{:S(2)}, u32[]{:S(2)}) collective-permute-start(bf16[16,768]{1,0:T(8,128)(2,1)S(1)} %fusion.26), channel_id=1, source_target_pairs={{0,504},{8,0},{16,8},{24,16},{32,24},{40,32},{48,40},{56,48},{64,5... | collective-permute-start | bytes 73736 | tf_op jit(solution)/shard_map/ppermute | solution.py:11
  159.8 22.4 %copy-start.10 = (pred[64]{0:T(512)(128)(4,1)S(1)}, pred[64]{0:T(512)(128)(4,1)}, u32[]{:S(2)}) copy-start(pred[64]{0:T(512)(128)(4,1)} %copy-done.9) | copy-start | bytes 196
  159.8 22.4 %copy-start.13 = (pred[64]{0:T(512)(128)(4,1)S(1)}, pred[64]{0:T(512)(128)(4,1)}, u32[]{:S(2)}) copy-start(pred[64]{0:T(512)(128)(4,1)} %copy-done.11) | copy-start | bytes 196
  159.8 22.4 %copy-start.6 = (pred[64]{0:T(512)(128)(4,1)S(1)}, pred[64]{0:T(512)(128)(4,1)}, u32[]{:S(2)}) copy-start(pred[64]{0:T(512)(128)(4,1)} %copy-done.5) | copy-start | bytes 196
  159.8 22.4 %copy-start.8 = (pred[64]{0:T(512)(128)(4,1)S(1)}, pred[64]{0:T(512)(128)(4,1)}, u32[]{:S(2)}) copy-start(pred[64]{0:T(512)(128)(4,1)} %copy-done.7) | copy-start | bytes 196
  161.9 15.9 %collective-permute-start.12 = (bf16[16,768]{1,0:T(8,128)(2,1)S(1)}, bf16[16,768]{1,0:T(8,128)(2,1)S(1)}, u32[]{:S(2)}, u32[]{:S(2)}) collective-permute-start(bf16[16,768]{1,0:T(8,128)(2,1)S(1)} %get-tuple-element.19), channel_id=1, source_target_pairs={{0,8},{8,16},{16,24},{24,32},{32,40},{40,48},{48,56},{56,64},{64,7... | collective-permute-start | bytes 73736 | tf_op jit(solution)/shard_map/ppermute | solution.py:11
  164.4 14.5 %collective-permute-start.13 = (bf16[16,768]{1,0:T(8,128)(2,1)S(1)}, bf16[16,768]{1,0:T(8,128)(2,1)S(1)}, u32[]{:S(2)}, u32[]{:S(2)}) collective-permute-start(bf16[16,768]{1,0:T(8,128)(2,1)S(1)} %get-tuple-element.19), channel_id=1, source_target_pairs={{0,504},{8,0},{16,8},{24,16},{32,24},{40,32},{48,40},{56,48},{64,5... | collective-permute-start | bytes 73736 | tf_op jit(solution)/shard_map/ppermute | solution.py:11
  171.4 8.5 %collective-permute-start.14 = (bf16[16,768]{1,0:T(8,128)(2,1)S(1)}, bf16[16,768]{1,0:T(8,128)(2,1)S(1)}, u32[]{:S(2)}, u32[]{:S(2)}) collective-permute-start(bf16[16,768]{1,0:T(8,128)(2,1)S(1)} %get-tuple-element.19), channel_id=1, source_target_pairs={{0,1},{1,2},{2,3},{3,4},{4,5},{5,6},{6,7},{7,0},{8,9},{9,10},{10,1... | collective-permute-start | bytes 73736 | tf_op jit(solution)/shard_map/ppermute | solution.py:11
  175.2 6.0 %collective-permute-start.15 = (bf16[16,768]{1,0:T(8,128)(2,1)S(1)}, bf16[16,768]{1,0:T(8,128)(2,1)S(1)}, u32[]{:S(2)}, u32[]{:S(2)}) collective-permute-start(bf16[16,768]{1,0:T(8,128)(2,1)S(1)} %get-tuple-element.19), channel_id=1, source_target_pairs={{0,7},{1,0},{2,1},{3,2},{4,3},{5,4},{6,5},{7,6},{8,15},{9,8},{10,9... | collective-permute-start | bytes 73736 | tf_op jit(solution)/shard_map/ppermute | solution.py:11

commit v2 on v1

v2 whole, which is shorter than its diff:
```python
import jax
import jax.numpy as jnp
from jax import lax
from jax.experimental import pallas as pl
from jax.experimental.pallas import tpu as pltpu
from jax.sharding import PartitionSpec as P

ITERS = 2
LANES = 128
F32 = jnp.float32
BF16 = jnp.bfloat16
VMEM = pltpu.VMEM


def from_behind(shard, axis, by):
    peers = lax.axis_size(axis)
    return lax.ppermute(shard, axis, [(i, (i + by) % peers) for i in range(peers)])


def call(body, outs, *args):
    return pl.pallas_call(
        body,
        out_shape=[jax.ShapeDtypeStruct(shape, dtype) for shape, dtype in outs],
        in_specs=[pl.BlockSpec(memory_space=VMEM)] * len(args),
        out_specs=[pl.BlockSpec(memory_space=VMEM)] * len(outs),
        compiler_params=pltpu.CompilerParams(vmem_limit_bytes=16 * 2**20),
    )(*args)


def dot_nt(left, right):
    return lax.dot_general(left, right, (((1,), (1,)), ((), ())), preferred_element_type=F32)


def dot_nn(left, right):
    return jnp.dot(left, right, preferred_element_type=F32)


def margins(fields, picks):
    cases = fields[0].shape[0]
    width = picks.shape[1] // len(fields)
    every = dot_nn(jnp.concatenate(fields, axis=0), picks)
    owner = lax.broadcasted_iota(jnp.int32, (cases, picks.shape[1]), 1) // width
    kept = every[:cases]
    for d in range(1, len(fields)):
        kept = jnp.where(owner == d, every[d * cases : (d + 1) * cases], kept)
    return kept.astype(BF16)


def restrict_body(v, f0, f1, f2, f3, picks, basis, block, coef):
    edge = margins([f0[...], f1[...], f2[...], f3[...]], picks[...])
    whole = jnp.concatenate([v[...], edge], axis=1)
    block[...] = whole
    tall = jnp.concatenate([whole] * (LANES // whole.shape[0]), axis=0)
    part = dot_nt(basis[...], tall).astype(BF16)
    for m in range(coef.shape[0]):
        coef[m] = part


def coarse_body(coef, inverse, share):
    peers, kdef, _ = coef.shape
    cases = 16
    per = LANES // cases
    every = coef[...].reshape(peers * kdef, LANES)
    lane = lax.broadcasted_iota(jnp.int32, every.shape, 1) // cases
    tiles = inverse.shape[0] // per
    sums = [None] * tiles
    for q in range(per):
        here = jnp.where(lane == q, every, jnp.zeros_like(every))
        for t in range(tiles):
            term = dot_nn(inverse[per * t + q], here)
            sums[t] = term if sums[t] is None else sums[t] + term
    for t in range(tiles):
        share[:, t, :] = sums[t]


def prolong_of(arrived, kdef):
    cases = 16
    total = jnp.sum(arrived, axis=0)
    tiles = total.shape[0]
    row = lax.broadcasted_iota(jnp.int32, (cases, LANES), 0)
    lane = lax.broadcasted_iota(jnp.int32, (cases, LANES), 1)
    out = None
    for t in range(tiles):
        spread = jnp.where(lane % cases == row, total[t : t + 1], 0.0).astype(BF16)
        target = lax.broadcasted_iota(jnp.int32, (LANES, kdef), 0) // cases + t * (LANES // cases)
        onto = (target == lax.broadcasted_iota(jnp.int32, (LANES, kdef), 1)).astype(BF16)
        term = dot_nn(spread, onto)
        out = term if out is None else out + term
    return out.astype(BF16)


def correct_body(first, arrived, block, inverse, basis, *rest):
    if first:
        total, rounded = rest
    else:
        before, total, rounded = rest
    owned = total.shape[1]
    value = dot_nt(block[...], inverse[...])
    prolong = prolong_of(arrived[...], basis.shape[0])
    value = value + dot_nn(prolong, basis[:, :owned])
    if not first:
        value = before[...] + value
    total[...] = value
    rounded[...] = value.astype(BF16)


def residual_body(last, v, f0, f1, f2, f3, picks, stiff, load, *outs):
    edge = margins([f0[...], f1[...], f2[...], f3[...]], picks[...])
    whole = jnp.concatenate([v[...], edge], axis=1)
    value = load[...] - dot_nt(whole, stiff[...])
    outs[0][...] = value if last else value.astype(BF16)


def local(load, stiffness, block_inverse, deflation, margin_rows, coarse_inverse):
    own_load = load[0]
    stiff_rows = stiffness[0]
    inverse_rows = block_inverse[0]
    basis_rows = deflation[0]
    cases, owned = own_load.shape
    kdef, nb = basis_rows.shape
    groups = lax.axis_size("group")
    members = lax.axis_size("member")
    tiles = coarse_inverse.shape[0] * cases // LANES
    picks = (
        lax.broadcasted_iota(jnp.int32, (owned, nb - owned), 0) == margin_rows[0].reshape(1, nb - owned)
    ).astype(BF16)

    def around(values):
        return (
            from_behind(values, "group", 1),
            from_behind(values, "group", -1),
            from_behind(values, "member", 1),
            from_behind(values, "member", -1),
        )

    field = own_load.astype(BF16)
    solution = None
    for step in range(ITERS):
        block, coef = call(
            restrict_body,
            [((cases, nb), BF16), ((members, kdef, LANES), BF16)],
            field, *around(field), picks, basis_rows,
        )
        gathered = lax.all_to_all(coef, "member", 0, 0, tiled=True)
        (share,) = call(coarse_body, [((groups, tiles, LANES), F32)], gathered, coarse_inverse)
        arrived = lax.all_to_all(share, "group", 0, 0, tiled=True)
        before = () if step == 0 else (solution,)
        solution, rounded = call(
            lambda *refs: correct_body(step == 0, *refs),
            [((cases, owned), F32), ((cases, owned), BF16)],
            arrived, block, inverse_rows, basis_rows, *before,
        )
        last = step == ITERS - 1
        (field,) = call(
            lambda *refs: residual_body(last, *refs),
            [((cases, owned), F32 if last else BF16)],
            rounded, *around(rounded), picks, stiff_rows, own_load,
        )
    return (solution[None], field[None])


def solution(mesh):
    placed = (
        P(("group", "member"), None, None),
        P(("group", "member"), None, None),
        P(("group", "member"), None, None),
        P(("group", "member"), None, None),
        P(("group", "member"), None, None),
        P("member", None, "group"),
    )
    return jax.shard_map(
        local,
        mesh=mesh,
        in_specs=placed,
        out_specs=(P(("group", "member"), None, None), P(("group", "member"), None, None)),
        check_vma=False,
    )
```

time: 186 us -> 148 us (0.80)
  local copies, waits for them, and re-layouts: 24.3 us -> 1.62 us
  waiting for transfers between devices: 6.2 us -> 25.4 us
  blocking collectives: 63.5 us -> 52.3 us
  starting transfers between devices: 71.2 us -> 60 us
  matrix products: 8.35 us -> 0 us
  other arithmetic: 8.75 us -> 1.1 us
  Pallas kernels: 0 us -> 5.67 us
    all_gather x2 -> x0, blocking collectives: 32.1 us -> none  [local(): gathered = lax.all_gather(own_coef, 'member', axis=1, tiled=True)]
    all_to_all x2 -> x4, blocking collectives: 31.4 us -> 52.3 us  [the longest x2 26.8 us: local(): arrived = lax.all_to_all(share, 'group', 0, 0, tiled=True)]
    ppermute x16, waiting for transfers between devices: 6.2 us -> 25.4 us  [from_behind(): lax.ppermute(shard, axis, [(i, (i + by) % peers) for i in range(peers)])]
    gather x32 -> x0, local copies, waits for them, and re-layouts: 12.8 us -> none  [the longest x8 3.23 us: extend(): jnp.take(from_member_lower, own_lists[2], axis=1)]
    ppermute x16, starting transfers between devices: 71.2 us -> 60 us  [from_behind(): lax.ppermute(shard, axis, [(i, (i + by) % peers) for i in range(peers)])]
    dot_general x10 -> x0, matrix products: 8.35 us -> none  [the longest x2 3.09 us: local(): jnp.einsum('cn,un->cu', block_values, inverse_rows, preferred_element_typ...]
    pallas_call x0 -> x8, Pallas kernels: none -> 5.67 us  [call(): pl.pallas_call(body, out_shape=[jax.ShapeDtypeStruct(shape, dtype) for sh...]
    ppermute x16 -> x0, local copies, waits for them, and re-layouts: 5.63 us -> none  [from_behind(): lax.ppermute(shard, axis, [(i, (i + by) % peers) for i in range(peers)])]
  transfers between devices with their start and end apart: 16 -> 16, of which waited for: 2 -> 4; matrix products, arithmetic and copies ran while one was open for 10% -> 1% of each run, Pallas kernels for 0% -> 0%
where the time goes in v2:
time: 148 us; the launch traced here: 147 us
  starting transfers between devices  60 us (41%)
  blocking collectives  52.3 us (35%)
  waiting for transfers between devices  25.4 us (17%)
  Pallas kernels  5.67 us (4%)
  local copies, waits for them, and re-layouts  1.62 us (1%)
    ppermute x16, starting transfers between devices, from_behind(): lax.ppermute(shard, axis, [(i, (i + by) % peers) for i in range(peers)])  60 us
    all_to_all x2, blocking collectives, local(): arrived = lax.all_to_all(share, 'group', 0, 0, tiled=True)  26.8 us
    ppermute x16, waiting for transfers between devices, from_behind(): lax.ppermute(shard, axis, [(i, (i + by) % peers) for i in range(peers)])  25.4 us
    all_to_all x2, blocking collectives, local(): gathered = lax.all_to_all(coef, 'member', 0, 0, tiled=True)  25.4 us
    pallas_call x8, Pallas kernels, call(): pl.pallas_call(body, out_shape=[jax.ShapeDtypeStruct(shape, dtype) for sh...  5.67 us
  transfers between devices with their start and end apart: 16, of which 4 were waited for; matrix products, arithmetic and copies ran while one was open for 1% of the time, Pallas kernels for 0%

profile of v2, /device:TPU:1, one launch (start us, length us, event | category | flops | bytes accessed | tf_op | source)
XLA Modules:
  0.0 147.0 jit_solution(9676541965700132545)
XLA Ops:
  0.6 1.0 bitcast_convert_fusion.v
  1.6 8.7 %collective-permute-start.3 = (bf16[16,768]{1,0:T(8,128)(2,1)S(1)}, bf16[16,768]{1,0:T(8,128)(2,1)S(1)}, u32[]{:S(2)}, u32[]{:S(2)}) collective-permute-start(bf16[16,768]{1,0:T(8,128)(2,1)S(1)} %bitcast_convert_fusion.v), channel_id=1, source_target_pairs={{0,7},{1,0},{2,1},{3,2},{4,3},{5,4},{6,5},{7,6},{8,15},{9,8},{10,9... | collective-permute-start | bytes 73736 | tf_op jit(solution)/shard_map/ppermute | solution.py:17
  10.3 1.9 %collective-permute-start.2 = (bf16[16,768]{1,0:T(8,128)(2,1)S(1)}, bf16[16,768]{1,0:T(8,128)(2,1)S(1)}, u32[]{:S(2)}, u32[]{:S(2)}) collective-permute-start(bf16[16,768]{1,0:T(8,128)(2,1)S(1)} %bitcast_convert_fusion.v), channel_id=1, source_target_pairs={{0,1},{1,2},{2,3},{3,4},{4,5},{5,6},{6,7},{7,0},{8,9},{9,10},{10,1... | collective-permute-start | bytes 73736 | tf_op jit(solution)/shard_map/ppermute | solution.py:17
  12.3 10.7 %collective-permute-start.1 = (bf16[16,768]{1,0:T(8,128)(2,1)S(1)}, bf16[16,768]{1,0:T(8,128)(2,1)S(1)}, u32[]{:S(2)}, u32[]{:S(2)}) collective-permute-start(bf16[16,768]{1,0:T(8,128)(2,1)S(1)} %bitcast_convert_fusion.v), channel_id=1, source_target_pairs={{0,504},{8,0},{16,8},{24,16},{32,24},{40,32},{48,40},{56,48},{64,5... | collective-permute-start | bytes 73736 | tf_op jit(solution)/shard_map/ppermute | solution.py:17
  23.0 1.9 %collective-permute-start = (bf16[16,768]{1,0:T(8,128)(2,1)S(1)}, bf16[16,768]{1,0:T(8,128)(2,1)S(1)}, u32[]{:S(2)}, u32[]{:S(2)}) collective-permute-start(bf16[16,768]{1,0:T(8,128)(2,1)S(1)} %bitcast_convert_fusion.v), channel_id=1, source_target_pairs={{0,8},{8,16},{16,24},{24,32},{32,40},{40,48},{48,56},{56,64},{64,7... | collective-permute-start | bytes 73736 | tf_op jit(solution)/shard_map/ppermute | solution.py:17
  24.9 0.8 eq.10
  25.7 0.1 fusion.picks.refs_5_
  25.8 0.0 collective-permute-done.3.f3
  25.9 0.0 collective-permute-done.2.f2
  25.9 0.0 collective-permute-done.1.f1
  25.9 5.9 %collective-permute-done.f0 = bf16[16,768]{1,0:T(8,128)(2,1)S(1)} collective-permute-done((bf16[16,768]{1,0:T(8,128)(2,1)S(1)}, bf16[16,768]{1,0:T(8,128)(2,1)S(1)}, u32[]{:S(2)}, u32[]{:S(2)}) %collective-permute-start) | collective-permute-done | bytes 24608 | tf_op jit(solution)/shard_map/ppermute | solution.py:17
  31.8 0.8 copy-done.3
  32.6 0.4 shard_map.77
  33.0 13.4 %all_to_all.20.coef = bf16[8,32,128]{2,1,0:T(8,128)(2,1)S(1)} all-to-all(bf16[8,32,128]{2,1,0:T(8,128)(2,1)S(1)} %get-tuple-element.10), channel_id=1, replica_groups=mesh['group'=64,'member'=8] {'member'}, dimensions={0} | all-to-all | bytes 131072 | tf_op jit(solution)/shard_map/all_to_all | solution.py:144
  46.4 0.5 shard_map.78
  46.9 13.4 %all_to_all.21.refs_0_ = f32[64,4,128]{2,1,0:T(4,128)S(1)} all-to-all(f32[64,4,128]{2,1,0:T(4,128)S(1)} %shard_map.78), channel_id=1, replica_groups=mesh['group'=64,'member'=8] {'group'}, dimensions={0} | all-to-all | bytes 262144 | tf_op jit(solution)/shard_map/all_to_all | solution.py:146
  60.3 0.7 shard_map.79
  61.0 3.8 %collective-permute-start.7 = (bf16[16,768]{1,0:T(8,128)(2,1)S(1)}, bf16[16,768]{1,0:T(8,128)(2,1)S(1)}, u32[]{:S(2)}, u32[]{:S(2)}) collective-permute-start(bf16[16,768]{1,0:T(8,128)(2,1)S(1)} %get-tuple-element.12.refs_0_), channel_id=1, source_target_pairs={{0,7},{1,0},{2,1},{3,2},{4,3},{5,4},{6,5},{7,6},{8,15},{9,8},{10,9... | collective-permute-start | bytes 73736 | tf_op jit(solution)/shard_map/ppermute | solution.py:17
  64.8 2.7 %collective-permute-start.6 = (bf16[16,768]{1,0:T(8,128)(2,1)S(1)}, bf16[16,768]{1,0:T(8,128)(2,1)S(1)}, u32[]{:S(2)}, u32[]{:S(2)}) collective-permute-start(bf16[16,768]{1,0:T(8,128)(2,1)S(1)} %get-tuple-element.12.refs_0_), channel_id=1, source_target_pairs={{0,1},{1,2},{2,3},{3,4},{4,5},{5,6},{6,7},{7,0},{8,9},{9,10},{10,1... | collective-permute-start | bytes 73736 | tf_op jit(solution)/shard_map/ppermute | solution.py:17
  67.5 4.1 %collective-permute-start.5 = (bf16[16,768]{1,0:T(8,128)(2,1)S(1)}, bf16[16,768]{1,0:T(8,128)(2,1)S(1)}, u32[]{:S(2)}, u32[]{:S(2)}) collective-permute-start(bf16[16,768]{1,0:T(8,128)(2,1)S(1)} %get-tuple-element.12.refs_0_), channel_id=1, source_target_pairs={{0,504},{8,0},{16,8},{24,16},{32,24},{40,32},{48,40},{56,48},{64,5... | collective-permute-start | bytes 73736 | tf_op jit(solution)/shard_map/ppermute | solution.py:17
  71.6 1.9 %collective-permute-start.4 = (bf16[16,768]{1,0:T(8,128)(2,1)S(1)}, bf16[16,768]{1,0:T(8,128)(2,1)S(1)}, u32[]{:S(2)}, u32[]{:S(2)}) collective-permute-start(bf16[16,768]{1,0:T(8,128)(2,1)S(1)} %get-tuple-element.12.refs_0_), channel_id=1, source_target_pairs={{0,8},{8,16},{16,24},{24,32},{32,40},{40,48},{48,56},{56,64},{64,7... | collective-permute-start | bytes 73736 | tf_op jit(solution)/shard_map/ppermute | solution.py:17
  73.5 0.0 collective-permute-done.7.refs_4_
  73.5 0.0 collective-permute-done.6.refs_3_
  73.5 0.0 collective-permute-done.5.refs_2_
  73.6 6.9 %collective-permute-done.4.refs_1_ = bf16[16,768]{1,0:T(8,128)(2,1)S(1)} collective-permute-done((bf16[16,768]{1,0:T(8,128)(2,1)S(1)}, bf16[16,768]{1,0:T(8,128)(2,1)S(1)}, u32[]{:S(2)}, u32[]{:S(2)}) %collective-permute-start.4) | collective-permute-done | bytes 24608 | tf_op jit(solution)/shard_map/ppermute | solution.py:17
  80.4 0.6 shard_map.80.v
  81.0 2.3 %collective-permute-start.11 = (bf16[16,768]{1,0:T(8,128)(2,1)S(1)}, bf16[16,768]{1,0:T(8,128)(2,1)S(1)}, u32[]{:S(2)}, u32[]{:S(2)}) collective-permute-start(bf16[16,768]{1,0:T(8,128)(2,1)S(1)} %shard_map.80.v), channel_id=1, source_target_pairs={{0,7},{1,0},{2,1},{3,2},{4,3},{5,4},{6,5},{7,6},{8,15},{9,8},{10,9... | collective-permute-start | bytes 73736 | tf_op jit(solution)/shard_map/ppermute | solution.py:17
  83.3 4.2 %collective-permute-start.10 = (bf16[16,768]{1,0:T(8,128)(2,1)S(1)}, bf16[16,768]{1,0:T(8,128)(2,1)S(1)}, u32[]{:S(2)}, u32[]{:S(2)}) collective-permute-start(bf16[16,768]{1,0:T(8,128)(2,1)S(1)} %shard_map.80.v), channel_id=1, source_target_pairs={{0,1},{1,2},{2,3},{3,4},{4,5},{5,6},{6,7},{7,0},{8,9},{9,10},{10,1... | collective-permute-start | bytes 73736 | tf_op jit(solution)/shard_map/ppermute | solution.py:17
  87.5 1.9 %collective-permute-start.9 = (bf16[16,768]{1,0:T(8,128)(2,1)S(1)}, bf16[16,768]{1,0:T(8,128)(2,1)S(1)}, u32[]{:S(2)}, u32[]{:S(2)}) collective-permute-start(bf16[16,768]{1,0:T(8,128)(2,1)S(1)} %shard_map.80.v), channel_id=1, source_target_pairs={{0,504},{8,0},{16,8},{24,16},{32,24},{40,32},{48,40},{56,48},{64,5... | collective-permute-start | bytes 73736 | tf_op jit(solution)/shard_map/ppermute | solution.py:17
  89.4 3.4 %collective-permute-start.8 = (bf16[16,768]{1,0:T(8,128)(2,1)S(1)}, bf16[16,768]{1,0:T(8,128)(2,1)S(1)}, u32[]{:S(2)}, u32[]{:S(2)}) collective-permute-start(bf16[16,768]{1,0:T(8,128)(2,1)S(1)} %shard_map.80.v), channel_id=1, source_target_pairs={{0,8},{8,16},{16,24},{24,32},{32,40},{40,48},{48,56},{56,64},{64,7... | collective-permute-start | bytes 73736 | tf_op jit(solution)/shard_map/ppermute | solution.py:17
  92.8 0.0 collective-permute-done.11.f3
  92.8 0.0 collective-permute-done.10.f2
  92.8 0.0 collective-permute-done.9.f1
  92.8 5.8 %collective-permute-done.8.f0 = bf16[16,768]{1,0:T(8,128)(2,1)S(1)} collective-permute-done((bf16[16,768]{1,0:T(8,128)(2,1)S(1)}, bf16[16,768]{1,0:T(8,128)(2,1)S(1)}, u32[]{:S(2)}, u32[]{:S(2)}) %collective-permute-start.8) | collective-permute-done | bytes 24608 | tf_op jit(solution)/shard_map/ppermute | solution.py:17
  98.6 0.4 shard_map.81
  99.0 12.1 %all_to_all.22.coef = bf16[8,32,128]{2,1,0:T(8,128)(2,1)S(1)} all-to-all(bf16[8,32,128]{2,1,0:T(8,128)(2,1)S(1)} %get-tuple-element.13), channel_id=1, replica_groups=mesh['group'=64,'member'=8] {'member'}, dimensions={0} | all-to-all | bytes 131072 | tf_op jit(solution)/shard_map/all_to_all | solution.py:144
  111.1 0.5 shard_map.82
  111.6 13.4 %all_to_all.23.refs_0_ = f32[64,4,128]{2,1,0:T(4,128)S(1)} all-to-all(f32[64,4,128]{2,1,0:T(4,128)S(1)} %shard_map.82), channel_id=1, replica_groups=mesh['group'=64,'member'=8] {'group'}, dimensions={0} | all-to-all | bytes 262144 | tf_op jit(solution)/shard_map/all_to_all | solution.py:146
  125.0 1.4 shard_map.83
  126.4 3.8 %collective-permute-start.15 = (bf16[16,768]{1,0:T(8,128)(2,1)S(1)}, bf16[16,768]{1,0:T(8,128)(2,1)S(1)}, u32[]{:S(2)}, u32[]{:S(2)}) collective-permute-start(bf16[16,768]{1,0:T(8,128)(2,1)S(1)} %get-tuple-element.17.refs_0_), channel_id=1, source_target_pairs={{0,7},{1,0},{2,1},{3,2},{4,3},{5,4},{6,5},{7,6},{8,15},{9,8},{10,9... | collective-permute-start | bytes 73736 | tf_op jit(solution)/shard_map/ppermute | solution.py:17
  130.2 2.7 %collective-permute-start.14 = (bf16[16,768]{1,0:T(8,128)(2,1)S(1)}, bf16[16,768]{1,0:T(8,128)(2,1)S(1)}, u32[]{:S(2)}, u32[]{:S(2)}) collective-permute-start(bf16[16,768]{1,0:T(8,128)(2,1)S(1)} %get-tuple-element.17.refs_0_), channel_id=1, source_target_pairs={{0,1},{1,2},{2,3},{3,4},{4,5},{5,6},{6,7},{7,0},{8,9},{9,10},{10,1... | collective-permute-start | bytes 73736 | tf_op jit(solution)/shard_map/ppermute | solution.py:17
  132.9 4.1 %collective-permute-start.13 = (bf16[16,768]{1,0:T(8,128)(2,1)S(1)}, bf16[16,768]{1,0:T(8,128)(2,1)S(1)}, u32[]{:S(2)}, u32[]{:S(2)}) collective-permute-start(bf16[16,768]{1,0:T(8,128)(2,1)S(1)} %get-tuple-element.17.refs_0_), channel_id=1, source_target_pairs={{0,504},{8,0},{16,8},{24,16},{32,24},{40,32},{48,40},{56,48},{64,5... | collective-permute-start | bytes 73736 | tf_op jit(solution)/shard_map/ppermute | solution.py:17
  136.9 1.9 %collective-permute-start.12 = (bf16[16,768]{1,0:T(8,128)(2,1)S(1)}, bf16[16,768]{1,0:T(8,128)(2,1)S(1)}, u32[]{:S(2)}, u32[]{:S(2)}) collective-permute-start(bf16[16,768]{1,0:T(8,128)(2,1)S(1)} %get-tuple-element.17.refs_0_), channel_id=1, source_target_pairs={{0,8},{8,16},{16,24},{24,32},{32,40},{40,48},{48,56},{56,64},{64,7... | collective-permute-start | bytes 73736 | tf_op jit(solution)/shard_map/ppermute | solution.py:17
  138.9 0.0 collective-permute-done.15.refs_4_
  138.9 0.0 collective-permute-done.14.refs_3_
  138.9 0.0 collective-permute-done.13.refs_2_
  138.9 6.8 %collective-permute-done.12.refs_1_ = bf16[16,768]{1,0:T(8,128)(2,1)S(1)} collective-permute-done((bf16[16,768]{1,0:T(8,128)(2,1)S(1)}, bf16[16,768]{1,0:T(8,128)(2,1)S(1)}, u32[]{:S(2)}, u32[]{:S(2)}) %collective-permute-start.12) | collective-permute-done | bytes 24608 | tf_op jit(solution)/shard_map/ppermute | solution.py:17
  145.8 1.3 shard_map.84
  (11 shorter events, 0.0 us)
Async XLA Ops:
  0.6 45.7 %copy-start.2 = (bf16[32,64,256]{2,1,0:T(8,128)(2,1)S(1)}, bf16[32,64,256]{2,1,0:T(8,128)(2,1)}, u32[]{:S(2)}) copy-start(bf16[32,64,256]{2,1,0:T(8,128)(2,1)} %inverse.3) | copy-start | bytes 3145732
  0.6 59.7 %copy-start = (bf16[1,768,1024]{2,1,0:T(8,128)(2,1)S(1)}, bf16[1,768,1024]{2,1,0:T(8,128)(2,1)}, u32[]{:S(2)}) copy-start(bf16[1,768,1024]{2,1,0:T(8,128)(2,1)} %param.8) | copy-start | bytes 4718596
  1.6 24.2 %collective-permute-start.3 = (bf16[16,768]{1,0:T(8,128)(2,1)S(1)}, bf16[16,768]{1,0:T(8,128)(2,1)S(1)}, u32[]{:S(2)}, u32[]{:S(2)}) collective-permute-start(bf16[16,768]{1,0:T(8,128)(2,1)S(1)} %bitcast_convert_fusion.v), channel_id=1, source_target_pairs={{0,7},{1,0},{2,1},{3,2},{4,3},{5,4},{6,5},{7,6},{8,15},{9,8},{10,9... | collective-permute-start | bytes 73736 | tf_op jit(solution)/shard_map/ppermute | solution.py:17
  10.3 15.5 %collective-permute-start.2 = (bf16[16,768]{1,0:T(8,128)(2,1)S(1)}, bf16[16,768]{1,0:T(8,128)(2,1)S(1)}, u32[]{:S(2)}, u32[]{:S(2)}) collective-permute-start(bf16[16,768]{1,0:T(8,128)(2,1)S(1)} %bitcast_convert_fusion.v), channel_id=1, source_target_pairs={{0,1},{1,2},{2,3},{3,4},{4,5},{5,6},{6,7},{7,0},{8,9},{9,10},{10,1... | collective-permute-start | bytes 73736 | tf_op jit(solution)/shard_map/ppermute | solution.py:17
  12.3 13.6 %collective-permute-start.1 = (bf16[16,768]{1,0:T(8,128)(2,1)S(1)}, bf16[16,768]{1,0:T(8,128)(2,1)S(1)}, u32[]{:S(2)}, u32[]{:S(2)}) collective-permute-start(bf16[16,768]{1,0:T(8,128)(2,1)S(1)} %bitcast_convert_fusion.v), channel_id=1, source_target_pairs={{0,504},{8,0},{16,8},{24,16},{32,24},{40,32},{48,40},{56,48},{64,5... | collective-permute-start | bytes 73736 | tf_op jit(solution)/shard_map/ppermute | solution.py:17
  23.0 8.8 %collective-permute-start = (bf16[16,768]{1,0:T(8,128)(2,1)S(1)}, bf16[16,768]{1,0:T(8,128)(2,1)S(1)}, u32[]{:S(2)}, u32[]{:S(2)}) collective-permute-start(bf16[16,768]{1,0:T(8,128)(2,1)S(1)} %bitcast_convert_fusion.v), channel_id=1, source_target_pairs={{0,8},{8,16},{16,24},{24,32},{32,40},{40,48},{48,56},{56,64},{64,7... | collective-permute-start | bytes 73736 | tf_op jit(solution)/shard_map/ppermute | solution.py:17
  31.8 0.8 copy-start.3
  32.6 27.7 %copy-start.4 = (bf16[1,32,1024]{2,1,0:T(8,128)(2,1)S(1)}, bf16[1,32,1024]{2,1,0:T(8,128)(2,1)}, u32[]{:S(2)}) copy-start(bf16[1,32,1024]{2,1,0:T(8,128)(2,1)} %param.9) | copy-start | bytes 196612
  46.4 34.0 %copy-start.1 = (bf16[1,768,1024]{2,1,0:T(8,128)(2,1)S(1)}, bf16[1,768,1024]{2,1,0:T(8,128)(2,1)}, u32[]{:S(2)}) copy-start(bf16[1,768,1024]{2,1,0:T(8,128)(2,1)} %param.7) | copy-start | bytes 4718596
  46.4 34.0 %copy-start.5 = (f32[1,16,768]{2,1,0:T(8,128)S(1)}, f32[1,16,768]{2,1,0:T(8,128)}, u32[]{:S(2)}) copy-start(f32[1,16,768]{2,1,0:T(8,128)} %param.6) | copy-start | bytes 147460
  61.0 12.5 %collective-permute-start.7 = (bf16[16,768]{1,0:T(8,128)(2,1)S(1)}, bf16[16,768]{1,0:T(8,128)(2,1)S(1)}, u32[]{:S(2)}, u32[]{:S(2)}) collective-permute-start(bf16[16,768]{1,0:T(8,128)(2,1)S(1)} %get-tuple-element.12.refs_0_), channel_id=1, source_target_pairs={{0,7},{1,0},{2,1},{3,2},{4,3},{5,4},{6,5},{7,6},{8,15},{9,8},{10,9... | collective-permute-start | bytes 73736 | tf_op jit(solution)/shard_map/ppermute | solution.py:17
  64.8 8.7 %collective-permute-start.6 = (bf16[16,768]{1,0:T(8,128)(2,1)S(1)}, bf16[16,768]{1,0:T(8,128)(2,1)S(1)}, u32[]{:S(2)}, u32[]{:S(2)}) collective-permute-start(bf16[16,768]{1,0:T(8,128)(2,1)S(1)} %get-tuple-element.12.refs_0_), channel_id=1, source_target_pairs={{0,1},{1,2},{2,3},{3,4},{4,5},{5,6},{6,7},{7,0},{8,9},{9,10},{10,1... | collective-permute-start | bytes 73736 | tf_op jit(solution)/shard_map/ppermute | solution.py:17
  67.5 6.0 %collective-permute-start.5 = (bf16[16,768]{1,0:T(8,128)(2,1)S(1)}, bf16[16,768]{1,0:T(8,128)(2,1)S(1)}, u32[]{:S(2)}, u32[]{:S(2)}) collective-permute-start(bf16[16,768]{1,0:T(8,128)(2,1)S(1)} %get-tuple-element.12.refs_0_), channel_id=1, source_target_pairs={{0,504},{8,0},{16,8},{24,16},{32,24},{40,32},{48,40},{56,48},{64,5... | collective-permute-start | bytes 73736 | tf_op jit(solution)/shard_map/ppermute | solution.py:17
  71.6 8.8 %collective-permute-start.4 = (bf16[16,768]{1,0:T(8,128)(2,1)S(1)}, bf16[16,768]{1,0:T(8,128)(2,1)S(1)}, u32[]{:S(2)}, u32[]{:S(2)}) collective-permute-start(bf16[16,768]{1,0:T(8,128)(2,1)S(1)} %get-tuple-element.12.refs_0_), channel_id=1, source_target_pairs={{0,8},{8,16},{16,24},{24,32},{32,40},{40,48},{48,56},{56,64},{64,7... | collective-permute-start | bytes 73736 | tf_op jit(solution)/shard_map/ppermute | solution.py:17
  81.0 11.8 %collective-permute-start.11 = (bf16[16,768]{1,0:T(8,128)(2,1)S(1)}, bf16[16,768]{1,0:T(8,128)(2,1)S(1)}, u32[]{:S(2)}, u32[]{:S(2)}) collective-permute-start(bf16[16,768]{1,0:T(8,128)(2,1)S(1)} %shard_map.80.v), channel_id=1, source_target_pairs={{0,7},{1,0},{2,1},{3,2},{4,3},{5,4},{6,5},{7,6},{8,15},{9,8},{10,9... | collective-permute-start | bytes 73736 | tf_op jit(solution)/shard_map/ppermute | solution.py:17
  83.3 9.5 %collective-permute-start.10 = (bf16[16,768]{1,0:T(8,128)(2,1)S(1)}, bf16[16,768]{1,0:T(8,128)(2,1)S(1)}, u32[]{:S(2)}, u32[]{:S(2)}) collective-permute-start(bf16[16,768]{1,0:T(8,128)(2,1)S(1)} %shard_map.80.v), channel_id=1, source_target_pairs={{0,1},{1,2},{2,3},{3,4},{4,5},{5,6},{6,7},{7,0},{8,9},{9,10},{10,1... | collective-permute-start | bytes 73736 | tf_op jit(solution)/shard_map/ppermute | solution.py:17
  87.5 5.3 %collective-permute-start.9 = (bf16[16,768]{1,0:T(8,128)(2,1)S(1)}, bf16[16,768]{1,0:T(8,128)(2,1)S(1)}, u32[]{:S(2)}, u32[]{:S(2)}) collective-permute-start(bf16[16,768]{1,0:T(8,128)(2,1)S(1)} %shard_map.80.v), channel_id=1, source_target_pairs={{0,504},{8,0},{16,8},{24,16},{32,24},{40,32},{48,40},{56,48},{64,5... | collective-permute-start | bytes 73736 | tf_op jit(solution)/shard_map/ppermute | solution.py:17
  89.4 9.2 %collective-permute-start.8 = (bf16[16,768]{1,0:T(8,128)(2,1)S(1)}, bf16[16,768]{1,0:T(8,128)(2,1)S(1)}, u32[]{:S(2)}, u32[]{:S(2)}) collective-permute-start(bf16[16,768]{1,0:T(8,128)(2,1)S(1)} %shard_map.80.v), channel_id=1, source_target_pairs={{0,8},{8,16},{16,24},{24,32},{32,40},{40,48},{48,56},{56,64},{64,7... | collective-permute-start | bytes 73736 | tf_op jit(solution)/shard_map/ppermute | solution.py:17
  126.4 12.5 %collective-permute-start.15 = (bf16[16,768]{1,0:T(8,128)(2,1)S(1)}, bf16[16,768]{1,0:T(8,128)(2,1)S(1)}, u32[]{:S(2)}, u32[]{:S(2)}) collective-permute-start(bf16[16,768]{1,0:T(8,128)(2,1)S(1)} %get-tuple-element.17.refs_0_), channel_id=1, source_target_pairs={{0,7},{1,0},{2,1},{3,2},{4,3},{5,4},{6,5},{7,6},{8,15},{9,8},{10,9... | collective-permute-start | bytes 73736 | tf_op jit(solution)/shard_map/ppermute | solution.py:17
  130.2 8.7 %collective-permute-start.14 = (bf16[16,768]{1,0:T(8,128)(2,1)S(1)}, bf16[16,768]{1,0:T(8,128)(2,1)S(1)}, u32[]{:S(2)}, u32[]{:S(2)}) collective-permute-start(bf16[16,768]{1,0:T(8,128)(2,1)S(1)} %get-tuple-element.17.refs_0_), channel_id=1, source_target_pairs={{0,1},{1,2},{2,3},{3,4},{4,5},{5,6},{6,7},{7,0},{8,9},{9,10},{10,1... | collective-permute-start | bytes 73736 | tf_op jit(solution)/shard_map/ppermute | solution.py:17
  132.9 6.0 %collective-permute-start.13 = (bf16[16,768]{1,0:T(8,128)(2,1)S(1)}, bf16[16,768]{1,0:T(8,128)(2,1)S(1)}, u32[]{:S(2)}, u32[]{:S(2)}) collective-permute-start(bf16[16,768]{1,0:T(8,128)(2,1)S(1)} %get-tuple-element.17.refs_0_), channel_id=1, source_target_pairs={{0,504},{8,0},{16,8},{24,16},{32,24},{40,32},{48,40},{56,48},{64,5... | collective-permute-start | bytes 73736 | tf_op jit(solution)/shard_map/ppermute | solution.py:17
  136.9 8.8 %collective-permute-start.12 = (bf16[16,768]{1,0:T(8,128)(2,1)S(1)}, bf16[16,768]{1,0:T(8,128)(2,1)S(1)}, u32[]{:S(2)}, u32[]{:S(2)}) collective-permute-start(bf16[16,768]{1,0:T(8,128)(2,1)S(1)} %get-tuple-element.17.refs_0_), channel_id=1, source_target_pairs={{0,8},{8,16},{16,24},{24,32},{32,40},{40,48},{48,56},{56,64},{64,7... | collective-permute-start | bytes 73736 | tf_op jit(solution)/shard_map/ppermute | solution.py:17

commit v3 on v2

--- a/solution.py
+++ b/solution.py
@@ -35,19 +35,23 @@
     return jnp.dot(left, right, preferred_element_type=F32)
 
 
-def margins(fields, picks):
+def exchanged(shard, axis, first):
+    peers = lax.axis_size(axis)
+    pairs = [((first + i) % peers, (first + (i ^ 1)) % peers) for i in range(peers)]
+    return lax.ppermute(shard, axis, pairs)
+
+
+def margins(fields, picks, owner):
     cases = fields[0].shape[0]
-    width = picks.shape[1] // len(fields)
     every = dot_nn(jnp.concatenate(fields, axis=0), picks)
-    owner = lax.broadcasted_iota(jnp.int32, (cases, picks.shape[1]), 1) // width
     kept = every[:cases]
     for d in range(1, len(fields)):
         kept = jnp.where(owner == d, every[d * cases : (d + 1) * cases], kept)
     return kept.astype(BF16)
 
 
-def restrict_body(v, f0, f1, f2, f3, picks, basis, block, coef):
-    edge = margins([f0[...], f1[...], f2[...], f3[...]], picks[...])
+def restrict_body(v, pair, other, lower, upper, picks, owner, basis, block, coef):
+    edge = margins([lower[...], upper[...], pair[...], other[...]], picks[...], owner[...])
     whole = jnp.concatenate([v[...], edge], axis=1)
     block[...] = whole
     tall = jnp.concatenate([whole] * (LANES // whole.shape[0]), axis=0)
@@ -104,11 +108,16 @@
     rounded[...] = value.astype(BF16)
 
 
-def residual_body(last, v, f0, f1, f2, f3, picks, stiff, load, *outs):
-    edge = margins([f0[...], f1[...], f2[...], f3[...]], picks[...])
+def residual_body(last, v, pair, other, lower, upper, picks, owner, stiff, load, *rest):
+    edge = margins([lower[...], upper[...], pair[...], other[...]], picks[...], owner[...])
     whole = jnp.concatenate([v[...], edge], axis=1)
     value = load[...] - dot_nt(whole, stiff[...])
-    outs[0][...] = value if last else value.astype(BF16)
+    if last:
+        total, out, passed = rest
+        passed[...] = total[...]
+        out[...] = value
+    else:
+        rest[0][...] = value.astype(BF16)
 
 
 def local(load, stiffness, block_inverse, deflation, margin_rows, coarse_inverse):
@@ -125,13 +134,16 @@
         lax.broadcasted_iota(jnp.int32, (owned, nb - owned), 0) == margin_rows[0].reshape(1, nb - owned)
     ).astype(BF16)
 
+    source = lax.broadcasted_iota(jnp.int32, (1, nb - owned), 1) // margin_rows.shape[2]
+    even = lax.axis_index("member") % 2 == 0
+    owner = jnp.where((source >= 2) & even, 5 - source, source)
+
     def around(values):
-        return (
-            from_behind(values, "group", 1),
-            from_behind(values, "group", -1),
-            from_behind(values, "member", 1),
-            from_behind(values, "member", -1),
-        )
+        from_pair = exchanged(values, "member", 0)
+        from_other = exchanged(values, "member", 1)
+        from_lower = from_behind(values, "group", 1)
+        from_upper = from_behind(values, "group", -1)
+        return from_pair, from_other, from_lower, from_upper
 
     field = own_load.astype(BF16)
     solution = None
@@ -139,7 +151,7 @@
         block, coef = call(
             restrict_body,
             [((cases, nb), BF16), ((members, kdef, LANES), BF16)],
-            field, *around(field), picks, basis_rows,
+            field, *around(field), picks, owner, basis_rows,
         )
         gathered = lax.all_to_all(coef, "member", 0, 0, tiled=True)
         (share,) = call(coarse_body, [((groups, tiles, LANES), F32)], gathered, coarse_inverse)
@@ -151,12 +163,13 @@
             arrived, block, inverse_rows, basis_rows, *before,
         )
         last = step == ITERS - 1
-        (field,) = call(
+        kept = (solution,) if last else ()
+        field, *passed = call(
             lambda *refs: residual_body(last, *refs),
-            [((cases, owned), F32 if last else BF16)],
-            rounded, *around(rounded), picks, stiff_rows, own_load,
+            [((cases, owned), F32 if last else BF16)] + [((cases, owned), F32)] * last,
+            rounded, *around(rounded), picks, owner, stiff_rows, own_load, *kept,
         )
-    return (solution[None], field[None])
+    return (passed[0][None], field[None])
 
 
 def solution(mesh):

time: 148 us -> 138 us (0.932)
  waiting for transfers between devices: 25.4 us -> 3.1 us
  blocking collectives: 52.3 us -> 59.9 us
  starting transfers between devices: 60 us -> 64.7 us
    ppermute x0 -> x8, starting transfers between devices: none -> 28 us  [exchanged(): return lax.ppermute(shard, axis, pairs)]
    ppermute x16 -> x8, waiting for transfers between devices: 25.4 us -> 0.3 us  [from_behind(): lax.ppermute(shard, axis, [(i, (i + by) % peers) for i in range(peers)])]
    ppermute x16 -> x8, starting transfers between devices: 60 us -> 36.6 us  [from_behind(): lax.ppermute(shard, axis, [(i, (i + by) % peers) for i in range(peers)])]
    all_to_all x2, blocking collectives: 26.8 us -> 33.9 us  [local(): arrived = lax.all_to_all(share, 'group', 0, 0, tiled=True)]
    ppermute x0 -> x8, waiting for transfers between devices: none -> 2.81 us  [exchanged(): return lax.ppermute(shard, axis, pairs)]
where the time goes in v3:
time: 138 us; the launch traced here: 136 us
  starting transfers between devices  64.7 us (47%)
  blocking collectives  59.9 us (43%)
  Pallas kernels  5.05 us (4%)
  waiting for transfers between devices  3.1 us (2%)
  local copies, waits for them, and re-layouts  1.62 us (1%)
    ppermute x8, starting transfers between devices, from_behind(): lax.ppermute(shard, axis, [(i, (i + by) % peers) for i in range(peers)])  36.6 us
    all_to_all x2, blocking collectives, local(): arrived = lax.all_to_all(share, 'group', 0, 0, tiled=True)  33.9 us
    ppermute x8, starting transfers between devices, exchanged(): return lax.ppermute(shard, axis, pairs)  28 us
    all_to_all x2, blocking collectives, local(): gathered = lax.all_to_all(coef, 'member', 0, 0, tiled=True)  26 us
    pallas_call x8, Pallas kernels, call(): pl.pallas_call(body, out_shape=[jax.ShapeDtypeStruct(shape, dtype) for sh...  5.05 us
    ppermute x8, waiting for transfers between devices, exchanged(): return lax.ppermute(shard, axis, pairs)  2.81 us
  transfers between devices with their start and end apart: 16, of which 4 were waited for; matrix products, arithmetic and copies ran while one was open for 1% of the time, Pallas kernels for 0%

profile of v3, /device:TPU:1, one launch (start us, length us, event | category | flops | bytes accessed | tf_op | source)
XLA Modules:
  0.0 136.4 jit_solution(498011111596887456)
XLA Ops:
  0.6 1.0 bitcast_convert_fusion.v
  1.6 14.7 %collective-permute-start.3 = (bf16[16,768]{1,0:T(8,128)(2,1)S(1)}, bf16[16,768]{1,0:T(8,128)(2,1)S(1)}, u32[]{:S(2)}, u32[]{:S(2)}) collective-permute-start(bf16[16,768]{1,0:T(8,128)(2,1)S(1)} %bitcast_convert_fusion.v), channel_id=1, source_target_pairs={{0,504},{8,0},{16,8},{24,16},{32,24},{40,32},{48,40},{56,48},{64,5... | collective-permute-start | bytes 73736 | tf_op jit(solution)/shard_map/ppermute | solution.py:17
  16.3 1.9 %collective-permute-start.2 = (bf16[16,768]{1,0:T(8,128)(2,1)S(1)}, bf16[16,768]{1,0:T(8,128)(2,1)S(1)}, u32[]{:S(2)}, u32[]{:S(2)}) collective-permute-start(bf16[16,768]{1,0:T(8,128)(2,1)S(1)} %bitcast_convert_fusion.v), channel_id=1, source_target_pairs={{0,8},{8,16},{16,24},{24,32},{32,40},{40,48},{48,56},{56,64},{64,7... | collective-permute-start | bytes 73736 | tf_op jit(solution)/shard_map/ppermute | solution.py:17
  18.2 5.1 %collective-permute-start.1 = (bf16[16,768]{1,0:T(8,128)(2,1)S(1)}, bf16[16,768]{1,0:T(8,128)(2,1)S(1)}, u32[]{:S(2)}, u32[]{:S(2)}) collective-permute-start(bf16[16,768]{1,0:T(8,128)(2,1)S(1)} %bitcast_convert_fusion.v), channel_id=1, source_target_pairs={{1,2},{2,1},{3,4},{4,3},{5,6},{6,5},{7,0},{0,7},{9,10},{10,9},{11,... | collective-permute-start | bytes 73736 | tf_op jit(solution)/shard_map/ppermute | solution.py:41
  23.3 2.2 %collective-permute-start = (bf16[16,768]{1,0:T(8,128)(2,1)S(1)}, bf16[16,768]{1,0:T(8,128)(2,1)S(1)}, u32[]{:S(2)}, u32[]{:S(2)}) collective-permute-start(bf16[16,768]{1,0:T(8,128)(2,1)S(1)} %bitcast_convert_fusion.v), channel_id=1, source_target_pairs={{0,1},{1,0},{2,3},{3,2},{4,5},{5,4},{6,7},{7,6},{8,9},{9,8},{10,11... | collective-permute-start | bytes 73736 | tf_op jit(solution)/shard_map/ppermute | solution.py:41
  25.5 0.8 eq.15
  26.3 0.1 fusion.picks.refs_5_
  26.5 0.0 collective-permute-done.3.upper
  26.5 0.0 collective-permute-done.2.lower
  26.5 0.0 collective-permute-done.1.other
  26.5 0.0 collective-permute-done.pair
  26.5 0.0 copy-start.3
  26.5 0.8 copy-done.3
  27.4 0.4 shard_map.77
  27.7 14.0 %all_to_all.20.coef = bf16[8,32,128]{2,1,0:T(8,128)(2,1)S(1)} all-to-all(bf16[8,32,128]{2,1,0:T(8,128)(2,1)S(1)} %get-tuple-element.12), channel_id=1, replica_groups=mesh['group'=64,'member'=8] {'member'}, dimensions={0} | all-to-all | bytes 131072 | tf_op jit(solution)/shard_map/all_to_all | solution.py:156
  41.7 0.5 shard_map.78
  42.2 16.8 %all_to_all.21.refs_0_ = f32[64,4,128]{2,1,0:T(4,128)S(1)} all-to-all(f32[64,4,128]{2,1,0:T(4,128)S(1)} %shard_map.78), channel_id=1, replica_groups=mesh['group'=64,'member'=8] {'group'}, dimensions={0} | all-to-all | bytes 262144 | tf_op jit(solution)/shard_map/all_to_all | solution.py:158
  59.1 0.7 shard_map.79
  59.8 3.4 %collective-permute-start.7 = (bf16[16,768]{1,0:T(8,128)(2,1)S(1)}, bf16[16,768]{1,0:T(8,128)(2,1)S(1)}, u32[]{:S(2)}, u32[]{:S(2)}) collective-permute-start(bf16[16,768]{1,0:T(8,128)(2,1)S(1)} %get-tuple-element.14.refs_0_), channel_id=1, source_target_pairs={{0,504},{8,0},{16,8},{24,16},{32,24},{40,32},{48,40},{56,48},{64,5... | collective-permute-start | bytes 73736 | tf_op jit(solution)/shard_map/ppermute | solution.py:17
  63.2 1.9 %collective-permute-start.6 = (bf16[16,768]{1,0:T(8,128)(2,1)S(1)}, bf16[16,768]{1,0:T(8,128)(2,1)S(1)}, u32[]{:S(2)}, u32[]{:S(2)}) collective-permute-start(bf16[16,768]{1,0:T(8,128)(2,1)S(1)} %get-tuple-element.14.refs_0_), channel_id=1, source_target_pairs={{0,8},{8,16},{16,24},{24,32},{32,40},{40,48},{48,56},{56,64},{64,7... | collective-permute-start | bytes 73736 | tf_op jit(solution)/shard_map/ppermute | solution.py:17
  65.2 4.9 %collective-permute-start.5 = (bf16[16,768]{1,0:T(8,128)(2,1)S(1)}, bf16[16,768]{1,0:T(8,128)(2,1)S(1)}, u32[]{:S(2)}, u32[]{:S(2)}) collective-permute-start(bf16[16,768]{1,0:T(8,128)(2,1)S(1)} %get-tuple-element.14.refs_0_), channel_id=1, source_target_pairs={{1,2},{2,1},{3,4},{4,3},{5,6},{6,5},{7,0},{0,7},{9,10},{10,9},{11,... | collective-permute-start | bytes 73736 | tf_op jit(solution)/shard_map/ppermute | solution.py:41
  70.1 1.9 %collective-permute-start.4 = (bf16[16,768]{1,0:T(8,128)(2,1)S(1)}, bf16[16,768]{1,0:T(8,128)(2,1)S(1)}, u32[]{:S(2)}, u32[]{:S(2)}) collective-permute-start(bf16[16,768]{1,0:T(8,128)(2,1)S(1)} %get-tuple-element.14.refs_0_), channel_id=1, source_target_pairs={{0,1},{1,0},{2,3},{3,2},{4,5},{5,4},{6,7},{7,6},{8,9},{9,8},{10,11... | collective-permute-start | bytes 73736 | tf_op jit(solution)/shard_map/ppermute | solution.py:41
  72.0 0.0 collective-permute-done.7.refs_4_
  72.1 0.0 collective-permute-done.6.refs_3_
  72.1 0.0 collective-permute-done.5.refs_2_
  72.1 1.1 collective-permute-done.4.refs_1_
  73.2 0.6 shard_map.80.v
  73.8 7.4 %collective-permute-start.11 = (bf16[16,768]{1,0:T(8,128)(2,1)S(1)}, bf16[16,768]{1,0:T(8,128)(2,1)S(1)}, u32[]{:S(2)}, u32[]{:S(2)}) collective-permute-start(bf16[16,768]{1,0:T(8,128)(2,1)S(1)} %shard_map.80.v), channel_id=1, source_target_pairs={{0,504},{8,0},{16,8},{24,16},{32,24},{40,32},{48,40},{56,48},{64,5... | collective-permute-start | bytes 73736 | tf_op jit(solution)/shard_map/ppermute | solution.py:17
  81.2 1.9 %collective-permute-start.10 = (bf16[16,768]{1,0:T(8,128)(2,1)S(1)}, bf16[16,768]{1,0:T(8,128)(2,1)S(1)}, u32[]{:S(2)}, u32[]{:S(2)}) collective-permute-start(bf16[16,768]{1,0:T(8,128)(2,1)S(1)} %shard_map.80.v), channel_id=1, source_target_pairs={{0,8},{8,16},{16,24},{24,32},{32,40},{40,48},{48,56},{56,64},{64,7... | collective-permute-start | bytes 73736 | tf_op jit(solution)/shard_map/ppermute | solution.py:17
  83.1 3.2 %collective-permute-start.9 = (bf16[16,768]{1,0:T(8,128)(2,1)S(1)}, bf16[16,768]{1,0:T(8,128)(2,1)S(1)}, u32[]{:S(2)}, u32[]{:S(2)}) collective-permute-start(bf16[16,768]{1,0:T(8,128)(2,1)S(1)} %shard_map.80.v), channel_id=1, source_target_pairs={{1,2},{2,1},{3,4},{4,3},{5,6},{6,5},{7,0},{0,7},{9,10},{10,9},{11,... | collective-permute-start | bytes 73736 | tf_op jit(solution)/shard_map/ppermute | solution.py:41
  86.4 4.1 %collective-permute-start.8 = (bf16[16,768]{1,0:T(8,128)(2,1)S(1)}, bf16[16,768]{1,0:T(8,128)(2,1)S(1)}, u32[]{:S(2)}, u32[]{:S(2)}) collective-permute-start(bf16[16,768]{1,0:T(8,128)(2,1)S(1)} %shard_map.80.v), channel_id=1, source_target_pairs={{0,1},{1,0},{2,3},{3,2},{4,5},{5,4},{6,7},{7,6},{8,9},{9,8},{10,11... | collective-permute-start | bytes 73736 | tf_op jit(solution)/shard_map/ppermute | solution.py:41
  90.5 0.0 collective-permute-done.11.upper
  90.5 0.0 collective-permute-done.10.lower
  90.5 0.0 collective-permute-done.9.other
  90.5 0.8 collective-permute-done.8.pair
  91.3 0.4 shard_map.81
  91.7 12.0 %all_to_all.22.coef = bf16[8,32,128]{2,1,0:T(8,128)(2,1)S(1)} all-to-all(bf16[8,32,128]{2,1,0:T(8,128)(2,1)S(1)} %get-tuple-element.15), channel_id=1, replica_groups=mesh['group'=64,'member'=8] {'member'}, dimensions={0} | all-to-all | bytes 131072 | tf_op jit(solution)/shard_map/all_to_all | solution.py:156
  103.7 0.5 shard_map.82
  104.2 17.0 %all_to_all.23.refs_0_ = f32[64,4,128]{2,1,0:T(4,128)S(1)} all-to-all(f32[64,4,128]{2,1,0:T(4,128)S(1)} %shard_map.82), channel_id=1, replica_groups=mesh['group'=64,'member'=8] {'group'}, dimensions={0} | all-to-all | bytes 262144 | tf_op jit(solution)/shard_map/all_to_all | solution.py:158
  121.3 0.7 shard_map.83
  122.0 3.4 %collective-permute-start.15 = (bf16[16,768]{1,0:T(8,128)(2,1)S(1)}, bf16[16,768]{1,0:T(8,128)(2,1)S(1)}, u32[]{:S(2)}, u32[]{:S(2)}) collective-permute-start(bf16[16,768]{1,0:T(8,128)(2,1)S(1)} %get-tuple-element.18.refs_0_), channel_id=1, source_target_pairs={{0,504},{8,0},{16,8},{24,16},{32,24},{40,32},{48,40},{56,48},{64,5... | collective-permute-start | bytes 73736 | tf_op jit(solution)/shard_map/ppermute | solution.py:17
  125.5 1.9 %collective-permute-start.14 = (bf16[16,768]{1,0:T(8,128)(2,1)S(1)}, bf16[16,768]{1,0:T(8,128)(2,1)S(1)}, u32[]{:S(2)}, u32[]{:S(2)}) collective-permute-start(bf16[16,768]{1,0:T(8,128)(2,1)S(1)} %get-tuple-element.18.refs_0_), channel_id=1, source_target_pairs={{0,8},{8,16},{16,24},{24,32},{32,40},{40,48},{48,56},{56,64},{64,7... | collective-permute-start | bytes 73736 | tf_op jit(solution)/shard_map/ppermute | solution.py:17
  127.4 4.6 %collective-permute-start.13 = (bf16[16,768]{1,0:T(8,128)(2,1)S(1)}, bf16[16,768]{1,0:T(8,128)(2,1)S(1)}, u32[]{:S(2)}, u32[]{:S(2)}) collective-permute-start(bf16[16,768]{1,0:T(8,128)(2,1)S(1)} %get-tuple-element.18.refs_0_), channel_id=1, source_target_pairs={{1,2},{2,1},{3,4},{4,3},{5,6},{6,5},{7,0},{0,7},{9,10},{10,9},{11,... | collective-permute-start | bytes 73736 | tf_op jit(solution)/shard_map/ppermute | solution.py:41
  132.0 1.9 %collective-permute-start.12 = (bf16[16,768]{1,0:T(8,128)(2,1)S(1)}, bf16[16,768]{1,0:T(8,128)(2,1)S(1)}, u32[]{:S(2)}, u32[]{:S(2)}) collective-permute-start(bf16[16,768]{1,0:T(8,128)(2,1)S(1)} %get-tuple-element.18.refs_0_), channel_id=1, source_target_pairs={{0,1},{1,0},{2,3},{3,2},{4,5},{5,4},{6,7},{7,6},{8,9},{9,8},{10,11... | collective-permute-start | bytes 73736 | tf_op jit(solution)/shard_map/ppermute | solution.py:41
  134.0 0.0 collective-permute-done.15.refs_4_
  134.0 0.3 collective-permute-done.14.refs_3_
  134.3 0.9 collective-permute-done.12.refs_1_
  135.1 1.3 shard_map.84
  (12 shorter events, 0.0 us)
Async XLA Ops:
  0.6 41.1 %copy-start.2 = (bf16[32,64,256]{2,1,0:T(8,128)(2,1)S(1)}, bf16[32,64,256]{2,1,0:T(8,128)(2,1)}, u32[]{:S(2)}) copy-start(bf16[32,64,256]{2,1,0:T(8,128)(2,1)} %inverse.3) | copy-start | bytes 3145732
  0.6 58.4 %copy-start = (bf16[1,768,1024]{2,1,0:T(8,128)(2,1)S(1)}, bf16[1,768,1024]{2,1,0:T(8,128)(2,1)}, u32[]{:S(2)}) copy-start(bf16[1,768,1024]{2,1,0:T(8,128)(2,1)} %param.8) | copy-start | bytes 4718596
  1.6 24.9 %collective-permute-start.3 = (bf16[16,768]{1,0:T(8,128)(2,1)S(1)}, bf16[16,768]{1,0:T(8,128)(2,1)S(1)}, u32[]{:S(2)}, u32[]{:S(2)}) collective-permute-start(bf16[16,768]{1,0:T(8,128)(2,1)S(1)} %bitcast_convert_fusion.v), channel_id=1, source_target_pairs={{0,504},{8,0},{16,8},{24,16},{32,24},{40,32},{48,40},{56,48},{64,5... | collective-permute-start | bytes 73736 | tf_op jit(solution)/shard_map/ppermute | solution.py:17
  16.3 10.2 %collective-permute-start.2 = (bf16[16,768]{1,0:T(8,128)(2,1)S(1)}, bf16[16,768]{1,0:T(8,128)(2,1)S(1)}, u32[]{:S(2)}, u32[]{:S(2)}) collective-permute-start(bf16[16,768]{1,0:T(8,128)(2,1)S(1)} %bitcast_convert_fusion.v), channel_id=1, source_target_pairs={{0,8},{8,16},{16,24},{24,32},{32,40},{40,48},{48,56},{56,64},{64,7... | collective-permute-start | bytes 73736 | tf_op jit(solution)/shard_map/ppermute | solution.py:17
  18.2 8.3 %collective-permute-start.1 = (bf16[16,768]{1,0:T(8,128)(2,1)S(1)}, bf16[16,768]{1,0:T(8,128)(2,1)S(1)}, u32[]{:S(2)}, u32[]{:S(2)}) collective-permute-start(bf16[16,768]{1,0:T(8,128)(2,1)S(1)} %bitcast_convert_fusion.v), channel_id=1, source_target_pairs={{1,2},{2,1},{3,4},{4,3},{5,6},{6,5},{7,0},{0,7},{9,10},{10,9},{11,... | collective-permute-start | bytes 73736 | tf_op jit(solution)/shard_map/ppermute | solution.py:41
  23.3 3.2 %collective-permute-start = (bf16[16,768]{1,0:T(8,128)(2,1)S(1)}, bf16[16,768]{1,0:T(8,128)(2,1)S(1)}, u32[]{:S(2)}, u32[]{:S(2)}) collective-permute-start(bf16[16,768]{1,0:T(8,128)(2,1)S(1)} %bitcast_convert_fusion.v), channel_id=1, source_target_pairs={{0,1},{1,0},{2,3},{3,2},{4,5},{5,4},{6,7},{7,6},{8,9},{9,8},{10,11... | collective-permute-start | bytes 73736 | tf_op jit(solution)/shard_map/ppermute | solution.py:41
  26.5 0.8 copy-start.3
  41.7 31.5 %copy-start.1 = (bf16[1,768,1024]{2,1,0:T(8,128)(2,1)S(1)}, bf16[1,768,1024]{2,1,0:T(8,128)(2,1)}, u32[]{:S(2)}) copy-start(bf16[1,768,1024]{2,1,0:T(8,128)(2,1)} %param.7) | copy-start | bytes 4718596
  41.7 31.5 %copy-start.5 = (f32[1,16,768]{2,1,0:T(8,128)S(1)}, f32[1,16,768]{2,1,0:T(8,128)}, u32[]{:S(2)}) copy-start(f32[1,16,768]{2,1,0:T(8,128)} %param.6) | copy-start | bytes 147460
  59.1 32.3 %copy-start.4 = (bf16[1,32,1024]{2,1,0:T(8,128)(2,1)S(1)}, bf16[1,32,1024]{2,1,0:T(8,128)(2,1)}, u32[]{:S(2)}) copy-start(bf16[1,32,1024]{2,1,0:T(8,128)(2,1)} %param.9) | copy-start | bytes 196612
  59.8 12.3 %collective-permute-start.7 = (bf16[16,768]{1,0:T(8,128)(2,1)S(1)}, bf16[16,768]{1,0:T(8,128)(2,1)S(1)}, u32[]{:S(2)}, u32[]{:S(2)}) collective-permute-start(bf16[16,768]{1,0:T(8,128)(2,1)S(1)} %get-tuple-element.14.refs_0_), channel_id=1, source_target_pairs={{0,504},{8,0},{16,8},{24,16},{32,24},{40,32},{48,40},{56,48},{64,5... | collective-permute-start | bytes 73736 | tf_op jit(solution)/shard_map/ppermute | solution.py:17
  63.2 8.8 %collective-permute-start.6 = (bf16[16,768]{1,0:T(8,128)(2,1)S(1)}, bf16[16,768]{1,0:T(8,128)(2,1)S(1)}, u32[]{:S(2)}, u32[]{:S(2)}) collective-permute-start(bf16[16,768]{1,0:T(8,128)(2,1)S(1)} %get-tuple-element.14.refs_0_), channel_id=1, source_target_pairs={{0,8},{8,16},{16,24},{24,32},{32,40},{40,48},{48,56},{56,64},{64,7... | collective-permute-start | bytes 73736 | tf_op jit(solution)/shard_map/ppermute | solution.py:17
  65.2 6.9 %collective-permute-start.5 = (bf16[16,768]{1,0:T(8,128)(2,1)S(1)}, bf16[16,768]{1,0:T(8,128)(2,1)S(1)}, u32[]{:S(2)}, u32[]{:S(2)}) collective-permute-start(bf16[16,768]{1,0:T(8,128)(2,1)S(1)} %get-tuple-element.14.refs_0_), channel_id=1, source_target_pairs={{1,2},{2,1},{3,4},{4,3},{5,6},{6,5},{7,0},{0,7},{9,10},{10,9},{11,... | collective-permute-start | bytes 73736 | tf_op jit(solution)/shard_map/ppermute | solution.py:41
  70.1 3.1 %collective-permute-start.4 = (bf16[16,768]{1,0:T(8,128)(2,1)S(1)}, bf16[16,768]{1,0:T(8,128)(2,1)S(1)}, u32[]{:S(2)}, u32[]{:S(2)}) collective-permute-start(bf16[16,768]{1,0:T(8,128)(2,1)S(1)} %get-tuple-element.14.refs_0_), channel_id=1, source_target_pairs={{0,1},{1,0},{2,3},{3,2},{4,5},{5,4},{6,7},{7,6},{8,9},{9,8},{10,11... | collective-permute-start | bytes 73736 | tf_op jit(solution)/shard_map/ppermute | solution.py:41
  73.8 16.7 %collective-permute-start.11 = (bf16[16,768]{1,0:T(8,128)(2,1)S(1)}, bf16[16,768]{1,0:T(8,128)(2,1)S(1)}, u32[]{:S(2)}, u32[]{:S(2)}) collective-permute-start(bf16[16,768]{1,0:T(8,128)(2,1)S(1)} %shard_map.80.v), channel_id=1, source_target_pairs={{0,504},{8,0},{16,8},{24,16},{32,24},{40,32},{48,40},{56,48},{64,5... | collective-permute-start | bytes 73736 | tf_op jit(solution)/shard_map/ppermute | solution.py:17
  81.2 9.3 %collective-permute-start.10 = (bf16[16,768]{1,0:T(8,128)(2,1)S(1)}, bf16[16,768]{1,0:T(8,128)(2,1)S(1)}, u32[]{:S(2)}, u32[]{:S(2)}) collective-permute-start(bf16[16,768]{1,0:T(8,128)(2,1)S(1)} %shard_map.80.v), channel_id=1, source_target_pairs={{0,8},{8,16},{16,24},{24,32},{32,40},{40,48},{48,56},{56,64},{64,7... | collective-permute-start | bytes 73736 | tf_op jit(solution)/shard_map/ppermute | solution.py:17
  83.1 7.4 %collective-permute-start.9 = (bf16[16,768]{1,0:T(8,128)(2,1)S(1)}, bf16[16,768]{1,0:T(8,128)(2,1)S(1)}, u32[]{:S(2)}, u32[]{:S(2)}) collective-permute-start(bf16[16,768]{1,0:T(8,128)(2,1)S(1)} %shard_map.80.v), channel_id=1, source_target_pairs={{1,2},{2,1},{3,4},{4,3},{5,6},{6,5},{7,0},{0,7},{9,10},{10,9},{11,... | collective-permute-start | bytes 73736 | tf_op jit(solution)/shard_map/ppermute | solution.py:41
  86.4 4.9 %collective-permute-start.8 = (bf16[16,768]{1,0:T(8,128)(2,1)S(1)}, bf16[16,768]{1,0:T(8,128)(2,1)S(1)}, u32[]{:S(2)}, u32[]{:S(2)}) collective-permute-start(bf16[16,768]{1,0:T(8,128)(2,1)S(1)} %shard_map.80.v), channel_id=1, source_target_pairs={{0,1},{1,0},{2,3},{3,2},{4,5},{5,4},{6,7},{7,6},{8,9},{9,8},{10,11... | collective-permute-start | bytes 73736 | tf_op jit(solution)/shard_map/ppermute | solution.py:41
  122.0 11.9 %collective-permute-start.15 = (bf16[16,768]{1,0:T(8,128)(2,1)S(1)}, bf16[16,768]{1,0:T(8,128)(2,1)S(1)}, u32[]{:S(2)}, u32[]{:S(2)}) collective-permute-start(bf16[16,768]{1,0:T(8,128)(2,1)S(1)} %get-tuple-element.18.refs_0_), channel_id=1, source_target_pairs={{0,504},{8,0},{16,8},{24,16},{32,24},{40,32},{48,40},{56,48},{64,5... | collective-permute-start | bytes 73736 | tf_op jit(solution)/shard_map/ppermute | solution.py:17
  125.5 8.8 %collective-permute-start.14 = (bf16[16,768]{1,0:T(8,128)(2,1)S(1)}, bf16[16,768]{1,0:T(8,128)(2,1)S(1)}, u32[]{:S(2)}, u32[]{:S(2)}) collective-permute-start(bf16[16,768]{1,0:T(8,128)(2,1)S(1)} %get-tuple-element.18.refs_0_), channel_id=1, source_target_pairs={{0,8},{8,16},{16,24},{24,32},{32,40},{40,48},{48,56},{56,64},{64,7... | collective-permute-start | bytes 73736 | tf_op jit(solution)/shard_map/ppermute | solution.py:17
  127.4 6.9 %collective-permute-start.13 = (bf16[16,768]{1,0:T(8,128)(2,1)S(1)}, bf16[16,768]{1,0:T(8,128)(2,1)S(1)}, u32[]{:S(2)}, u32[]{:S(2)}) collective-permute-start(bf16[16,768]{1,0:T(8,128)(2,1)S(1)} %get-tuple-element.18.refs_0_), channel_id=1, source_target_pairs={{1,2},{2,1},{3,4},{4,3},{5,6},{6,5},{7,0},{0,7},{9,10},{10,9},{11,... | collective-permute-start | bytes 73736 | tf_op jit(solution)/shard_map/ppermute | solution.py:41
  132.0 3.1 %collective-permute-start.12 = (bf16[16,768]{1,0:T(8,128)(2,1)S(1)}, bf16[16,768]{1,0:T(8,128)(2,1)S(1)}, u32[]{:S(2)}, u32[]{:S(2)}) collective-permute-start(bf16[16,768]{1,0:T(8,128)(2,1)S(1)} %get-tuple-element.18.refs_0_), channel_id=1, source_target_pairs={{0,1},{1,0},{2,3},{3,2},{4,5},{5,4},{6,7},{7,6},{8,9},{9,8},{10,11... | collective-permute-start | bytes 73736 | tf_op jit(solution)/shard_map/ppermute | solution.py:41

commit v4 on v3

v4 whole, which is shorter than its diff:
```python
import jax
import jax.numpy as jnp
from jax import lax
from jax.experimental import pallas as pl
from jax.experimental.pallas import tpu as pltpu
from jax.sharding import PartitionSpec as P

ITERS = 2
LANES = 128
HALF = 64
CASES = 16
DIGIT = 32
F32 = jnp.float32
BF16 = jnp.bfloat16
VMEM = pltpu.VMEM


def from_behind(shard, axis, by):
    peers = lax.axis_size(axis)
    return lax.ppermute(shard, axis, [(i, (i + by) % peers) for i in range(peers)])


def exchanged(shard, axis, first):
    peers = lax.axis_size(axis)
    pairs = [((first + i) % peers, (first + (i ^ 1)) % peers) for i in range(peers)]
    return lax.ppermute(shard, axis, pairs)


def call(body, outs, *args):
    return pl.pallas_call(
        body,
        out_shape=[jax.ShapeDtypeStruct(shape, dtype) for shape, dtype in outs],
        in_specs=[pl.BlockSpec(memory_space=VMEM)] * len(args),
        out_specs=[pl.BlockSpec(memory_space=VMEM)] * len(outs),
        compiler_params=pltpu.CompilerParams(vmem_limit_bytes=16 * 2**20),
        cost_estimate=pl.CostEstimate(flops=2**24, bytes_accessed=2**19, transcendentals=0),
    )(*args)


def dot_nt(left, right):
    return lax.dot_general(left, right, (((1,), (1,)), ((), ())), preferred_element_type=F32)


def dot_nn(left, right):
    return jnp.dot(left, right, preferred_element_type=F32)


def even_member():
    return lax.rem(lax.axis_index("member"), 2) == 0


def tall(rows):
    return jnp.concatenate([rows] * (LANES // rows.shape[0]), axis=0)


def lanes(shape):
    return lax.broadcasted_iota(jnp.int32, shape, 1)


def margins(lower, upper, pair, other, picks):
    every = dot_nn(jnp.concatenate([lower, upper, pair, other], axis=0), picks)
    source = lanes((CASES, picks.shape[1])) // HALF
    owner = jnp.where((source >= 2) & even_member(), 5 - source, source)
    kept = every[:CASES]
    for d in range(1, 4):
        kept = jnp.where(owner == d, every[d * CASES : (d + 1) * CASES], kept)
    return kept.astype(BF16)


def prepare_body(rows, basis, picks, held, for_pair, for_other):
    lists = rows[0]
    nb = basis.shape[1]
    owned = picks.shape[0]
    flat = jnp.concatenate([lists[d : d + 1] for d in range(4)], axis=1)
    spots = lax.broadcasted_iota(jnp.int32, picks.shape, 0)
    picks[...] = jnp.where(spots == flat, 1.0, 0.0).astype(BF16)
    held[...] = basis[...]
    even = even_member()
    edge = basis[:, nb - LANES :].astype(F32)
    edge = jnp.where(even, edge, pltpu.roll(edge, HALF, 1))
    turn = jnp.where(even, flat[:, LANES:], jnp.concatenate([lists[3:4], lists[2:3]], axis=1))
    high = jnp.broadcast_to((turn // DIGIT).astype(F32), edge.shape)
    low = jnp.broadcast_to((turn % DIGIT).astype(F32), edge.shape)
    parts = jnp.concatenate([edge, high, low], axis=1)
    side = lanes(parts.shape) % LANES >= HALF
    half = parts.shape[0] // 2
    for out, mine in ((for_pair, side), (for_other, jnp.logical_not(side))):
        kept = jnp.where(mine, parts, 0.0).astype(BF16)
        out[...] = jnp.concatenate([kept[:half], kept[half:]], axis=1)


def restrict_body(v, pair, other, lower, upper, picks, basis, block, coef):
    edge = margins(lower[...], upper[...], pair[...], other[...], picks[...])
    whole = jnp.concatenate([v[...], edge], axis=1)
    block[...] = whole
    part = dot_nt(basis[...], tall(whole)).astype(BF16)
    for m in range(coef.shape[0]):
        coef[m] = part


def mixed_body(v, lower, upper, pair, other, picks, basis, edge, message):
    value = v[...]
    rows = jnp.concatenate([lower[...], upper[...]], axis=0)
    every = dot_nn(rows, picks[:, :LANES])
    lane = lanes((CASES, LANES))
    near = jnp.where(lane < HALF, every[:CASES], every[CASES:]).astype(BF16)
    edge[...] = near
    known = jnp.concatenate([value, near], axis=1)
    own = dot_nt(basis[:, : known.shape[1]], tall(known))
    width = 3 * LANES
    unfold = lambda ref: jnp.concatenate([ref[CASES:, :width], ref[CASES:, width:]], axis=0)
    first, second = unfold(pair), unfold(other)
    digits = (first[:1, LANES:] + second[:1, LANES:]).astype(F32)
    spot = (digits[:, :LANES] * DIGIT + digits[:, LANES:]).astype(jnp.int32)
    choice = lax.broadcasted_iota(jnp.int32, (value.shape[1], LANES), 0) == spot
    chosen = dot_nn(value, jnp.where(choice, 1.0, 0.0).astype(BF16))
    spread = tall(chosen.astype(BF16))
    to_first = dot_nt(first[:, :LANES], spread)
    to_second = dot_nt(second[:, :LANES], spread)
    head = own.astype(BF16).astype(F32)
    place = lanes(own.shape) // CASES
    out = jnp.concatenate([chosen, pltpu.roll(chosen, HALF, 1)], axis=0)
    out = jnp.where(place == 3, to_second, out)
    out = jnp.where(place == 2, to_first, out)
    out = jnp.where(place == 1, own - head, out)
    out = jnp.where(place == 0, head, out).astype(BF16)
    for m in range(message.shape[0]):
        message[m] = out


def shares_of(every, inverse, share):
    per = LANES // CASES
    lane = lanes(every.shape) // CASES
    tiles = inverse.shape[0] // per
    sums = [None] * tiles
    for q in range(per):
        here = jnp.where(lane == q, every, jnp.zeros_like(every))
        for t in range(tiles):
            term = dot_nn(inverse[per * t + q], here)
            sums[t] = term if sums[t] is None else sums[t] + term
    for t in range(tiles):
        share[:, t, :] = sums[t]


def coarse_body(coef, inverse, share):
    shares_of(coef[...].reshape(-1, LANES), inverse, share)


def coarse_mixed_body(message, inverse, share):
    peers, kdef, _ = message.shape
    source = lax.broadcasted_iota(jnp.int32, (LANES, 3 * LANES), 0)
    target = lanes((LANES, 3 * LANES))
    group = source // CASES
    part = jnp.where(group < 2, 0, group - 1)
    hit = (part == target // LANES) & (source % CASES == target % CASES)
    parts = dot_nn(message[...].reshape(peers * kdef, LANES), jnp.where(hit, 1.0, 0.0).astype(BF16))
    every = []
    for m in range(peers):
        pair = m ^ 1
        other = (m + 1) % peers if m % 2 else (m - 1) % peers
        at = lambda k, j: parts[k * kdef : (k + 1) * kdef, j * LANES : (j + 1) * LANES]
        every.append(at(m, 0) + at(pair, 1) + at(other, 2))
    shares_of(jnp.concatenate(every, axis=0).astype(BF16), inverse, share)


def prolong_of(arrived, kdef):
    total = jnp.sum(arrived, axis=0)
    tiles = total.shape[0]
    row = lax.broadcasted_iota(jnp.int32, (CASES, LANES), 0)
    lane = lanes((CASES, LANES))
    out = None
    for t in range(tiles):
        spread = jnp.where(lane % CASES == row, total[t : t + 1], 0.0).astype(BF16)
        target = lax.broadcasted_iota(jnp.int32, (LANES, kdef), 0) // CASES + t * (LANES // CASES)
        onto = (target == lanes((LANES, kdef))).astype(BF16)
        term = dot_nn(spread, onto)
        out = term if out is None else out + term
    return out.astype(BF16)


def correct_body(arrived, block, inverse, basis, for_pair, for_other, total, rounded, pair, other):
    value = dot_nt(block[...], inverse[...])
    prolong = prolong_of(arrived[...], basis.shape[0])
    value = value + dot_nn(prolong, basis[:, : total.shape[1]])
    total[...] = value
    short = value.astype(BF16)
    rounded[...] = short
    for out, more in ((pair, for_pair), (other, for_other)):
        out[:CASES] = short
        out[CASES:] = more[...]


def correct_mixed_body(arrived, v, edge, message, inverse, basis, before, total, rounded):
    me = lax.axis_index("member")
    peers = message.shape[0]
    even = even_member()
    pair = jnp.where(even, me + 1, me - 1)
    other = lax.rem(jnp.where(even, me + peers - 1, me + 1), peers)
    from_pair = message[pair, :CASES].astype(F32)
    from_other = message[other, CASES:].astype(F32)
    high = jnp.where(even, from_pair, from_other)
    low = jnp.where(even, from_other, from_pair)
    far = jnp.where(lanes(high.shape) < HALF, pltpu.roll(low, HALF, 1), high).astype(BF16)
    block = jnp.concatenate([v[...], edge[...], far], axis=1)
    value = dot_nt(block, inverse[...])
    prolong = prolong_of(arrived[...], basis.shape[0])
    value = before[...] + (value + dot_nn(prolong, basis[:, : total.shape[1]]))
    total[...] = value
    rounded[...] = value.astype(BF16)


def residual_body(last, v, pair, other, lower, upper, picks, stiff, load, *rest):
    edge = margins(lower[...], upper[...], pair[:CASES], other[:CASES], picks[...])
    whole = jnp.concatenate([v[...], edge], axis=1)
    value = load[...] - dot_nt(whole, stiff[...])
    if last:
        total, out, passed = rest
        passed[...] = total[...]
        out[...] = value
    else:
        rest[0][...] = value.astype(BF16)


def local(load, stiffness, block_inverse, deflation, margin_rows, coarse_inverse):
    own_load = load[0]
    stiff_rows = stiffness[0]
    inverse_rows = block_inverse[0]
    cases, owned = own_load.shape
    kdef, nb = deflation.shape[1:]
    groups = lax.axis_size("group")
    members = lax.axis_size("member")
    tiles = coarse_inverse.shape[0] * cases // LANES

    def group_around(values):
        return from_behind(values, "group", 1), from_behind(values, "group", -1)

    def member_around(for_pair, for_other):
        return exchanged(for_pair, "member", 0), exchanged(for_other, "member", 1)

    field = own_load.astype(BF16)
    near = member_around(field, field)
    far = group_around(field)
    picks, basis, for_pair, for_other = call(
        prepare_body,
        [((owned, nb - owned), BF16), ((kdef, nb), BF16)] + [((kdef // 2, 6 * LANES), BF16)] * 2,
        margin_rows, deflation[0],
    )
    block, coef = call(
        restrict_body,
        [((cases, nb), BF16), ((members, kdef, LANES), BF16)],
        field, *near, *far, picks, basis,
    )
    gathered = lax.all_to_all(coef, "member", 0, 0, tiled=True)
    share_shape = [((groups, tiles, LANES), F32)]
    (share,) = call(coarse_body, share_shape, gathered, coarse_inverse)
    arrived = lax.all_to_all(share, "group", 0, 0, tiled=True)
    total, rounded, for_pair, for_other = call(
        correct_body,
        [((cases, owned), F32), ((cases, owned), BF16)] + [((cases + kdef // 2, owned), BF16)] * 2,
        arrived, block, inverse_rows, basis, for_pair, for_other,
    )
    near = member_around(for_pair, for_other)
    (field,) = call(
        lambda *refs: residual_body(False, *refs),
        [((cases, owned), BF16)],
        rounded, *near, *group_around(rounded), picks, stiff_rows, own_load,
    )

    edge, message = call(
        mixed_body,
        [((cases, LANES), BF16), ((members, kdef, LANES), BF16)],
        field, *group_around(field), *near, picks, basis,
    )
    message = lax.all_to_all(message, "member", 0, 0, tiled=True)
    (share,) = call(coarse_mixed_body, share_shape, message, coarse_inverse)
    arrived = lax.all_to_all(share, "group", 0, 0, tiled=True)
    total, rounded = call(
        correct_mixed_body,
        [((cases, owned), F32), ((cases, owned), BF16)],
        arrived, field, edge, message, inverse_rows, basis, total,
    )
    residual, solution_out = call(
        lambda *refs: residual_body(True, *refs),
        [((cases, owned), F32)] * 2,
        rounded, *member_around(rounded, rounded), *group_around(rounded), picks, stiff_rows, own_load, total,
    )
    return (solution_out[None], residual[None])


def solution(mesh):
    placed = (
        P(("group", "member"), None, None),
        P(("group", "member"), None, None),
        P(("group", "member"), None, None),
        P(("group", "member"), None, None),
        P(("group", "member"), None, None),
        P("member", None, "group"),
    )
    return jax.shard_map(
        local,
        mesh=mesh,
        in_specs=placed,
        out_specs=(P(("group", "member"), None, None), P(("group", "member"), None, None)),
        check_vma=False,
    )
```

time: 138 us -> 136 us (0.986)
  starting transfers between devices: 64.7 us -> 52.6 us
  waiting for transfers between devices: 3.1 us -> 13.3 us
    all_to_all x0 -> x1, blocking collectives: none -> 15.1 us  [local(): message = lax.all_to_all(message, 'member', 0, 0, tiled=True)]
    ppermute x8, waiting for transfers between devices: 0.3 us -> 13.3 us  [from_behind(): lax.ppermute(shard, axis, [(i, (i + by) % peers) for i in range(peers)])]
    all_to_all x2 -> x1, blocking collectives: 26 us -> 13.2 us  [local(): gathered = lax.all_to_all(coef, 'member', 0, 0, tiled=True)]
    ppermute x8 -> x6, starting transfers between devices: 28 us -> 19.4 us  [exchanged(): return lax.ppermute(shard, axis, pairs)]
    all_to_all x2, blocking collectives: 33.9 us -> 30.2 us  [local(): arrived = lax.all_to_all(share, 'group', 0, 0, tiled=True)]
    ppermute x8, starting transfers between devices: 36.6 us -> 33.2 us  [from_behind(): lax.ppermute(shard, axis, [(i, (i + by) % peers) for i in range(peers)])]
    ppermute x8 -> x6, waiting for transfers between devices: 2.81 us -> 0.02 us  [exchanged(): return lax.ppermute(shard, axis, pairs)]
    unnamed x12 -> x14, local copies, waits for them, and re-layouts: 0.85 us -> 2.76 us
  transfers between devices with their start and end apart: 16 -> 14, of which waited for: 4 -> 3; matrix products, arithmetic and copies ran while one was open for 1% -> 0% of each run, Pallas kernels for 0% -> 0%
where the time goes in v4:
time: 136 us; the launch traced here: 135 us
  blocking collectives  58.6 us (43%)
  starting transfers between devices  52.6 us (39%)
  waiting for transfers between devices  13.3 us (10%)
  Pallas kernels  5.63 us (4%)
  local copies, waits for them, and re-layouts  2.76 us (2%)
    ppermute x8, starting transfers between devices, from_behind(): lax.ppermute(shard, axis, [(i, (i + by) % peers) for i in range(peers)])  33.2 us
    all_to_all x2, blocking collectives, local(): arrived = lax.all_to_all(share, 'group', 0, 0, tiled=True)  30.2 us
    ppermute x6, starting transfers between devices, exchanged(): return lax.ppermute(shard, axis, pairs)  19.4 us
    all_to_all x1, blocking collectives, local(): message = lax.all_to_all(message, 'member', 0, 0, tiled=True)  15.1 us
    ppermute x8, waiting for transfers between devices, from_behind(): lax.ppermute(shard, axis, [(i, (i + by) % peers) for i in range(peers)])  13.3 us
    all_to_all x1, blocking collectives, local(): gathered = lax.all_to_all(coef, 'member', 0, 0, tiled=True)  13.2 us
    pallas_call x9, Pallas kernels, call(): pl.pallas_call(body, out_shape=[jax.ShapeDtypeStruct(shape, dtype) for sh...  5.63 us
    unnamed x14, local copies, waits for them, and re-layouts  2.76 us
  transfers between devices with their start and end apart: 14, of which 3 were waited for; matrix products, arithmetic and copies ran while one was open for 0% of the time, Pallas kernels for 0%

profile of v4, /device:TPU:1, one launch (start us, length us, event | category | flops | bytes accessed | tf_op | source)
XLA Modules:
  0.0 134.7 jit_solution(6111267989427029998)
XLA Ops:
  0.6 0.0 copy-start
  0.6 0.9 bitcast_convert_fusion.v
  1.6 14.7 %collective-permute-start.3 = (bf16[16,768]{1,0:T(8,128)(2,1)S(1)}, bf16[16,768]{1,0:T(8,128)(2,1)S(1)}, u32[]{:S(2)}, u32[]{:S(2)}) collective-permute-start(bf16[16,768]{1,0:T(8,128)(2,1)S(1)} %bitcast_convert_fusion.v), channel_id=1, source_target_pairs={{0,504},{8,0},{16,8},{24,16},{32,24},{40,32},{48,40},{56,48},{64,5... | collective-permute-start | bytes 73736 | tf_op jit(solution)/shard_map/ppermute | solution.py:20
  16.3 1.9 %collective-permute-start.2 = (bf16[16,768]{1,0:T(8,128)(2,1)S(1)}, bf16[16,768]{1,0:T(8,128)(2,1)S(1)}, u32[]{:S(2)}, u32[]{:S(2)}) collective-permute-start(bf16[16,768]{1,0:T(8,128)(2,1)S(1)} %bitcast_convert_fusion.v), channel_id=1, source_target_pairs={{0,8},{8,16},{16,24},{24,32},{32,40},{40,48},{48,56},{56,64},{64,7... | collective-permute-start | bytes 73736 | tf_op jit(solution)/shard_map/ppermute | solution.py:20
  18.2 5.1 %collective-permute-start.1 = (bf16[16,768]{1,0:T(8,128)(2,1)S(1)}, bf16[16,768]{1,0:T(8,128)(2,1)S(1)}, u32[]{:S(2)}, u32[]{:S(2)}) collective-permute-start(bf16[16,768]{1,0:T(8,128)(2,1)S(1)} %bitcast_convert_fusion.v), channel_id=1, source_target_pairs={{1,2},{2,1},{3,4},{4,3},{5,6},{6,5},{7,0},{0,7},{9,10},{10,9},{11,... | collective-permute-start | bytes 73736 | tf_op jit(solution)/shard_map/ppermute | solution.py:26
  23.2 2.2 %collective-permute-start = (bf16[16,768]{1,0:T(8,128)(2,1)S(1)}, bf16[16,768]{1,0:T(8,128)(2,1)S(1)}, u32[]{:S(2)}, u32[]{:S(2)}) collective-permute-start(bf16[16,768]{1,0:T(8,128)(2,1)S(1)} %bitcast_convert_fusion.v), channel_id=1, source_target_pairs={{0,1},{1,0},{2,3},{3,2},{4,5},{5,4},{6,7},{7,6},{8,9},{9,8},{10,11... | collective-permute-start | bytes 73736 | tf_op jit(solution)/shard_map/ppermute | solution.py:26
  25.5 0.0 copy-start.5
  25.5 0.8 copy-done.5
  26.3 0.7 copy-done.6
  27.0 0.2 shard_map.77
  27.2 0.0 collective-permute-done.3.upper
  27.3 0.0 collective-permute-done.2.lower
  27.3 0.0 collective-permute-done.1.other
  27.3 0.0 collective-permute-done.pair
  27.3 0.4 shard_map.78
  27.7 13.2 %all_to_all.20.coef = bf16[8,32,128]{2,1,0:T(8,128)(2,1)S(1)} all-to-all(bf16[8,32,128]{2,1,0:T(8,128)(2,1)S(1)} %get-tuple-element.20), channel_id=1, replica_groups=mesh['group'=64,'member'=8] {'member'}, dimensions={0} | all-to-all | bytes 131072 | tf_op jit(solution)/shard_map/all_to_all | solution.py:253
  40.9 1.2 copy-done.2
  42.1 0.5 shard_map.79
  42.6 16.8 %all_to_all.21.arrived = f32[64,4,128]{2,1,0:T(4,128)S(1)} all-to-all(f32[64,4,128]{2,1,0:T(4,128)S(1)} %shard_map.79), channel_id=1, replica_groups=mesh['group'=64,'member'=8] {'group'}, dimensions={0} | all-to-all | bytes 262144 | tf_op jit(solution)/shard_map/all_to_all | solution.py:256
  59.4 0.7 shard_map.80
  60.2 0.0 copy-start.3
  60.2 4.2 %collective-permute-start.4 = (bf16[32,768]{1,0:T(8,128)(2,1)S(1)}, bf16[32,768]{1,0:T(8,128)(2,1)S(1)}, u32[]{:S(2)}, u32[]{:S(2)}) collective-permute-start(bf16[32,768]{1,0:T(8,128)(2,1)S(1)} %get-tuple-element.25), channel_id=1, source_target_pairs={{0,1},{1,0},{2,3},{3,2},{4,5},{5,4},{6,7},{7,6},{8,9},{9,8},{10,11... | collective-permute-start | bytes 147464 | tf_op jit(solution)/shard_map/ppermute | solution.py:26
  64.4 2.3 %collective-permute-start.5 = (bf16[32,768]{1,0:T(8,128)(2,1)S(1)}, bf16[32,768]{1,0:T(8,128)(2,1)S(1)}, u32[]{:S(2)}, u32[]{:S(2)}) collective-permute-start(bf16[32,768]{1,0:T(8,128)(2,1)S(1)} %get-tuple-element.26), channel_id=1, source_target_pairs={{1,2},{2,1},{3,4},{4,3},{5,6},{6,5},{7,0},{0,7},{9,10},{10,9},{11,... | collective-permute-start | bytes 147464 | tf_op jit(solution)/shard_map/ppermute | solution.py:26
  66.7 3.1 %collective-permute-start.7 = (bf16[16,768]{1,0:T(8,128)(2,1)S(1)}, bf16[16,768]{1,0:T(8,128)(2,1)S(1)}, u32[]{:S(2)}, u32[]{:S(2)}) collective-permute-start(bf16[16,768]{1,0:T(8,128)(2,1)S(1)} %get-tuple-element.24.refs_0_), channel_id=1, source_target_pairs={{0,504},{8,0},{16,8},{24,16},{32,24},{40,32},{48,40},{56,48},{64,5... | collective-permute-start | bytes 73736 | tf_op jit(solution)/shard_map/ppermute | solution.py:20
  69.8 2.1 %collective-permute-start.6 = (bf16[16,768]{1,0:T(8,128)(2,1)S(1)}, bf16[16,768]{1,0:T(8,128)(2,1)S(1)}, u32[]{:S(2)}, u32[]{:S(2)}) collective-permute-start(bf16[16,768]{1,0:T(8,128)(2,1)S(1)} %get-tuple-element.24.refs_0_), channel_id=1, source_target_pairs={{0,8},{8,16},{16,24},{24,32},{32,40},{40,48},{48,56},{56,64},{64,7... | collective-permute-start | bytes 73736 | tf_op jit(solution)/shard_map/ppermute | solution.py:20
  72.0 0.0 collective-permute-done.7.refs_4_
  72.0 6.6 %collective-permute-done.6.refs_3_ = bf16[16,768]{1,0:T(8,128)(2,1)S(1)} collective-permute-done((bf16[16,768]{1,0:T(8,128)(2,1)S(1)}, bf16[16,768]{1,0:T(8,128)(2,1)S(1)}, u32[]{:S(2)}, u32[]{:S(2)}) %collective-permute-start.6) | collective-permute-done | bytes 24608 | tf_op jit(solution)/shard_map/ppermute | solution.py:20
  78.6 0.0 collective-permute-done.4.refs_1_.pair
  78.6 0.0 collective-permute-done.5.refs_2_.other
  78.6 0.6 shard_map.81.v
  79.2 1.9 %collective-permute-start.9 = (bf16[16,768]{1,0:T(8,128)(2,1)S(1)}, bf16[16,768]{1,0:T(8,128)(2,1)S(1)}, u32[]{:S(2)}, u32[]{:S(2)}) collective-permute-start(bf16[16,768]{1,0:T(8,128)(2,1)S(1)} %shard_map.81.v), channel_id=1, source_target_pairs={{0,504},{8,0},{16,8},{24,16},{32,24},{40,32},{48,40},{56,48},{64,5... | collective-permute-start | bytes 73736 | tf_op jit(solution)/shard_map/ppermute | solution.py:20
  81.2 3.4 %collective-permute-start.8 = (bf16[16,768]{1,0:T(8,128)(2,1)S(1)}, bf16[16,768]{1,0:T(8,128)(2,1)S(1)}, u32[]{:S(2)}, u32[]{:S(2)}) collective-permute-start(bf16[16,768]{1,0:T(8,128)(2,1)S(1)} %shard_map.81.v), channel_id=1, source_target_pairs={{0,8},{8,16},{16,24},{24,32},{32,40},{40,48},{48,56},{56,64},{64,7... | collective-permute-start | bytes 73736 | tf_op jit(solution)/shard_map/ppermute | solution.py:20
  84.6 0.0 collective-permute-done.9.upper
  84.6 5.4 %collective-permute-done.8.lower = bf16[16,768]{1,0:T(8,128)(2,1)S(1)} collective-permute-done((bf16[16,768]{1,0:T(8,128)(2,1)S(1)}, bf16[16,768]{1,0:T(8,128)(2,1)S(1)}, u32[]{:S(2)}, u32[]{:S(2)}) %collective-permute-start.8) | collective-permute-done | bytes 24608 | tf_op jit(solution)/shard_map/ppermute | solution.py:20
  90.0 0.5 shard_map.82
  90.5 15.1 %all_to_all.22.message = bf16[8,32,128]{2,1,0:T(8,128)(2,1)S(1)} all-to-all(bf16[8,32,128]{2,1,0:T(8,128)(2,1)S(1)} %get-tuple-element.27), channel_id=1, replica_groups=mesh['group'=64,'member'=8] {'member'}, dimensions={0} | all-to-all | bytes 131072 | tf_op jit(solution)/shard_map/all_to_all | solution.py:274
  105.7 0.7 shard_map.83
  106.3 13.4 %all_to_all.23.arrived = f32[64,4,128]{2,1,0:T(4,128)S(1)} all-to-all(f32[64,4,128]{2,1,0:T(4,128)S(1)} %shard_map.83), channel_id=1, replica_groups=mesh['group'=64,'member'=8] {'group'}, dimensions={0} | all-to-all | bytes 262144 | tf_op jit(solution)/shard_map/all_to_all | solution.py:276
  119.8 0.7 shard_map.84
  120.5 4.1 %collective-permute-start.13 = (bf16[16,768]{1,0:T(8,128)(2,1)S(1)}, bf16[16,768]{1,0:T(8,128)(2,1)S(1)}, u32[]{:S(2)}, u32[]{:S(2)}) collective-permute-start(bf16[16,768]{1,0:T(8,128)(2,1)S(1)} %get-tuple-element.30.refs_0_), channel_id=1, source_target_pairs={{0,504},{8,0},{16,8},{24,16},{32,24},{40,32},{48,40},{56,48},{64,5... | collective-permute-start | bytes 73736 | tf_op jit(solution)/shard_map/ppermute | solution.py:20
  124.6 1.9 %collective-permute-start.12 = (bf16[16,768]{1,0:T(8,128)(2,1)S(1)}, bf16[16,768]{1,0:T(8,128)(2,1)S(1)}, u32[]{:S(2)}, u32[]{:S(2)}) collective-permute-start(bf16[16,768]{1,0:T(8,128)(2,1)S(1)} %get-tuple-element.30.refs_0_), channel_id=1, source_target_pairs={{0,8},{8,16},{16,24},{24,32},{32,40},{40,48},{48,56},{56,64},{64,7... | collective-permute-start | bytes 73736 | tf_op jit(solution)/shard_map/ppermute | solution.py:20
  126.5 3.6 %collective-permute-start.11 = (bf16[16,768]{1,0:T(8,128)(2,1)S(1)}, bf16[16,768]{1,0:T(8,128)(2,1)S(1)}, u32[]{:S(2)}, u32[]{:S(2)}) collective-permute-start(bf16[16,768]{1,0:T(8,128)(2,1)S(1)} %get-tuple-element.30.refs_0_), channel_id=1, source_target_pairs={{1,2},{2,1},{3,4},{4,3},{5,6},{6,5},{7,0},{0,7},{9,10},{10,9},{11,... | collective-permute-start | bytes 73736 | tf_op jit(solution)/shard_map/ppermute | solution.py:26
  130.2 1.9 %collective-permute-start.10 = (bf16[16,768]{1,0:T(8,128)(2,1)S(1)}, bf16[16,768]{1,0:T(8,128)(2,1)S(1)}, u32[]{:S(2)}, u32[]{:S(2)}) collective-permute-start(bf16[16,768]{1,0:T(8,128)(2,1)S(1)} %get-tuple-element.30.refs_0_), channel_id=1, source_target_pairs={{0,1},{1,0},{2,3},{3,2},{4,5},{5,4},{6,7},{7,6},{8,9},{9,8},{10,11... | collective-permute-start | bytes 73736 | tf_op jit(solution)/shard_map/ppermute | solution.py:26
  132.1 0.0 collective-permute-done.13.refs_4_
  132.1 1.3 collective-permute-done.12.refs_3_
  133.4 0.0 collective-permute-done.11.refs_2_
  133.4 0.0 collective-permute-done.10.refs_1_
  133.4 1.3 shard_map.85
  (8 shorter events, 0.0 us)
Async XLA Ops:
  0.6 58.8 %copy-start = (bf16[1,768,1024]{2,1,0:T(8,128)(2,1)S(1)}, bf16[1,768,1024]{2,1,0:T(8,128)(2,1)}, u32[]{:S(2)}) copy-start(bf16[1,768,1024]{2,1,0:T(8,128)(2,1)} %param.8) | copy-start | bytes 4718596
  1.6 25.7 %collective-permute-start.3 = (bf16[16,768]{1,0:T(8,128)(2,1)S(1)}, bf16[16,768]{1,0:T(8,128)(2,1)S(1)}, u32[]{:S(2)}, u32[]{:S(2)}) collective-permute-start(bf16[16,768]{1,0:T(8,128)(2,1)S(1)} %bitcast_convert_fusion.v), channel_id=1, source_target_pairs={{0,504},{8,0},{16,8},{24,16},{32,24},{40,32},{48,40},{56,48},{64,5... | collective-permute-start | bytes 73736 | tf_op jit(solution)/shard_map/ppermute | solution.py:20
  16.3 11.0 %collective-permute-start.2 = (bf16[16,768]{1,0:T(8,128)(2,1)S(1)}, bf16[16,768]{1,0:T(8,128)(2,1)S(1)}, u32[]{:S(2)}, u32[]{:S(2)}) collective-permute-start(bf16[16,768]{1,0:T(8,128)(2,1)S(1)} %bitcast_convert_fusion.v), channel_id=1, source_target_pairs={{0,8},{8,16},{16,24},{24,32},{32,40},{40,48},{48,56},{56,64},{64,7... | collective-permute-start | bytes 73736 | tf_op jit(solution)/shard_map/ppermute | solution.py:20
  18.2 9.1 %collective-permute-start.1 = (bf16[16,768]{1,0:T(8,128)(2,1)S(1)}, bf16[16,768]{1,0:T(8,128)(2,1)S(1)}, u32[]{:S(2)}, u32[]{:S(2)}) collective-permute-start(bf16[16,768]{1,0:T(8,128)(2,1)S(1)} %bitcast_convert_fusion.v), channel_id=1, source_target_pairs={{1,2},{2,1},{3,4},{4,3},{5,6},{6,5},{7,0},{0,7},{9,10},{10,9},{11,... | collective-permute-start | bytes 73736 | tf_op jit(solution)/shard_map/ppermute | solution.py:26
  23.2 4.0 %collective-permute-start = (bf16[16,768]{1,0:T(8,128)(2,1)S(1)}, bf16[16,768]{1,0:T(8,128)(2,1)S(1)}, u32[]{:S(2)}, u32[]{:S(2)}) collective-permute-start(bf16[16,768]{1,0:T(8,128)(2,1)S(1)} %bitcast_convert_fusion.v), channel_id=1, source_target_pairs={{0,1},{1,0},{2,3},{3,2},{4,5},{5,4},{6,7},{7,6},{8,9},{9,8},{10,11... | collective-permute-start | bytes 73736 | tf_op jit(solution)/shard_map/ppermute | solution.py:26
  25.5 0.8 copy-start.5
  26.3 0.7 copy-start.6
  40.9 1.2 copy-start.2
  42.1 36.5 %copy-start.1 = (bf16[1,768,1024]{2,1,0:T(8,128)(2,1)S(1)}, bf16[1,768,1024]{2,1,0:T(8,128)(2,1)}, u32[]{:S(2)}) copy-start(bf16[1,768,1024]{2,1,0:T(8,128)(2,1)} %param.7) | copy-start | bytes 4718596
  42.1 36.5 %copy-start.4 = (f32[1,16,768]{2,1,0:T(8,128)S(1)}, f32[1,16,768]{2,1,0:T(8,128)}, u32[]{:S(2)}) copy-start(f32[1,16,768]{2,1,0:T(8,128)} %param.6) | copy-start | bytes 147460
  60.2 45.5 %copy-start.3 = (bf16[32,64,256]{2,1,0:T(8,128)(2,1)S(1)}, bf16[32,64,256]{2,1,0:T(8,128)(2,1)}, u32[]{:S(2)}) copy-start(bf16[32,64,256]{2,1,0:T(8,128)(2,1)} %inverse.3) | copy-start | bytes 3145732
  60.2 18.5 %collective-permute-start.4 = (bf16[32,768]{1,0:T(8,128)(2,1)S(1)}, bf16[32,768]{1,0:T(8,128)(2,1)S(1)}, u32[]{:S(2)}, u32[]{:S(2)}) collective-permute-start(bf16[32,768]{1,0:T(8,128)(2,1)S(1)} %get-tuple-element.25), channel_id=1, source_target_pairs={{0,1},{1,0},{2,3},{3,2},{4,5},{5,4},{6,7},{7,6},{8,9},{9,8},{10,11... | collective-permute-start | bytes 147464 | tf_op jit(solution)/shard_map/ppermute | solution.py:26
  64.4 14.2 %collective-permute-start.5 = (bf16[32,768]{1,0:T(8,128)(2,1)S(1)}, bf16[32,768]{1,0:T(8,128)(2,1)S(1)}, u32[]{:S(2)}, u32[]{:S(2)}) collective-permute-start(bf16[32,768]{1,0:T(8,128)(2,1)S(1)} %get-tuple-element.26), channel_id=1, source_target_pairs={{1,2},{2,1},{3,4},{4,3},{5,6},{6,5},{7,0},{0,7},{9,10},{10,9},{11,... | collective-permute-start | bytes 147464 | tf_op jit(solution)/shard_map/ppermute | solution.py:26
  66.7 5.3 %collective-permute-start.7 = (bf16[16,768]{1,0:T(8,128)(2,1)S(1)}, bf16[16,768]{1,0:T(8,128)(2,1)S(1)}, u32[]{:S(2)}, u32[]{:S(2)}) collective-permute-start(bf16[16,768]{1,0:T(8,128)(2,1)S(1)} %get-tuple-element.24.refs_0_), channel_id=1, source_target_pairs={{0,504},{8,0},{16,8},{24,16},{32,24},{40,32},{48,40},{56,48},{64,5... | collective-permute-start | bytes 73736 | tf_op jit(solution)/shard_map/ppermute | solution.py:20
  69.8 8.8 %collective-permute-start.6 = (bf16[16,768]{1,0:T(8,128)(2,1)S(1)}, bf16[16,768]{1,0:T(8,128)(2,1)S(1)}, u32[]{:S(2)}, u32[]{:S(2)}) collective-permute-start(bf16[16,768]{1,0:T(8,128)(2,1)S(1)} %get-tuple-element.24.refs_0_), channel_id=1, source_target_pairs={{0,8},{8,16},{16,24},{24,32},{32,40},{40,48},{48,56},{56,64},{64,7... | collective-permute-start | bytes 73736 | tf_op jit(solution)/shard_map/ppermute | solution.py:20
  79.2 5.3 %collective-permute-start.9 = (bf16[16,768]{1,0:T(8,128)(2,1)S(1)}, bf16[16,768]{1,0:T(8,128)(2,1)S(1)}, u32[]{:S(2)}, u32[]{:S(2)}) collective-permute-start(bf16[16,768]{1,0:T(8,128)(2,1)S(1)} %shard_map.81.v), channel_id=1, source_target_pairs={{0,504},{8,0},{16,8},{24,16},{32,24},{40,32},{48,40},{56,48},{64,5... | collective-permute-start | bytes 73736 | tf_op jit(solution)/shard_map/ppermute | solution.py:20
  81.2 8.8 %collective-permute-start.8 = (bf16[16,768]{1,0:T(8,128)(2,1)S(1)}, bf16[16,768]{1,0:T(8,128)(2,1)S(1)}, u32[]{:S(2)}, u32[]{:S(2)}) collective-permute-start(bf16[16,768]{1,0:T(8,128)(2,1)S(1)} %shard_map.81.v), channel_id=1, source_target_pairs={{0,8},{8,16},{16,24},{24,32},{32,40},{40,48},{48,56},{56,64},{64,7... | collective-permute-start | bytes 73736 | tf_op jit(solution)/shard_map/ppermute | solution.py:20
  120.5 11.6 %collective-permute-start.13 = (bf16[16,768]{1,0:T(8,128)(2,1)S(1)}, bf16[16,768]{1,0:T(8,128)(2,1)S(1)}, u32[]{:S(2)}, u32[]{:S(2)}) collective-permute-start(bf16[16,768]{1,0:T(8,128)(2,1)S(1)} %get-tuple-element.30.refs_0_), channel_id=1, source_target_pairs={{0,504},{8,0},{16,8},{24,16},{32,24},{40,32},{48,40},{56,48},{64,5... | collective-permute-start | bytes 73736 | tf_op jit(solution)/shard_map/ppermute | solution.py:20
  124.6 8.8 %collective-permute-start.12 = (bf16[16,768]{1,0:T(8,128)(2,1)S(1)}, bf16[16,768]{1,0:T(8,128)(2,1)S(1)}, u32[]{:S(2)}, u32[]{:S(2)}) collective-permute-start(bf16[16,768]{1,0:T(8,128)(2,1)S(1)} %get-tuple-element.30.refs_0_), channel_id=1, source_target_pairs={{0,8},{8,16},{16,24},{24,32},{32,40},{40,48},{48,56},{56,64},{64,7... | collective-permute-start | bytes 73736 | tf_op jit(solution)/shard_map/ppermute | solution.py:20
  126.5 6.9 %collective-permute-start.11 = (bf16[16,768]{1,0:T(8,128)(2,1)S(1)}, bf16[16,768]{1,0:T(8,128)(2,1)S(1)}, u32[]{:S(2)}, u32[]{:S(2)}) collective-permute-start(bf16[16,768]{1,0:T(8,128)(2,1)S(1)} %get-tuple-element.30.refs_0_), channel_id=1, source_target_pairs={{1,2},{2,1},{3,4},{4,3},{5,6},{6,5},{7,0},{0,7},{9,10},{10,9},{11,... | collective-permute-start | bytes 73736 | tf_op jit(solution)/shard_map/ppermute | solution.py:26
  130.2 3.2 %collective-permute-start.10 = (bf16[16,768]{1,0:T(8,128)(2,1)S(1)}, bf16[16,768]{1,0:T(8,128)(2,1)S(1)}, u32[]{:S(2)}, u32[]{:S(2)}) collective-permute-start(bf16[16,768]{1,0:T(8,128)(2,1)S(1)} %get-tuple-element.30.refs_0_), channel_id=1, source_target_pairs={{0,1},{1,0},{2,3},{3,2},{4,5},{5,4},{6,7},{7,6},{8,9},{9,8},{10,11... | collective-permute-start | bytes 73736 | tf_op jit(solution)/shard_map/ppermute | solution.py:26

commit v5 on v4

--- a/solution.py
+++ b/solution.py
@@ -5,7 +5,7 @@
 from jax.experimental.pallas import tpu as pltpu
 from jax.sharding import PartitionSpec as P
 
-ITERS = 2
+
 LANES = 128
 HALF = 64
 CASES = 16
@@ -26,14 +26,14 @@
     return lax.ppermute(shard, axis, pairs)
 
 
-def call(body, outs, *args):
+def call(body, outs, *args, space=VMEM, scratch=()):
     return pl.pallas_call(
         body,
         out_shape=[jax.ShapeDtypeStruct(shape, dtype) for shape, dtype in outs],
-        in_specs=[pl.BlockSpec(memory_space=VMEM)] * len(args),
+        in_specs=[pl.BlockSpec(memory_space=space)] * len(args),
         out_specs=[pl.BlockSpec(memory_space=VMEM)] * len(outs),
+        scratch_shapes=list(scratch),
         compiler_params=pltpu.CompilerParams(vmem_limit_bytes=16 * 2**20),
-        cost_estimate=pl.CostEstimate(flops=2**24, bytes_accessed=2**19, transcendentals=0),
     )(*args)
 
 
@@ -67,14 +67,25 @@
     return kept.astype(BF16)
 
 
-def prepare_body(rows, basis, picks, held, for_pair, for_other):
+def begin_body(far_load, far_rows, far_basis, far_inverse, field, picks, basis, for_pair, for_other, inverse,
+               load, rows, sems):
+    moves = [
+        pltpu.make_async_copy(source, target, sems.at[i])
+        for i, (source, target) in enumerate(
+            ((far_load, load), (far_rows, rows), (far_basis, basis), (far_inverse, inverse))
+        )
+    ]
+    for move in moves:
+        move.start()
+    moves[1].wait()
     lists = rows[0]
     nb = basis.shape[1]
-    owned = picks.shape[0]
     flat = jnp.concatenate([lists[d : d + 1] for d in range(4)], axis=1)
     spots = lax.broadcasted_iota(jnp.int32, picks.shape, 0)
     picks[...] = jnp.where(spots == flat, 1.0, 0.0).astype(BF16)
-    held[...] = basis[...]
+    moves[0].wait()
+    field[...] = load[...].astype(BF16)
+    moves[2].wait()
     even = even_member()
     edge = basis[:, nb - LANES :].astype(F32)
     edge = jnp.where(even, edge, pltpu.roll(edge, HALF, 1))
@@ -87,6 +98,7 @@
     for out, mine in ((for_pair, side), (for_other, jnp.logical_not(side))):
         kept = jnp.where(mine, parts, 0.0).astype(BF16)
         out[...] = jnp.concatenate([kept[:half], kept[half:]], axis=1)
+    moves[3].wait()
 
 
 def restrict_body(v, pair, other, lower, upper, picks, basis, block, coef):
@@ -108,7 +120,7 @@
     known = jnp.concatenate([value, near], axis=1)
     own = dot_nt(basis[:, : known.shape[1]], tall(known))
     width = 3 * LANES
-    unfold = lambda ref: jnp.concatenate([ref[CASES:, :width], ref[CASES:, width:]], axis=0)
+    unfold = lambda ref: jnp.concatenate([ref[:, :width], ref[:, width:]], axis=0)
     first, second = unfold(pair), unfold(other)
     digits = (first[:1, LANES:] + second[:1, LANES:]).astype(F32)
     spot = (digits[:, :LANES] * DIGIT + digits[:, LANES:]).astype(jnp.int32)
@@ -218,7 +230,10 @@
         passed[...] = total[...]
         out[...] = value
     else:
-        rest[0][...] = value.astype(BF16)
+        out, from_pair, from_other = rest
+        out[...] = value.astype(BF16)
+        from_pair[...] = pair[CASES:]
+        from_other[...] = other[CASES:]
 
 
 def local(load, stiffness, block_inverse, deflation, margin_rows, coarse_inverse):
@@ -232,19 +247,26 @@
     tiles = coarse_inverse.shape[0] * cases // LANES
 
     def group_around(values):
-        return from_behind(values, "group", 1), from_behind(values, "group", -1)
+        lower = from_behind(values, "group", 1)
+        upper = from_behind(values, "group", -1)
+        return lower, upper
 
     def member_around(for_pair, for_other):
-        return exchanged(for_pair, "member", 0), exchanged(for_other, "member", 1)
-
-    field = own_load.astype(BF16)
+        pair = exchanged(for_pair, "member", 0)
+        other = exchanged(for_other, "member", 1)
+        return pair, other
+
+    field, picks, basis, for_pair, for_other, inverse_coarse = call(
+        begin_body,
+        [((cases, owned), BF16), ((owned, nb - owned), BF16), ((kdef, nb), BF16)]
+        + [((kdef // 2, 6 * LANES), BF16)] * 2
+        + [(coarse_inverse.shape, BF16)],
+        *(pltpu.with_memory_space_constraint(a, pltpu.HBM) for a in (own_load, margin_rows, deflation[0], coarse_inverse)),
+        space=pltpu.HBM,
+        scratch=(VMEM((cases, owned), F32), VMEM(margin_rows.shape, jnp.int32), pltpu.SemaphoreType.DMA((4,))),
+    )
     near = member_around(field, field)
     far = group_around(field)
-    picks, basis, for_pair, for_other = call(
-        prepare_body,
-        [((owned, nb - owned), BF16), ((kdef, nb), BF16)] + [((kdef // 2, 6 * LANES), BF16)] * 2,
-        margin_rows, deflation[0],
-    )
     block, coef = call(
         restrict_body,
         [((cases, nb), BF16), ((members, kdef, LANES), BF16)],
@@ -252,7 +274,7 @@
     )
     gathered = lax.all_to_all(coef, "member", 0, 0, tiled=True)
     share_shape = [((groups, tiles, LANES), F32)]
-    (share,) = call(coarse_body, share_shape, gathered, coarse_inverse)
+    (share,) = call(coarse_body, share_shape, gathered, inverse_coarse)
     arrived = lax.all_to_all(share, "group", 0, 0, tiled=True)
     total, rounded, for_pair, for_other = call(
         correct_body,
@@ -260,19 +282,19 @@
         arrived, block, inverse_rows, basis, for_pair, for_other,
     )
     near = member_around(for_pair, for_other)
-    (field,) = call(
+    field, from_pair, from_other = call(
         lambda *refs: residual_body(False, *refs),
-        [((cases, owned), BF16)],
+        [((cases, owned), BF16)] + [((kdef // 2, owned), BF16)] * 2,
         rounded, *near, *group_around(rounded), picks, stiff_rows, own_load,
     )
 
     edge, message = call(
         mixed_body,
         [((cases, LANES), BF16), ((members, kdef, LANES), BF16)],
-        field, *group_around(field), *near, picks, basis,
+        field, *group_around(field), from_pair, from_other, picks, basis,
     )
     message = lax.all_to_all(message, "member", 0, 0, tiled=True)
-    (share,) = call(coarse_mixed_body, share_shape, message, coarse_inverse)
+    (share,) = call(coarse_mixed_body, share_shape, message, inverse_coarse)
     arrived = lax.all_to_all(share, "group", 0, 0, tiled=True)
     total, rounded = call(
         correct_mixed_body,

time: 136 us -> 135 us (level)
  local copies, waits for them, and re-layouts: 2.76 us -> 0.01 us
    unnamed x14 -> x6, local copies, waits for them, and re-layouts: 2.76 us -> 0.01 us
  transfers between devices with their start and end apart: 14 -> 14, of which waited for: 3 -> 4; matrix products, arithmetic and copies ran while one was open for 0% -> 0% of each run, Pallas kernels for 0% -> 0%
where the time goes in v5:
time: 135 us; the launch traced here: 134 us
  blocking collectives  59.5 us (44%)
  starting transfers between devices  52.4 us (39%)
  waiting for transfers between devices  14.2 us (11%)
  Pallas kernels  6.85 us (5%)
    ppermute x8, starting transfers between devices, from_behind(): lax.ppermute(shard, axis, [(i, (i + by) % peers) for i in range(peers)])  33.2 us
    all_to_all x2, blocking collectives, local(): arrived = lax.all_to_all(share, 'group', 0, 0, tiled=True)  30.2 us
    ppermute x6, starting transfers between devices, exchanged(): return lax.ppermute(shard, axis, pairs)  19.2 us
    all_to_all x1, blocking collectives, local(): message = lax.all_to_all(message, 'member', 0, 0, tiled=True)  15.1 us
    all_to_all x1, blocking collectives, local(): gathered = lax.all_to_all(coef, 'member', 0, 0, tiled=True)  14.1 us
    ppermute x8, waiting for transfers between devices, from_behind(): lax.ppermute(shard, axis, [(i, (i + by) % peers) for i in range(peers)])  13.3 us
    pallas_call x9, Pallas kernels, call(): pl.pallas_call(body, out_shape=[jax.ShapeDtypeStruct(shape, dtype) for sh...  6.85 us
  transfers between devices with their start and end apart: 14, of which 4 were waited for; matrix products, arithmetic and copies ran while one was open for 0% of the time, Pallas kernels for 0%

profile of v5, /device:TPU:1, one launch (start us, length us, event | category | flops | bytes accessed | tf_op | source)
XLA Modules:
  0.0 133.8 jit_solution(6787052329858235216)
XLA Ops:
  0.6 0.0 copy-start
  0.6 1.5 %shard_map.77 = (bf16[16,768]{1,0:T(8,128)(2,1)S(1)}, bf16[768,256]{1,0:T(8,128)(2,1)S(1)}, bf16[32,1024]{1,0:T(8,128)(2,1)S(1)}, bf16[16,768]{1,0:T(8,128)(2,1)...) custom-call(f32[16,768]{1,0:T(8,128)} %bitcast.10, s32[1,4,64]{2,1,0:T(4,128)} %far_rows.1, ...), custom_call_target="tpu_custom_call" | custom-call | tf_op jit(solution)/shard_map/pallas_call | solution.py:30
  2.1 14.7 %collective-permute-start.3 = (bf16[16,768]{1,0:T(8,128)(2,1)S(1)}, bf16[16,768]{1,0:T(8,128)(2,1)S(1)}, u32[]{:S(2)}, u32[]{:S(2)}) collective-permute-start(bf16[16,768]{1,0:T(8,128)(2,1)S(1)} %get-tuple-element.23.v), channel_id=1, source_target_pairs={{0,504},{8,0},{16,8},{24,16},{32,24},{40,32},{48,40},{56,48},{64,5... | collective-permute-start | bytes 73736 | tf_op jit(solution)/shard_map/ppermute | solution.py:20
  16.8 1.9 %collective-permute-start.2 = (bf16[16,768]{1,0:T(8,128)(2,1)S(1)}, bf16[16,768]{1,0:T(8,128)(2,1)S(1)}, u32[]{:S(2)}, u32[]{:S(2)}) collective-permute-start(bf16[16,768]{1,0:T(8,128)(2,1)S(1)} %get-tuple-element.23.v), channel_id=1, source_target_pairs={{0,8},{8,16},{16,24},{24,32},{32,40},{40,48},{48,56},{56,64},{64,7... | collective-permute-start | bytes 73736 | tf_op jit(solution)/shard_map/ppermute | solution.py:20
  18.7 5.1 %collective-permute-start.1 = (bf16[16,768]{1,0:T(8,128)(2,1)S(1)}, bf16[16,768]{1,0:T(8,128)(2,1)S(1)}, u32[]{:S(2)}, u32[]{:S(2)}) collective-permute-start(bf16[16,768]{1,0:T(8,128)(2,1)S(1)} %get-tuple-element.23.v), channel_id=1, source_target_pairs={{1,2},{2,1},{3,4},{4,3},{5,6},{6,5},{7,0},{0,7},{9,10},{10,9},{11,... | collective-permute-start | bytes 73736 | tf_op jit(solution)/shard_map/ppermute | solution.py:26
  23.8 2.2 %collective-permute-start = (bf16[16,768]{1,0:T(8,128)(2,1)S(1)}, bf16[16,768]{1,0:T(8,128)(2,1)S(1)}, u32[]{:S(2)}, u32[]{:S(2)}) collective-permute-start(bf16[16,768]{1,0:T(8,128)(2,1)S(1)} %get-tuple-element.23.v), channel_id=1, source_target_pairs={{0,1},{1,0},{2,3},{3,2},{4,5},{5,4},{6,7},{7,6},{8,9},{9,8},{10,11... | collective-permute-start | bytes 73736 | tf_op jit(solution)/shard_map/ppermute | solution.py:26
  26.0 0.0 collective-permute-done.3.upper
  26.0 0.0 collective-permute-done.2.lower
  26.1 0.0 collective-permute-done.1.other
  26.1 0.8 collective-permute-done.pair
  26.9 0.4 shard_map.78
  27.3 14.1 %all_to_all.20.coef = bf16[8,32,128]{2,1,0:T(8,128)(2,1)S(1)} all-to-all(bf16[8,32,128]{2,1,0:T(8,128)(2,1)S(1)} %get-tuple-element.26), channel_id=1, replica_groups=mesh['group'=64,'member'=8] {'member'}, dimensions={0} | all-to-all | bytes 131072 | tf_op jit(solution)/shard_map/all_to_all | solution.py:275
  41.4 0.0 copy-start.1
  41.4 0.0 copy-start.2
  41.4 0.5 shard_map.79
  41.9 16.8 %all_to_all.21.arrived = f32[64,4,128]{2,1,0:T(4,128)S(1)} all-to-all(f32[64,4,128]{2,1,0:T(4,128)S(1)} %shard_map.79), channel_id=1, replica_groups=mesh['group'=64,'member'=8] {'group'}, dimensions={0} | all-to-all | bytes 262144 | tf_op jit(solution)/shard_map/all_to_all | solution.py:278
  58.7 0.0 copy-done
  58.7 0.7 shard_map.80
  59.5 4.1 %collective-permute-start.4 = (bf16[32,768]{1,0:T(8,128)(2,1)S(1)}, bf16[32,768]{1,0:T(8,128)(2,1)S(1)}, u32[]{:S(2)}, u32[]{:S(2)}) collective-permute-start(bf16[32,768]{1,0:T(8,128)(2,1)S(1)} %get-tuple-element.32), channel_id=1, source_target_pairs={{0,1},{1,0},{2,3},{3,2},{4,5},{5,4},{6,7},{7,6},{8,9},{9,8},{10,11... | collective-permute-start | bytes 147464 | tf_op jit(solution)/shard_map/ppermute | solution.py:26
  63.6 2.3 %collective-permute-start.5 = (bf16[32,768]{1,0:T(8,128)(2,1)S(1)}, bf16[32,768]{1,0:T(8,128)(2,1)S(1)}, u32[]{:S(2)}, u32[]{:S(2)}) collective-permute-start(bf16[32,768]{1,0:T(8,128)(2,1)S(1)} %get-tuple-element.33), channel_id=1, source_target_pairs={{1,2},{2,1},{3,4},{4,3},{5,6},{6,5},{7,0},{0,7},{9,10},{10,9},{11,... | collective-permute-start | bytes 147464 | tf_op jit(solution)/shard_map/ppermute | solution.py:26
  65.9 3.1 %collective-permute-start.7 = (bf16[16,768]{1,0:T(8,128)(2,1)S(1)}, bf16[16,768]{1,0:T(8,128)(2,1)S(1)}, u32[]{:S(2)}, u32[]{:S(2)}) collective-permute-start(bf16[16,768]{1,0:T(8,128)(2,1)S(1)} %get-tuple-element.31.refs_0_), channel_id=1, source_target_pairs={{0,504},{8,0},{16,8},{24,16},{32,24},{40,32},{48,40},{56,48},{64,5... | collective-permute-start | bytes 73736 | tf_op jit(solution)/shard_map/ppermute | solution.py:20
  69.0 2.1 %collective-permute-start.6 = (bf16[16,768]{1,0:T(8,128)(2,1)S(1)}, bf16[16,768]{1,0:T(8,128)(2,1)S(1)}, u32[]{:S(2)}, u32[]{:S(2)}) collective-permute-start(bf16[16,768]{1,0:T(8,128)(2,1)S(1)} %get-tuple-element.31.refs_0_), channel_id=1, source_target_pairs={{0,8},{8,16},{16,24},{24,32},{32,40},{40,48},{48,56},{56,64},{64,7... | collective-permute-start | bytes 73736 | tf_op jit(solution)/shard_map/ppermute | solution.py:20
  71.2 0.0 collective-permute-done.7.refs_4_
  71.2 6.6 %collective-permute-done.6.refs_3_ = bf16[16,768]{1,0:T(8,128)(2,1)S(1)} collective-permute-done((bf16[16,768]{1,0:T(8,128)(2,1)S(1)}, bf16[16,768]{1,0:T(8,128)(2,1)S(1)}, u32[]{:S(2)}, u32[]{:S(2)}) %collective-permute-start.6) | collective-permute-done | bytes 24608 | tf_op jit(solution)/shard_map/ppermute | solution.py:20
  77.8 0.0 collective-permute-done.4.refs_1_
  77.8 0.0 collective-permute-done.5.refs_2_
  77.8 0.0 copy-done.1
  77.8 0.0 copy-done.2
  77.8 0.6 shard_map.81
  78.4 1.9 %collective-permute-start.9 = (bf16[16,768]{1,0:T(8,128)(2,1)S(1)}, bf16[16,768]{1,0:T(8,128)(2,1)S(1)}, u32[]{:S(2)}, u32[]{:S(2)}) collective-permute-start(bf16[16,768]{1,0:T(8,128)(2,1)S(1)} %get-tuple-element.34.v), channel_id=1, source_target_pairs={{0,504},{8,0},{16,8},{24,16},{32,24},{40,32},{48,40},{56,48},{64,5... | collective-permute-start | bytes 73736 | tf_op jit(solution)/shard_map/ppermute | solution.py:20
  80.4 3.4 %collective-permute-start.8 = (bf16[16,768]{1,0:T(8,128)(2,1)S(1)}, bf16[16,768]{1,0:T(8,128)(2,1)S(1)}, u32[]{:S(2)}, u32[]{:S(2)}) collective-permute-start(bf16[16,768]{1,0:T(8,128)(2,1)S(1)} %get-tuple-element.34.v), channel_id=1, source_target_pairs={{0,8},{8,16},{16,24},{24,32},{32,40},{40,48},{48,56},{56,64},{64,7... | collective-permute-start | bytes 73736 | tf_op jit(solution)/shard_map/ppermute | solution.py:20
  83.8 0.0 collective-permute-done.9.upper
  83.8 5.4 %collective-permute-done.8.lower = bf16[16,768]{1,0:T(8,128)(2,1)S(1)} collective-permute-done((bf16[16,768]{1,0:T(8,128)(2,1)S(1)}, bf16[16,768]{1,0:T(8,128)(2,1)S(1)}, u32[]{:S(2)}, u32[]{:S(2)}) %collective-permute-start.8) | collective-permute-done | bytes 24608 | tf_op jit(solution)/shard_map/ppermute | solution.py:20
  89.2 0.5 shard_map.82
  89.7 15.1 %all_to_all.22.message = bf16[8,32,128]{2,1,0:T(8,128)(2,1)S(1)} all-to-all(bf16[8,32,128]{2,1,0:T(8,128)(2,1)S(1)} %get-tuple-element.37), channel_id=1, replica_groups=mesh['group'=64,'member'=8] {'member'}, dimensions={0} | all-to-all | bytes 131072 | tf_op jit(solution)/shard_map/all_to_all | solution.py:296
  104.8 0.7 shard_map.83
  105.5 13.4 %all_to_all.23.arrived = f32[64,4,128]{2,1,0:T(4,128)S(1)} all-to-all(f32[64,4,128]{2,1,0:T(4,128)S(1)} %shard_map.83), channel_id=1, replica_groups=mesh['group'=64,'member'=8] {'group'}, dimensions={0} | all-to-all | bytes 262144 | tf_op jit(solution)/shard_map/all_to_all | solution.py:298
  118.9 0.7 shard_map.84
  119.7 4.1 %collective-permute-start.13 = (bf16[16,768]{1,0:T(8,128)(2,1)S(1)}, bf16[16,768]{1,0:T(8,128)(2,1)S(1)}, u32[]{:S(2)}, u32[]{:S(2)}) collective-permute-start(bf16[16,768]{1,0:T(8,128)(2,1)S(1)} %get-tuple-element.40.refs_0_), channel_id=1, source_target_pairs={{0,504},{8,0},{16,8},{24,16},{32,24},{40,32},{48,40},{56,48},{64,5... | collective-permute-start | bytes 73736 | tf_op jit(solution)/shard_map/ppermute | solution.py:20
  123.8 1.9 %collective-permute-start.12 = (bf16[16,768]{1,0:T(8,128)(2,1)S(1)}, bf16[16,768]{1,0:T(8,128)(2,1)S(1)}, u32[]{:S(2)}, u32[]{:S(2)}) collective-permute-start(bf16[16,768]{1,0:T(8,128)(2,1)S(1)} %get-tuple-element.40.refs_0_), channel_id=1, source_target_pairs={{0,8},{8,16},{16,24},{24,32},{32,40},{40,48},{48,56},{56,64},{64,7... | collective-permute-start | bytes 73736 | tf_op jit(solution)/shard_map/ppermute | solution.py:20
  125.7 3.6 %collective-permute-start.11 = (bf16[16,768]{1,0:T(8,128)(2,1)S(1)}, bf16[16,768]{1,0:T(8,128)(2,1)S(1)}, u32[]{:S(2)}, u32[]{:S(2)}) collective-permute-start(bf16[16,768]{1,0:T(8,128)(2,1)S(1)} %get-tuple-element.40.refs_0_), channel_id=1, source_target_pairs={{1,2},{2,1},{3,4},{4,3},{5,6},{6,5},{7,0},{0,7},{9,10},{10,9},{11,... | collective-permute-start | bytes 73736 | tf_op jit(solution)/shard_map/ppermute | solution.py:26
  129.4 1.9 %collective-permute-start.10 = (bf16[16,768]{1,0:T(8,128)(2,1)S(1)}, bf16[16,768]{1,0:T(8,128)(2,1)S(1)}, u32[]{:S(2)}, u32[]{:S(2)}) collective-permute-start(bf16[16,768]{1,0:T(8,128)(2,1)S(1)} %get-tuple-element.40.refs_0_), channel_id=1, source_target_pairs={{0,1},{1,0},{2,3},{3,2},{4,5},{5,4},{6,7},{7,6},{8,9},{9,8},{10,11... | collective-permute-start | bytes 73736 | tf_op jit(solution)/shard_map/ppermute | solution.py:26
  131.3 0.0 collective-permute-done.13.refs_4_
  131.3 1.3 collective-permute-done.12.refs_3_
  132.6 0.0 collective-permute-done.11.refs_2_
  132.6 0.0 collective-permute-done.10.refs_1_
  132.6 1.3 shard_map.85
Async XLA Ops:
  0.6 58.1 %copy-start = (bf16[1,768,1024]{2,1,0:T(8,128)(2,1)S(1)}, bf16[1,768,1024]{2,1,0:T(8,128)(2,1)}, u32[]{:S(2)}) copy-start(bf16[1,768,1024]{2,1,0:T(8,128)(2,1)} %param.8) | copy-start | bytes 4718596
  2.1 23.9 %collective-permute-start.3 = (bf16[16,768]{1,0:T(8,128)(2,1)S(1)}, bf16[16,768]{1,0:T(8,128)(2,1)S(1)}, u32[]{:S(2)}, u32[]{:S(2)}) collective-permute-start(bf16[16,768]{1,0:T(8,128)(2,1)S(1)} %get-tuple-element.23.v), channel_id=1, source_target_pairs={{0,504},{8,0},{16,8},{24,16},{32,24},{40,32},{48,40},{56,48},{64,5... | collective-permute-start | bytes 73736 | tf_op jit(solution)/shard_map/ppermute | solution.py:20
  16.8 9.2 %collective-permute-start.2 = (bf16[16,768]{1,0:T(8,128)(2,1)S(1)}, bf16[16,768]{1,0:T(8,128)(2,1)S(1)}, u32[]{:S(2)}, u32[]{:S(2)}) collective-permute-start(bf16[16,768]{1,0:T(8,128)(2,1)S(1)} %get-tuple-element.23.v), channel_id=1, source_target_pairs={{0,8},{8,16},{16,24},{24,32},{32,40},{40,48},{48,56},{56,64},{64,7... | collective-permute-start | bytes 73736 | tf_op jit(solution)/shard_map/ppermute | solution.py:20
  18.7 7.3 %collective-permute-start.1 = (bf16[16,768]{1,0:T(8,128)(2,1)S(1)}, bf16[16,768]{1,0:T(8,128)(2,1)S(1)}, u32[]{:S(2)}, u32[]{:S(2)}) collective-permute-start(bf16[16,768]{1,0:T(8,128)(2,1)S(1)} %get-tuple-element.23.v), channel_id=1, source_target_pairs={{1,2},{2,1},{3,4},{4,3},{5,6},{6,5},{7,0},{0,7},{9,10},{10,9},{11,... | collective-permute-start | bytes 73736 | tf_op jit(solution)/shard_map/ppermute | solution.py:26
  23.8 3.1 %collective-permute-start = (bf16[16,768]{1,0:T(8,128)(2,1)S(1)}, bf16[16,768]{1,0:T(8,128)(2,1)S(1)}, u32[]{:S(2)}, u32[]{:S(2)}) collective-permute-start(bf16[16,768]{1,0:T(8,128)(2,1)S(1)} %get-tuple-element.23.v), channel_id=1, source_target_pairs={{0,1},{1,0},{2,3},{3,2},{4,5},{5,4},{6,7},{7,6},{8,9},{9,8},{10,11... | collective-permute-start | bytes 73736 | tf_op jit(solution)/shard_map/ppermute | solution.py:26
  41.4 36.4 %copy-start.1 = (bf16[1,768,1024]{2,1,0:T(8,128)(2,1)S(1)}, bf16[1,768,1024]{2,1,0:T(8,128)(2,1)}, u32[]{:S(2)}) copy-start(bf16[1,768,1024]{2,1,0:T(8,128)(2,1)} %param.7) | copy-start | bytes 4718596
  41.4 36.4 %copy-start.2 = (f32[1,16,768]{2,1,0:T(8,128)S(1)}, f32[1,16,768]{2,1,0:T(8,128)}, u32[]{:S(2)}) copy-start(f32[1,16,768]{2,1,0:T(8,128)} %param.6) | copy-start | bytes 147460
  59.5 18.3 %collective-permute-start.4 = (bf16[32,768]{1,0:T(8,128)(2,1)S(1)}, bf16[32,768]{1,0:T(8,128)(2,1)S(1)}, u32[]{:S(2)}, u32[]{:S(2)}) collective-permute-start(bf16[32,768]{1,0:T(8,128)(2,1)S(1)} %get-tuple-element.32), channel_id=1, source_target_pairs={{0,1},{1,0},{2,3},{3,2},{4,5},{5,4},{6,7},{7,6},{8,9},{9,8},{10,11... | collective-permute-start | bytes 147464 | tf_op jit(solution)/shard_map/ppermute | solution.py:26
  63.6 14.2 %collective-permute-start.5 = (bf16[32,768]{1,0:T(8,128)(2,1)S(1)}, bf16[32,768]{1,0:T(8,128)(2,1)S(1)}, u32[]{:S(2)}, u32[]{:S(2)}) collective-permute-start(bf16[32,768]{1,0:T(8,128)(2,1)S(1)} %get-tuple-element.33), channel_id=1, source_target_pairs={{1,2},{2,1},{3,4},{4,3},{5,6},{6,5},{7,0},{0,7},{9,10},{10,9},{11,... | collective-permute-start | bytes 147464 | tf_op jit(solution)/shard_map/ppermute | solution.py:26
  65.9 5.3 %collective-permute-start.7 = (bf16[16,768]{1,0:T(8,128)(2,1)S(1)}, bf16[16,768]{1,0:T(8,128)(2,1)S(1)}, u32[]{:S(2)}, u32[]{:S(2)}) collective-permute-start(bf16[16,768]{1,0:T(8,128)(2,1)S(1)} %get-tuple-element.31.refs_0_), channel_id=1, source_target_pairs={{0,504},{8,0},{16,8},{24,16},{32,24},{40,32},{48,40},{56,48},{64,5... | collective-permute-start | bytes 73736 | tf_op jit(solution)/shard_map/ppermute | solution.py:20
  69.0 8.8 %collective-permute-start.6 = (bf16[16,768]{1,0:T(8,128)(2,1)S(1)}, bf16[16,768]{1,0:T(8,128)(2,1)S(1)}, u32[]{:S(2)}, u32[]{:S(2)}) collective-permute-start(bf16[16,768]{1,0:T(8,128)(2,1)S(1)} %get-tuple-element.31.refs_0_), channel_id=1, source_target_pairs={{0,8},{8,16},{16,24},{24,32},{32,40},{40,48},{48,56},{56,64},{64,7... | collective-permute-start | bytes 73736 | tf_op jit(solution)/shard_map/ppermute | solution.py:20
  78.4 5.3 %collective-permute-start.9 = (bf16[16,768]{1,0:T(8,128)(2,1)S(1)}, bf16[16,768]{1,0:T(8,128)(2,1)S(1)}, u32[]{:S(2)}, u32[]{:S(2)}) collective-permute-start(bf16[16,768]{1,0:T(8,128)(2,1)S(1)} %get-tuple-element.34.v), channel_id=1, source_target_pairs={{0,504},{8,0},{16,8},{24,16},{32,24},{40,32},{48,40},{56,48},{64,5... | collective-permute-start | bytes 73736 | tf_op jit(solution)/shard_map/ppermute | solution.py:20
  80.4 8.8 %collective-permute-start.8 = (bf16[16,768]{1,0:T(8,128)(2,1)S(1)}, bf16[16,768]{1,0:T(8,128)(2,1)S(1)}, u32[]{:S(2)}, u32[]{:S(2)}) collective-permute-start(bf16[16,768]{1,0:T(8,128)(2,1)S(1)} %get-tuple-element.34.v), channel_id=1, source_target_pairs={{0,8},{8,16},{16,24},{24,32},{32,40},{40,48},{48,56},{56,64},{64,7... | collective-permute-start | bytes 73736 | tf_op jit(solution)/shard_map/ppermute | solution.py:20
  119.7 11.6 %collective-permute-start.13 = (bf16[16,768]{1,0:T(8,128)(2,1)S(1)}, bf16[16,768]{1,0:T(8,128)(2,1)S(1)}, u32[]{:S(2)}, u32[]{:S(2)}) collective-permute-start(bf16[16,768]{1,0:T(8,128)(2,1)S(1)} %get-tuple-element.40.refs_0_), channel_id=1, source_target_pairs={{0,504},{8,0},{16,8},{24,16},{32,24},{40,32},{48,40},{56,48},{64,5... | collective-permute-start | bytes 73736 | tf_op jit(solution)/shard_map/ppermute | solution.py:20
  123.8 8.8 %collective-permute-start.12 = (bf16[16,768]{1,0:T(8,128)(2,1)S(1)}, bf16[16,768]{1,0:T(8,128)(2,1)S(1)}, u32[]{:S(2)}, u32[]{:S(2)}) collective-permute-start(bf16[16,768]{1,0:T(8,128)(2,1)S(1)} %get-tuple-element.40.refs_0_), channel_id=1, source_target_pairs={{0,8},{8,16},{16,24},{24,32},{32,40},{40,48},{48,56},{56,64},{64,7... | collective-permute-start | bytes 73736 | tf_op jit(solution)/shard_map/ppermute | solution.py:20
  125.7 6.9 %collective-permute-start.11 = (bf16[16,768]{1,0:T(8,128)(2,1)S(1)}, bf16[16,768]{1,0:T(8,128)(2,1)S(1)}, u32[]{:S(2)}, u32[]{:S(2)}) collective-permute-start(bf16[16,768]{1,0:T(8,128)(2,1)S(1)} %get-tuple-element.40.refs_0_), channel_id=1, source_target_pairs={{1,2},{2,1},{3,4},{4,3},{5,6},{6,5},{7,0},{0,7},{9,10},{10,9},{11,... | collective-permute-start | bytes 73736 | tf_op jit(solution)/shard_map/ppermute | solution.py:26
  129.4 3.2 %collective-permute-start.10 = (bf16[16,768]{1,0:T(8,128)(2,1)S(1)}, bf16[16,768]{1,0:T(8,128)(2,1)S(1)}, u32[]{:S(2)}, u32[]{:S(2)}) collective-permute-start(bf16[16,768]{1,0:T(8,128)(2,1)S(1)} %get-tuple-element.40.refs_0_), channel_id=1, source_target_pairs={{0,1},{1,0},{2,3},{3,2},{4,5},{5,4},{6,7},{7,6},{8,9},{9,8},{10,11... | collective-permute-start | bytes 73736 | tf_op jit(solution)/shard_map/ppermute | solution.py:26

commit v6 on v5

--- a/solution.py
+++ b/solution.py
@@ -13,11 +13,6 @@
 F32 = jnp.float32
 BF16 = jnp.bfloat16
 VMEM = pltpu.VMEM
-
-
-def from_behind(shard, axis, by):
-    peers = lax.axis_size(axis)
-    return lax.ppermute(shard, axis, [(i, (i + by) % peers) for i in range(peers)])
 
 
 def exchanged(shard, axis, first):
@@ -45,8 +40,8 @@
     return jnp.dot(left, right, preferred_element_type=F32)
 
 
-def even_member():
-    return lax.rem(lax.axis_index("member"), 2) == 0
+def even(axis):
+    return lax.rem(lax.axis_index(axis), 2) == 0
 
 
 def tall(rows):
@@ -57,10 +52,12 @@
     return lax.broadcasted_iota(jnp.int32, shape, 1)
 
 
-def margins(lower, upper, pair, other, picks):
-    every = dot_nn(jnp.concatenate([lower, upper, pair, other], axis=0), picks)
+def margins(near, next_, pair, other, picks):
+    every = dot_nn(jnp.concatenate([near, next_, pair, other], axis=0), picks)
     source = lanes((CASES, picks.shape[1])) // HALF
-    owner = jnp.where((source >= 2) & even_member(), 5 - source, source)
+    by_group = jnp.where(even("group"), 1 - source, source)
+    by_member = jnp.where(even("member"), 5 - source, source)
+    owner = jnp.where(source < 2, by_group, by_member)
     kept = every[:CASES]
     for d in range(1, 4):
         kept = jnp.where(owner == d, every[d * CASES : (d + 1) * CASES], kept)
@@ -86,10 +83,10 @@
     moves[0].wait()
     field[...] = load[...].astype(BF16)
     moves[2].wait()
-    even = even_member()
+    upward = even("member")
     edge = basis[:, nb - LANES :].astype(F32)
-    edge = jnp.where(even, edge, pltpu.roll(edge, HALF, 1))
-    turn = jnp.where(even, flat[:, LANES:], jnp.concatenate([lists[3:4], lists[2:3]], axis=1))
+    edge = jnp.where(upward, edge, pltpu.roll(edge, HALF, 1))
+    turn = jnp.where(upward, flat[:, LANES:], jnp.concatenate([lists[3:4], lists[2:3]], axis=1))
     high = jnp.broadcast_to((turn // DIGIT).astype(F32), edge.shape)
     low = jnp.broadcast_to((turn % DIGIT).astype(F32), edge.shape)
     parts = jnp.concatenate([edge, high, low], axis=1)
@@ -101,8 +98,8 @@
     moves[3].wait()
 
 
-def restrict_body(v, pair, other, lower, upper, picks, basis, block, coef):
-    edge = margins(lower[...], upper[...], pair[...], other[...], picks[...])
+def restrict_body(v, pair, other, near, next_, picks, basis, block, coef):
+    edge = margins(near[...], next_[...], pair[...], other[...], picks[...])
     whole = jnp.concatenate([v[...], edge], axis=1)
     block[...] = whole
     part = dot_nt(basis[...], tall(whole)).astype(BF16)
@@ -110,14 +107,16 @@
         coef[m] = part
 
 
-def mixed_body(v, lower, upper, pair, other, picks, basis, edge, message):
+def mixed_body(v, near, next_, pair, other, picks, basis, edge, message):
     value = v[...]
-    rows = jnp.concatenate([lower[...], upper[...]], axis=0)
+    rows = jnp.concatenate([near[...], next_[...]], axis=0)
     every = dot_nn(rows, picks[:, :LANES])
     lane = lanes((CASES, LANES))
-    near = jnp.where(lane < HALF, every[:CASES], every[CASES:]).astype(BF16)
-    edge[...] = near
-    known = jnp.concatenate([value, near], axis=1)
+    swapped = jnp.where(lane < HALF, every[CASES:], every[:CASES])
+    straight = jnp.where(lane < HALF, every[:CASES], every[CASES:])
+    beside = jnp.where(even("group"), swapped, straight).astype(BF16)
+    edge[...] = beside
+    known = jnp.concatenate([value, beside], axis=1)
     own = dot_nt(basis[:, : known.shape[1]], tall(known))
     width = 3 * LANES
     unfold = lambda ref: jnp.concatenate([ref[:, :width], ref[:, width:]], axis=0)
@@ -205,13 +204,13 @@
 def correct_mixed_body(arrived, v, edge, message, inverse, basis, before, total, rounded):
     me = lax.axis_index("member")
     peers = message.shape[0]
-    even = even_member()
-    pair = jnp.where(even, me + 1, me - 1)
-    other = lax.rem(jnp.where(even, me + peers - 1, me + 1), peers)
+    upward = even("member")
+    pair = jnp.where(upward, me + 1, me - 1)
+    other = lax.rem(jnp.where(upward, me + peers - 1, me + 1), peers)
     from_pair = message[pair, :CASES].astype(F32)
     from_other = message[other, CASES:].astype(F32)
-    high = jnp.where(even, from_pair, from_other)
-    low = jnp.where(even, from_other, from_pair)
+    high = jnp.where(upward, from_pair, from_other)
+    low = jnp.where(upward, from_other, from_pair)
     far = jnp.where(lanes(high.shape) < HALF, pltpu.roll(low, HALF, 1), high).astype(BF16)
     block = jnp.concatenate([v[...], edge[...], far], axis=1)
     value = dot_nt(block, inverse[...])
@@ -221,8 +220,8 @@
     rounded[...] = value.astype(BF16)
 
 
-def residual_body(last, v, pair, other, lower, upper, picks, stiff, load, *rest):
-    edge = margins(lower[...], upper[...], pair[:CASES], other[:CASES], picks[...])
+def residual_body(last, v, pair, other, near, next_, picks, stiff, load, *rest):
+    edge = margins(near[...], next_[...], pair[:CASES], other[:CASES], picks[...])
     whole = jnp.concatenate([v[...], edge], axis=1)
     value = load[...] - dot_nt(whole, stiff[...])
     if last:
@@ -247,9 +246,9 @@
     tiles = coarse_inverse.shape[0] * cases // LANES
 
     def group_around(values):
-        lower = from_behind(values, "group", 1)
-        upper = from_behind(values, "group", -1)
-        return lower, upper
+        near = exchanged(values, "group", 0)
+        next_ = exchanged(values, "group", 1)
+        return near, next_
 
     def member_around(for_pair, for_other):
         pair = exchanged(for_pair, "member", 0)

time: 135 us -> 128 us (0.948)
  waiting for transfers between devices: 14.2 us -> 8.63 us
  blocking collectives: 59.5 us -> 57.1 us
  starting transfers between devices: 52.4 us -> 53.8 us
    ppermute x6 -> x14, starting transfers between devices: 19.2 us -> 53.8 us  [exchanged(): return lax.ppermute(shard, axis, pairs)]
    ppermute x8 -> x0, starting transfers between devices: 33.2 us -> none  [from_behind(): lax.ppermute(shard, axis, [(i, (i + by) % peers) for i in range(peers)])]
    ppermute x8 -> x0, waiting for transfers between devices: 13.3 us -> none  [from_behind(): lax.ppermute(shard, axis, [(i, (i + by) % peers) for i in range(peers)])]
    ppermute x6 -> x14, waiting for transfers between devices: 0.83 us -> 8.63 us  [exchanged(): return lax.ppermute(shard, axis, pairs)]
    all_to_all x2, blocking collectives: 30.2 us -> 28.4 us  [local(): arrived = lax.all_to_all(share, 'group', 0, 0, tiled=True)]
  transfers between devices with their start and end apart: 14 -> 14, of which waited for: 4 -> 6; matrix products, arithmetic and copies ran while one was open for 0% -> 0% of each run, Pallas kernels for 0% -> 0%
where the time goes in v6:
time: 128 us; the launch traced here: 127 us
  blocking collectives  57.1 us (45%)
  starting transfers between devices  53.8 us (42%)
  waiting for transfers between devices  8.63 us (7%)
  Pallas kernels  6.84 us (5%)
    ppermute x14, starting transfers between devices, exchanged(): return lax.ppermute(shard, axis, pairs)  53.8 us
    all_to_all x2, blocking collectives, local(): arrived = lax.all_to_all(share, 'group', 0, 0, tiled=True)  28.4 us
    all_to_all x1, blocking collectives, local(): message = lax.all_to_all(message, 'member', 0, 0, tiled=True)  15.1 us
    all_to_all x1, blocking collectives, local(): gathered = lax.all_to_all(coef, 'member', 0, 0, tiled=True)  13.5 us
    ppermute x14, waiting for transfers between devices, exchanged(): return lax.ppermute(shard, axis, pairs)  8.63 us
    pallas_call x9, Pallas kernels, call(): pl.pallas_call(body, out_shape=[jax.ShapeDtypeStruct(shape, dtype) for sh...  6.84 us
  transfers between devices with their start and end apart: 14, of which 6 were waited for; matrix products, arithmetic and copies ran while one was open for 0% of the time, Pallas kernels for 0%

profile of v6, /device:TPU:1, one launch (start us, length us, event | category | flops | bytes accessed | tf_op | source)
XLA Modules:
  0.0 127.2 jit_solution(1375619147840270218)
XLA Ops:
  0.6 0.0 copy-start
  0.6 1.5 %shard_map.77 = (bf16[16,768]{1,0:T(8,128)(2,1)S(1)}, bf16[768,256]{1,0:T(8,128)(2,1)S(1)}, bf16[32,1024]{1,0:T(8,128)(2,1)S(1)}, bf16[16,768]{1,0:T(8,128)(2,1)...) custom-call(f32[16,768]{1,0:T(8,128)} %bitcast.10, s32[1,4,64]{2,1,0:T(4,128)} %far_rows.1, ...), custom_call_target="tpu_custom_call" | custom-call | tf_op jit(solution)/shard_map/pallas_call | solution.py:25
  2.1 14.7 %collective-permute-start.3 = (bf16[16,768]{1,0:T(8,128)(2,1)S(1)}, bf16[16,768]{1,0:T(8,128)(2,1)S(1)}, u32[]{:S(2)}, u32[]{:S(2)}) collective-permute-start(bf16[16,768]{1,0:T(8,128)(2,1)S(1)} %get-tuple-element.23.v), channel_id=1, source_target_pairs={{8,16},{16,8},{24,32},{32,24},{40,48},{48,40},{56,64},{64,56},{72,... | collective-permute-start | bytes 73736 | tf_op jit(solution)/shard_map/ppermute | solution.py:21
  16.8 1.9 %collective-permute-start.2 = (bf16[16,768]{1,0:T(8,128)(2,1)S(1)}, bf16[16,768]{1,0:T(8,128)(2,1)S(1)}, u32[]{:S(2)}, u32[]{:S(2)}) collective-permute-start(bf16[16,768]{1,0:T(8,128)(2,1)S(1)} %get-tuple-element.23.v), channel_id=1, source_target_pairs={{0,8},{8,0},{16,24},{24,16},{32,40},{40,32},{48,56},{56,48},{64,72... | collective-permute-start | bytes 73736 | tf_op jit(solution)/shard_map/ppermute | solution.py:21
  18.7 5.1 %collective-permute-start.1 = (bf16[16,768]{1,0:T(8,128)(2,1)S(1)}, bf16[16,768]{1,0:T(8,128)(2,1)S(1)}, u32[]{:S(2)}, u32[]{:S(2)}) collective-permute-start(bf16[16,768]{1,0:T(8,128)(2,1)S(1)} %get-tuple-element.23.v), channel_id=1, source_target_pairs={{1,2},{2,1},{3,4},{4,3},{5,6},{6,5},{7,0},{0,7},{9,10},{10,9},{11,... | collective-permute-start | bytes 73736 | tf_op jit(solution)/shard_map/ppermute | solution.py:21
  23.8 2.2 %collective-permute-start = (bf16[16,768]{1,0:T(8,128)(2,1)S(1)}, bf16[16,768]{1,0:T(8,128)(2,1)S(1)}, u32[]{:S(2)}, u32[]{:S(2)}) collective-permute-start(bf16[16,768]{1,0:T(8,128)(2,1)S(1)} %get-tuple-element.23.v), channel_id=1, source_target_pairs={{0,1},{1,0},{2,3},{3,2},{4,5},{5,4},{6,7},{7,6},{8,9},{9,8},{10,11... | collective-permute-start | bytes 73736 | tf_op jit(solution)/shard_map/ppermute | solution.py:21
  26.0 0.0 collective-permute-done.3.next_
  26.0 0.0 collective-permute-done.2.near
  26.1 0.0 collective-permute-done.1.other
  26.1 0.8 collective-permute-done.pair
  26.9 0.4 shard_map.78
  27.3 13.5 %all_to_all.20.coef = bf16[8,32,128]{2,1,0:T(8,128)(2,1)S(1)} all-to-all(bf16[8,32,128]{2,1,0:T(8,128)(2,1)S(1)} %get-tuple-element.26), channel_id=1, replica_groups=mesh['group'=64,'member'=8] {'member'}, dimensions={0} | all-to-all | bytes 131072 | tf_op jit(solution)/shard_map/all_to_all | solution.py:274
  40.8 0.0 copy-start.1
  40.8 0.0 copy-start.2
  40.8 0.5 shard_map.79
  41.3 14.7 %all_to_all.21.arrived = f32[64,4,128]{2,1,0:T(4,128)S(1)} all-to-all(f32[64,4,128]{2,1,0:T(4,128)S(1)} %shard_map.79), channel_id=1, replica_groups=mesh['group'=64,'member'=8] {'group'}, dimensions={0} | all-to-all | bytes 262144 | tf_op jit(solution)/shard_map/all_to_all | solution.py:277
  56.0 0.0 copy-done
  56.0 0.7 shard_map.80
  56.7 4.2 %collective-permute-start.4 = (bf16[32,768]{1,0:T(8,128)(2,1)S(1)}, bf16[32,768]{1,0:T(8,128)(2,1)S(1)}, u32[]{:S(2)}, u32[]{:S(2)}) collective-permute-start(bf16[32,768]{1,0:T(8,128)(2,1)S(1)} %get-tuple-element.32), channel_id=1, source_target_pairs={{0,1},{1,0},{2,3},{3,2},{4,5},{5,4},{6,7},{7,6},{8,9},{9,8},{10,11... | collective-permute-start | bytes 147464 | tf_op jit(solution)/shard_map/ppermute | solution.py:21
  60.9 2.0 %collective-permute-start.5 = (bf16[32,768]{1,0:T(8,128)(2,1)S(1)}, bf16[32,768]{1,0:T(8,128)(2,1)S(1)}, u32[]{:S(2)}, u32[]{:S(2)}) collective-permute-start(bf16[32,768]{1,0:T(8,128)(2,1)S(1)} %get-tuple-element.33), channel_id=1, source_target_pairs={{1,2},{2,1},{3,4},{4,3},{5,6},{6,5},{7,0},{0,7},{9,10},{10,9},{11,... | collective-permute-start | bytes 147464 | tf_op jit(solution)/shard_map/ppermute | solution.py:21
  62.9 3.1 %collective-permute-start.7 = (bf16[16,768]{1,0:T(8,128)(2,1)S(1)}, bf16[16,768]{1,0:T(8,128)(2,1)S(1)}, u32[]{:S(2)}, u32[]{:S(2)}) collective-permute-start(bf16[16,768]{1,0:T(8,128)(2,1)S(1)} %get-tuple-element.31.refs_0_), channel_id=1, source_target_pairs={{8,16},{16,8},{24,32},{32,24},{40,48},{48,40},{56,64},{64,56},{72,... | collective-permute-start | bytes 73736 | tf_op jit(solution)/shard_map/ppermute | solution.py:21
  66.1 1.9 %collective-permute-start.6 = (bf16[16,768]{1,0:T(8,128)(2,1)S(1)}, bf16[16,768]{1,0:T(8,128)(2,1)S(1)}, u32[]{:S(2)}, u32[]{:S(2)}) collective-permute-start(bf16[16,768]{1,0:T(8,128)(2,1)S(1)} %get-tuple-element.31.refs_0_), channel_id=1, source_target_pairs={{0,8},{8,0},{16,24},{24,16},{32,40},{40,32},{48,56},{56,48},{64,72... | collective-permute-start | bytes 73736 | tf_op jit(solution)/shard_map/ppermute | solution.py:21
  68.0 3.7 %collective-permute-done.7.refs_4_ = bf16[16,768]{1,0:T(8,128)(2,1)S(1)} collective-permute-done((bf16[16,768]{1,0:T(8,128)(2,1)S(1)}, bf16[16,768]{1,0:T(8,128)(2,1)S(1)}, u32[]{:S(2)}, u32[]{:S(2)}) %collective-permute-start.7) | collective-permute-done | bytes 24608 | tf_op jit(solution)/shard_map/ppermute | solution.py:21
  71.7 0.0 collective-permute-done.6.refs_3_
  71.7 0.0 collective-permute-done.4.refs_1_
  71.7 0.0 collective-permute-done.5.refs_2_
  71.7 0.0 copy-done.1
  71.7 0.0 copy-done.2
  71.7 0.6 shard_map.81
  72.4 5.3 %collective-permute-start.9 = (bf16[16,768]{1,0:T(8,128)(2,1)S(1)}, bf16[16,768]{1,0:T(8,128)(2,1)S(1)}, u32[]{:S(2)}, u32[]{:S(2)}) collective-permute-start(bf16[16,768]{1,0:T(8,128)(2,1)S(1)} %get-tuple-element.34.v), channel_id=1, source_target_pairs={{8,16},{16,8},{24,32},{32,24},{40,48},{48,40},{56,64},{64,56},{72,... | collective-permute-start | bytes 73736 | tf_op jit(solution)/shard_map/ppermute | solution.py:21
  77.7 1.9 %collective-permute-start.8 = (bf16[16,768]{1,0:T(8,128)(2,1)S(1)}, bf16[16,768]{1,0:T(8,128)(2,1)S(1)}, u32[]{:S(2)}, u32[]{:S(2)}) collective-permute-start(bf16[16,768]{1,0:T(8,128)(2,1)S(1)} %get-tuple-element.34.v), channel_id=1, source_target_pairs={{0,8},{8,0},{16,24},{24,16},{32,40},{40,32},{48,56},{56,48},{64,72... | collective-permute-start | bytes 73736 | tf_op jit(solution)/shard_map/ppermute | solution.py:21
  79.6 1.6 %collective-permute-done.9.next_ = bf16[16,768]{1,0:T(8,128)(2,1)S(1)} collective-permute-done((bf16[16,768]{1,0:T(8,128)(2,1)S(1)}, bf16[16,768]{1,0:T(8,128)(2,1)S(1)}, u32[]{:S(2)}, u32[]{:S(2)}) %collective-permute-start.9) | collective-permute-done | bytes 24608 | tf_op jit(solution)/shard_map/ppermute | solution.py:21
  81.2 1.4 %collective-permute-done.8.near = bf16[16,768]{1,0:T(8,128)(2,1)S(1)} collective-permute-done((bf16[16,768]{1,0:T(8,128)(2,1)S(1)}, bf16[16,768]{1,0:T(8,128)(2,1)S(1)}, u32[]{:S(2)}, u32[]{:S(2)}) %collective-permute-start.8) | collective-permute-done | bytes 24608 | tf_op jit(solution)/shard_map/ppermute | solution.py:21
  82.5 0.5 shard_map.82
  83.1 15.1 %all_to_all.22.message = bf16[8,32,128]{2,1,0:T(8,128)(2,1)S(1)} all-to-all(bf16[8,32,128]{2,1,0:T(8,128)(2,1)S(1)} %get-tuple-element.37), channel_id=1, replica_groups=mesh['group'=64,'member'=8] {'member'}, dimensions={0} | all-to-all | bytes 131072 | tf_op jit(solution)/shard_map/all_to_all | solution.py:295
  98.2 0.7 shard_map.83
  98.9 13.7 %all_to_all.23.arrived = f32[64,4,128]{2,1,0:T(4,128)S(1)} all-to-all(f32[64,4,128]{2,1,0:T(4,128)S(1)} %shard_map.83), channel_id=1, replica_groups=mesh['group'=64,'member'=8] {'group'}, dimensions={0} | all-to-all | bytes 262144 | tf_op jit(solution)/shard_map/all_to_all | solution.py:297
  112.6 0.7 shard_map.84
  113.3 3.4 %collective-permute-start.13 = (bf16[16,768]{1,0:T(8,128)(2,1)S(1)}, bf16[16,768]{1,0:T(8,128)(2,1)S(1)}, u32[]{:S(2)}, u32[]{:S(2)}) collective-permute-start(bf16[16,768]{1,0:T(8,128)(2,1)S(1)} %get-tuple-element.40.refs_0_), channel_id=1, source_target_pairs={{8,16},{16,8},{24,32},{32,24},{40,48},{48,40},{56,64},{64,56},{72,... | collective-permute-start | bytes 73736 | tf_op jit(solution)/shard_map/ppermute | solution.py:21
  116.8 1.9 %collective-permute-start.12 = (bf16[16,768]{1,0:T(8,128)(2,1)S(1)}, bf16[16,768]{1,0:T(8,128)(2,1)S(1)}, u32[]{:S(2)}, u32[]{:S(2)}) collective-permute-start(bf16[16,768]{1,0:T(8,128)(2,1)S(1)} %get-tuple-element.40.refs_0_), channel_id=1, source_target_pairs={{0,8},{8,0},{16,24},{24,16},{32,40},{40,32},{48,56},{56,48},{64,72... | collective-permute-start | bytes 73736 | tf_op jit(solution)/shard_map/ppermute | solution.py:21
  118.7 4.1 %collective-permute-start.11 = (bf16[16,768]{1,0:T(8,128)(2,1)S(1)}, bf16[16,768]{1,0:T(8,128)(2,1)S(1)}, u32[]{:S(2)}, u32[]{:S(2)}) collective-permute-start(bf16[16,768]{1,0:T(8,128)(2,1)S(1)} %get-tuple-element.40.refs_0_), channel_id=1, source_target_pairs={{1,2},{2,1},{3,4},{4,3},{5,6},{6,5},{7,0},{0,7},{9,10},{10,9},{11,... | collective-permute-start | bytes 73736 | tf_op jit(solution)/shard_map/ppermute | solution.py:21
  122.9 1.9 %collective-permute-start.10 = (bf16[16,768]{1,0:T(8,128)(2,1)S(1)}, bf16[16,768]{1,0:T(8,128)(2,1)S(1)}, u32[]{:S(2)}, u32[]{:S(2)}) collective-permute-start(bf16[16,768]{1,0:T(8,128)(2,1)S(1)} %get-tuple-element.40.refs_0_), channel_id=1, source_target_pairs={{0,1},{1,0},{2,3},{3,2},{4,5},{5,4},{6,7},{7,6},{8,9},{9,8},{10,11... | collective-permute-start | bytes 73736 | tf_op jit(solution)/shard_map/ppermute | solution.py:21
  124.8 0.0 collective-permute-done.13.refs_4_
  124.8 0.0 collective-permute-done.12.refs_3_
  124.8 0.3 collective-permute-done.11.refs_2_
  125.1 0.9 collective-permute-done.10.refs_1_
  125.9 1.3 shard_map.85
Async XLA Ops:
  0.6 55.4 %copy-start = (bf16[1,768,1024]{2,1,0:T(8,128)(2,1)S(1)}, bf16[1,768,1024]{2,1,0:T(8,128)(2,1)}, u32[]{:S(2)}) copy-start(bf16[1,768,1024]{2,1,0:T(8,128)(2,1)} %param.8) | copy-start | bytes 4718596
  2.1 23.9 %collective-permute-start.3 = (bf16[16,768]{1,0:T(8,128)(2,1)S(1)}, bf16[16,768]{1,0:T(8,128)(2,1)S(1)}, u32[]{:S(2)}, u32[]{:S(2)}) collective-permute-start(bf16[16,768]{1,0:T(8,128)(2,1)S(1)} %get-tuple-element.23.v), channel_id=1, source_target_pairs={{8,16},{16,8},{24,32},{32,24},{40,48},{48,40},{56,64},{64,56},{72,... | collective-permute-start | bytes 73736 | tf_op jit(solution)/shard_map/ppermute | solution.py:21
  16.8 9.2 %collective-permute-start.2 = (bf16[16,768]{1,0:T(8,128)(2,1)S(1)}, bf16[16,768]{1,0:T(8,128)(2,1)S(1)}, u32[]{:S(2)}, u32[]{:S(2)}) collective-permute-start(bf16[16,768]{1,0:T(8,128)(2,1)S(1)} %get-tuple-element.23.v), channel_id=1, source_target_pairs={{0,8},{8,0},{16,24},{24,16},{32,40},{40,32},{48,56},{56,48},{64,72... | collective-permute-start | bytes 73736 | tf_op jit(solution)/shard_map/ppermute | solution.py:21
  18.7 7.3 %collective-permute-start.1 = (bf16[16,768]{1,0:T(8,128)(2,1)S(1)}, bf16[16,768]{1,0:T(8,128)(2,1)S(1)}, u32[]{:S(2)}, u32[]{:S(2)}) collective-permute-start(bf16[16,768]{1,0:T(8,128)(2,1)S(1)} %get-tuple-element.23.v), channel_id=1, source_target_pairs={{1,2},{2,1},{3,4},{4,3},{5,6},{6,5},{7,0},{0,7},{9,10},{10,9},{11,... | collective-permute-start | bytes 73736 | tf_op jit(solution)/shard_map/ppermute | solution.py:21
  23.8 3.1 %collective-permute-start = (bf16[16,768]{1,0:T(8,128)(2,1)S(1)}, bf16[16,768]{1,0:T(8,128)(2,1)S(1)}, u32[]{:S(2)}, u32[]{:S(2)}) collective-permute-start(bf16[16,768]{1,0:T(8,128)(2,1)S(1)} %get-tuple-element.23.v), channel_id=1, source_target_pairs={{0,1},{1,0},{2,3},{3,2},{4,5},{5,4},{6,7},{7,6},{8,9},{9,8},{10,11... | collective-permute-start | bytes 73736 | tf_op jit(solution)/shard_map/ppermute | solution.py:21
  40.8 31.0 %copy-start.1 = (bf16[1,768,1024]{2,1,0:T(8,128)(2,1)S(1)}, bf16[1,768,1024]{2,1,0:T(8,128)(2,1)}, u32[]{:S(2)}) copy-start(bf16[1,768,1024]{2,1,0:T(8,128)(2,1)} %param.7) | copy-start | bytes 4718596
  40.8 31.0 %copy-start.2 = (f32[1,16,768]{2,1,0:T(8,128)S(1)}, f32[1,16,768]{2,1,0:T(8,128)}, u32[]{:S(2)}) copy-start(f32[1,16,768]{2,1,0:T(8,128)} %param.6) | copy-start | bytes 147460
  56.7 15.0 %collective-permute-start.4 = (bf16[32,768]{1,0:T(8,128)(2,1)S(1)}, bf16[32,768]{1,0:T(8,128)(2,1)S(1)}, u32[]{:S(2)}, u32[]{:S(2)}) collective-permute-start(bf16[32,768]{1,0:T(8,128)(2,1)S(1)} %get-tuple-element.32), channel_id=1, source_target_pairs={{0,1},{1,0},{2,3},{3,2},{4,5},{5,4},{6,7},{7,6},{8,9},{9,8},{10,11... | collective-permute-start | bytes 147464 | tf_op jit(solution)/shard_map/ppermute | solution.py:21
  60.9 10.8 %collective-permute-start.5 = (bf16[32,768]{1,0:T(8,128)(2,1)S(1)}, bf16[32,768]{1,0:T(8,128)(2,1)S(1)}, u32[]{:S(2)}, u32[]{:S(2)}) collective-permute-start(bf16[32,768]{1,0:T(8,128)(2,1)S(1)} %get-tuple-element.33), channel_id=1, source_target_pairs={{1,2},{2,1},{3,4},{4,3},{5,6},{6,5},{7,0},{0,7},{9,10},{10,9},{11,... | collective-permute-start | bytes 147464 | tf_op jit(solution)/shard_map/ppermute | solution.py:21
  62.9 8.8 %collective-permute-start.7 = (bf16[16,768]{1,0:T(8,128)(2,1)S(1)}, bf16[16,768]{1,0:T(8,128)(2,1)S(1)}, u32[]{:S(2)}, u32[]{:S(2)}) collective-permute-start(bf16[16,768]{1,0:T(8,128)(2,1)S(1)} %get-tuple-element.31.refs_0_), channel_id=1, source_target_pairs={{8,16},{16,8},{24,32},{32,24},{40,48},{48,40},{56,64},{64,56},{72,... | collective-permute-start | bytes 73736 | tf_op jit(solution)/shard_map/ppermute | solution.py:21
  66.1 5.6 %collective-permute-start.6 = (bf16[16,768]{1,0:T(8,128)(2,1)S(1)}, bf16[16,768]{1,0:T(8,128)(2,1)S(1)}, u32[]{:S(2)}, u32[]{:S(2)}) collective-permute-start(bf16[16,768]{1,0:T(8,128)(2,1)S(1)} %get-tuple-element.31.refs_0_), channel_id=1, source_target_pairs={{0,8},{8,0},{16,24},{24,16},{32,40},{40,32},{48,56},{56,48},{64,72... | collective-permute-start | bytes 73736 | tf_op jit(solution)/shard_map/ppermute | solution.py:21
  72.4 8.8 %collective-permute-start.9 = (bf16[16,768]{1,0:T(8,128)(2,1)S(1)}, bf16[16,768]{1,0:T(8,128)(2,1)S(1)}, u32[]{:S(2)}, u32[]{:S(2)}) collective-permute-start(bf16[16,768]{1,0:T(8,128)(2,1)S(1)} %get-tuple-element.34.v), channel_id=1, source_target_pairs={{8,16},{16,8},{24,32},{32,24},{40,48},{48,40},{56,64},{64,56},{72,... | collective-permute-start | bytes 73736 | tf_op jit(solution)/shard_map/ppermute | solution.py:21
  77.7 4.9 %collective-permute-start.8 = (bf16[16,768]{1,0:T(8,128)(2,1)S(1)}, bf16[16,768]{1,0:T(8,128)(2,1)S(1)}, u32[]{:S(2)}, u32[]{:S(2)}) collective-permute-start(bf16[16,768]{1,0:T(8,128)(2,1)S(1)} %get-tuple-element.34.v), channel_id=1, source_target_pairs={{0,8},{8,0},{16,24},{24,16},{32,40},{40,32},{48,56},{56,48},{64,72... | collective-permute-start | bytes 73736 | tf_op jit(solution)/shard_map/ppermute | solution.py:21
  113.3 11.5 %collective-permute-start.13 = (bf16[16,768]{1,0:T(8,128)(2,1)S(1)}, bf16[16,768]{1,0:T(8,128)(2,1)S(1)}, u32[]{:S(2)}, u32[]{:S(2)}) collective-permute-start(bf16[16,768]{1,0:T(8,128)(2,1)S(1)} %get-tuple-element.40.refs_0_), channel_id=1, source_target_pairs={{8,16},{16,8},{24,32},{32,24},{40,48},{48,40},{56,64},{64,56},{72,... | collective-permute-start | bytes 73736 | tf_op jit(solution)/shard_map/ppermute | solution.py:21
  116.8 8.0 %collective-permute-start.12 = (bf16[16,768]{1,0:T(8,128)(2,1)S(1)}, bf16[16,768]{1,0:T(8,128)(2,1)S(1)}, u32[]{:S(2)}, u32[]{:S(2)}) collective-permute-start(bf16[16,768]{1,0:T(8,128)(2,1)S(1)} %get-tuple-element.40.refs_0_), channel_id=1, source_target_pairs={{0,8},{8,0},{16,24},{24,16},{32,40},{40,32},{48,56},{56,48},{64,72... | collective-permute-start | bytes 73736 | tf_op jit(solution)/shard_map/ppermute | solution.py:21
  118.7 6.4 %collective-permute-start.11 = (bf16[16,768]{1,0:T(8,128)(2,1)S(1)}, bf16[16,768]{1,0:T(8,128)(2,1)S(1)}, u32[]{:S(2)}, u32[]{:S(2)}) collective-permute-start(bf16[16,768]{1,0:T(8,128)(2,1)S(1)} %get-tuple-element.40.refs_0_), channel_id=1, source_target_pairs={{1,2},{2,1},{3,4},{4,3},{5,6},{6,5},{7,0},{0,7},{9,10},{10,9},{11,... | collective-permute-start | bytes 73736 | tf_op jit(solution)/shard_map/ppermute | solution.py:21
  122.9 3.1 %collective-permute-start.10 = (bf16[16,768]{1,0:T(8,128)(2,1)S(1)}, bf16[16,768]{1,0:T(8,128)(2,1)S(1)}, u32[]{:S(2)}, u32[]{:S(2)}) collective-permute-start(bf16[16,768]{1,0:T(8,128)(2,1)S(1)} %get-tuple-element.40.refs_0_), channel_id=1, source_target_pairs={{0,1},{1,0},{2,3},{3,2},{4,5},{5,4},{6,7},{7,6},{8,9},{9,8},{10,11... | collective-permute-start | bytes 73736 | tf_op jit(solution)/shard_map/ppermute | solution.py:21

commit v7 on v6

--- a/solution.py
+++ b/solution.py
@@ -64,7 +64,27 @@
     return kept.astype(BF16)
 
 
-def begin_body(far_load, far_rows, far_basis, far_inverse, field, picks, basis, for_pair, for_other, inverse,
+def two_margins(near, next_, picks, axis):
+    every = dot_nn(jnp.concatenate([near, next_], axis=0), picks)
+    lane = lanes((CASES, LANES))
+    swapped = jnp.where(lane < HALF, every[CASES:], every[:CASES])
+    straight = jnp.where(lane < HALF, every[:CASES], every[CASES:])
+    return jnp.where(even(axis), swapped, straight).astype(BF16)
+
+
+def one_hot(digits, rows):
+    spot = (digits[:, :LANES] * DIGIT + digits[:, LANES:]).astype(jnp.int32)
+    choice = lax.broadcasted_iota(jnp.int32, (rows, LANES), 0) == spot
+    return jnp.where(choice, 1.0, 0.0).astype(BF16)
+
+
+def partners(axis, peers):
+    me = lax.axis_index(axis)
+    upward = even(axis)
+    return jnp.where(upward, me + 1, me - 1), lax.rem(jnp.where(upward, me + peers - 1, me + 1), peers)
+
+
+def begin_body(far_load, far_rows, far_basis, far_inverse, field, picks, basis, for_pair, for_other, for_group, inverse,
                load, rows, sems):
     moves = [
         pltpu.make_async_copy(source, target, sems.at[i])
@@ -87,6 +107,12 @@
     edge = basis[:, nb - LANES :].astype(F32)
     edge = jnp.where(upward, edge, pltpu.roll(edge, HALF, 1))
     turn = jnp.where(upward, flat[:, LANES:], jnp.concatenate([lists[3:4], lists[2:3]], axis=1))
+    around = jnp.where(even("group"), flat[:, :LANES], jnp.concatenate([lists[1:2], lists[0:1]], axis=1))
+    tens = (around // DIGIT).astype(F32)
+    ones = (around % DIGIT).astype(F32)
+    pad = jnp.zeros((1, for_group.shape[1] - 2 * LANES), F32)
+    digits = jnp.concatenate([tens, ones, pad], axis=1)
+    for_group[...] = jnp.broadcast_to(digits, for_group.shape).astype(BF16)
     high = jnp.broadcast_to((turn // DIGIT).astype(F32), edge.shape)
     low = jnp.broadcast_to((turn % DIGIT).astype(F32), edge.shape)
     parts = jnp.concatenate([edge, high, low], axis=1)
@@ -108,13 +134,8 @@
 
 
 def mixed_body(v, near, next_, pair, other, picks, basis, edge, message):
-    value = v[...]
-    rows = jnp.concatenate([near[...], next_[...]], axis=0)
-    every = dot_nn(rows, picks[:, :LANES])
-    lane = lanes((CASES, LANES))
-    swapped = jnp.where(lane < HALF, every[CASES:], every[:CASES])
-    straight = jnp.where(lane < HALF, every[:CASES], every[CASES:])
-    beside = jnp.where(even("group"), swapped, straight).astype(BF16)
+    value = v[:CASES]
+    beside = two_margins(near[:CASES], next_[:CASES], picks[:, :LANES], "group")
     edge[...] = beside
     known = jnp.concatenate([value, beside], axis=1)
     own = dot_nt(basis[:, : known.shape[1]], tall(known))
@@ -122,9 +143,7 @@
     unfold = lambda ref: jnp.concatenate([ref[:, :width], ref[:, width:]], axis=0)
     first, second = unfold(pair), unfold(other)
     digits = (first[:1, LANES:] + second[:1, LANES:]).astype(F32)
-    spot = (digits[:, :LANES] * DIGIT + digits[:, LANES:]).astype(jnp.int32)
-    choice = lax.broadcasted_iota(jnp.int32, (value.shape[1], LANES), 0) == spot
-    chosen = dot_nn(value, jnp.where(choice, 1.0, 0.0).astype(BF16))
+    chosen = dot_nn(value, one_hot(digits, value.shape[1]))
     spread = tall(chosen.astype(BF16))
     to_first = dot_nt(first[:, :LANES], spread)
     to_second = dot_nt(second[:, :LANES], spread)
@@ -157,7 +176,7 @@
     shares_of(coef[...].reshape(-1, LANES), inverse, share)
 
 
-def coarse_mixed_body(message, inverse, share):
+def coarse_mixed_body(message, inverse, v, edge, inverse_rows, before, choice, out, total, share):
     peers, kdef, _ = message.shape
     source = lax.broadcasted_iota(jnp.int32, (LANES, 3 * LANES), 0)
     target = lanes((LANES, 3 * LANES))
@@ -172,6 +191,34 @@
         at = lambda k, j: parts[k * kdef : (k + 1) * kdef, j * LANES : (j + 1) * LANES]
         every.append(at(m, 0) + at(pair, 1) + at(other, 2))
     shares_of(jnp.concatenate(every, axis=0).astype(BF16), inverse, share)
+    pair, other = partners("member", peers)
+    from_pair = message[pair, :CASES].astype(F32)
+    from_other = message[other, CASES:].astype(F32)
+    upward = even("member")
+    high = jnp.where(upward, from_pair, from_other)
+    low = jnp.where(upward, from_other, from_pair)
+    left = lanes(high.shape) < HALF
+    far = jnp.where(left, pltpu.roll(low, HALF, 1), high).astype(BF16)
+    block = jnp.concatenate([v[:CASES], edge[...], far], axis=1)
+    value = before[...] + dot_nt(block, inverse_rows[...])
+    total[...] = value
+    short = share[...].astype(BF16)
+    groups = short.shape[0]
+    out[:, 0] = short
+    out[1:, 1] = short[:-1]
+    out[:1, 1] = short[-1:]
+    out[:-1, 2] = short[1:]
+    out[-1:, 2] = short[:1]
+    out[:, 3:] = jnp.zeros((groups, 2) + short.shape[1:], BF16)
+    chosen = dot_nn(value.astype(BF16), choice[...])
+    top, low = chosen[: CASES // 2], pltpu.roll(chosen, HALF, 1)[CASES // 2 :]
+    side = lanes(top.shape) < HALF
+    near, next_ = partners("group", groups)
+    rows = short.shape[1]
+    for target, kept in ((near, jnp.where(side, low, top)), (next_, jnp.where(side, top, low))):
+        kept = kept.astype(BF16)
+        out[target, 3] = kept[:rows]
+        out[target, 4] = kept[rows:]
 
 
 def prolong_of(arrived, kdef):
@@ -189,50 +236,60 @@
     return out.astype(BF16)
 
 
-def correct_body(arrived, block, inverse, basis, for_pair, for_other, total, rounded, pair, other):
+def correct_body(arrived, block, inverse, basis, for_pair, for_other, for_group, total, rounded, pair, other, group):
     value = dot_nt(block[...], inverse[...])
     prolong = prolong_of(arrived[...], basis.shape[0])
     value = value + dot_nn(prolong, basis[:, : total.shape[1]])
     total[...] = value
     short = value.astype(BF16)
     rounded[...] = short
-    for out, more in ((pair, for_pair), (other, for_other)):
+    for out, more in ((pair, for_pair), (other, for_other), (group, for_group)):
         out[:CASES] = short
         out[CASES:] = more[...]
 
 
-def correct_mixed_body(arrived, v, edge, message, inverse, basis, before, total, rounded):
-    me = lax.axis_index("member")
-    peers = message.shape[0]
-    upward = even("member")
-    pair = jnp.where(upward, me + 1, me - 1)
-    other = lax.rem(jnp.where(upward, me + peers - 1, me + 1), peers)
-    from_pair = message[pair, :CASES].astype(F32)
-    from_other = message[other, CASES:].astype(F32)
-    high = jnp.where(upward, from_pair, from_other)
-    low = jnp.where(upward, from_other, from_pair)
-    far = jnp.where(lanes(high.shape) < HALF, pltpu.roll(low, HALF, 1), high).astype(BF16)
-    block = jnp.concatenate([v[...], edge[...], far], axis=1)
-    value = dot_nt(block, inverse[...])
-    prolong = prolong_of(arrived[...], basis.shape[0])
-    value = before[...] + (value + dot_nn(prolong, basis[:, : total.shape[1]]))
+def correct_mixed_body(arrived, before, near, next_, basis, total, rounded, edge):
+    kdef = basis.shape[0]
+    upward = even("group")
+    first, second = partners("group", arrived.shape[0])
+    take = lambda k: jnp.concatenate([arrived[k, 3], arrived[k, 4]], axis=0).astype(F32)
+    widen = lambda part: jnp.concatenate([part, pltpu.roll(part, HALF, 1)], axis=0)
+    left = lanes((CASES, LANES)) < HALF
+    known = jnp.where(left, widen(take(second)), widen(take(first)))
+    known = jnp.where(upward, known, pltpu.roll(known, HALF, 1))
+    unfold = lambda ref: jnp.concatenate([ref[CASES:, :LANES], ref[CASES:, LANES : 2 * LANES]], axis=0)
+    vectors = jnp.where(lanes((kdef, LANES)) < HALF, unfold(next_).astype(F32), unfold(near).astype(F32))
+    vectors = jnp.where(upward, vectors, pltpu.roll(vectors, HALF, 1)).astype(BF16)
+    prolong = [prolong_of(arrived[:, k].astype(F32), kdef) for k in range(3)]
+    added = jnp.where(left, dot_nn(prolong[1], vectors), dot_nn(prolong[2], vectors))
+    edge[...] = (known + added).astype(BF16)
+    value = before[...] + dot_nn(prolong[0], basis[:, : total.shape[1]])
     total[...] = value
     rounded[...] = value.astype(BF16)
 
 
-def residual_body(last, v, pair, other, near, next_, picks, stiff, load, *rest):
-    edge = margins(near[...], next_[...], pair[:CASES], other[:CASES], picks[...])
+def residual_body(v, pair, other, near, next_, picks, basis, stiff, load, group, from_pair, from_other, choice):
+    edge = margins(near[:CASES], next_[:CASES], pair[:CASES], other[:CASES], picks[...])
     whole = jnp.concatenate([v[...], edge], axis=1)
     value = load[...] - dot_nt(whole, stiff[...])
-    if last:
-        total, out, passed = rest
-        passed[...] = total[...]
-        out[...] = value
-    else:
-        out, from_pair, from_other = rest
-        out[...] = value.astype(BF16)
-        from_pair[...] = pair[CASES:]
-        from_other[...] = other[CASES:]
+    from_pair[...] = pair[CASES:]
+    from_other[...] = other[CASES:]
+    owned = value.shape[1]
+    left = lanes((1, 2 * LANES)) % LANES < HALF
+    told = lambda ref: ref[CASES : CASES + 1, : 2 * LANES].astype(F32)
+    chosen = one_hot(jnp.where(left, told(next_), told(near)), owned)
+    choice[...] = chosen
+    vectors = dot_nn(basis[:, :owned], chosen).astype(BF16)
+    pad = jnp.zeros((CASES, owned - 2 * LANES), BF16)
+    group[:CASES] = value.astype(BF16)
+    group[CASES:] = jnp.concatenate([vectors[:CASES], vectors[CASES:], pad], axis=1)
+
+
+def finish_body(v, pair, other, edge, picks, stiff, load, total, out, passed):
+    far = two_margins(pair[...], other[...], picks[:, LANES:], "member")
+    whole = jnp.concatenate([v[...], edge[...], far], axis=1)
+    passed[...] = total[...]
+    out[...] = load[...] - dot_nt(whole, stiff[...])
 
 
 def local(load, stiffness, block_inverse, deflation, margin_rows, coarse_inverse):
@@ -255,10 +312,10 @@
         other = exchanged(for_other, "member", 1)
         return pair, other
 
-    field, picks, basis, for_pair, for_other, inverse_coarse = call(
+    field, picks, basis, for_pair, for_other, for_group, inverse_coarse = call(
         begin_body,
         [((cases, owned), BF16), ((owned, nb - owned), BF16), ((kdef, nb), BF16)]
-        + [((kdef // 2, 6 * LANES), BF16)] * 2
+        + [((kdef // 2, owned), BF16)] * 3
         + [(coarse_inverse.shape, BF16)],
         *(pltpu.with_memory_space_constraint(a, pltpu.HBM) for a in (own_load, margin_rows, deflation[0], coarse_inverse)),
         space=pltpu.HBM,
@@ -275,35 +332,41 @@
     share_shape = [((groups, tiles, LANES), F32)]
     (share,) = call(coarse_body, share_shape, gathered, inverse_coarse)
     arrived = lax.all_to_all(share, "group", 0, 0, tiled=True)
-    total, rounded, for_pair, for_other = call(
+    total, rounded, for_pair, for_other, for_group = call(
         correct_body,
-        [((cases, owned), F32), ((cases, owned), BF16)] + [((cases + kdef // 2, owned), BF16)] * 2,
-        arrived, block, inverse_rows, basis, for_pair, for_other,
+        [((cases, owned), F32), ((cases, owned), BF16)] + [((cases + kdef // 2, owned), BF16)] * 3,
+        arrived, block, inverse_rows, basis, for_pair, for_other, for_group,
     )
     near = member_around(for_pair, for_other)
-    field, from_pair, from_other = call(
-        lambda *refs: residual_body(False, *refs),
-        [((cases, owned), BF16)] + [((kdef // 2, owned), BF16)] * 2,
-        rounded, *near, *group_around(rounded), picks, stiff_rows, own_load,
-    )
-
+    field, from_pair, from_other, choice = call(
+        residual_body,
+        [((cases + kdef // 2, owned), BF16)] + [((kdef // 2, owned), BF16)] * 2 + [((owned, LANES), BF16)],
+        rounded, *near, *group_around(for_group), picks, basis, stiff_rows, own_load,
+    )
+
+    far = group_around(field)
     edge, message = call(
         mixed_body,
         [((cases, LANES), BF16), ((members, kdef, LANES), BF16)],
-        field, *group_around(field), from_pair, from_other, picks, basis,
+        field, *far, from_pair, from_other, picks, basis,
     )
     message = lax.all_to_all(message, "member", 0, 0, tiled=True)
-    (share,) = call(coarse_mixed_body, share_shape, message, inverse_coarse)
+    share, total = call(
+        coarse_mixed_body,
+        [((groups, 5, tiles, LANES), BF16), ((cases, owned), F32)],
+        message, inverse_coarse, field, edge, inverse_rows, total, choice,
+        scratch=(VMEM((groups, tiles, LANES), F32),),
+    )
     arrived = lax.all_to_all(share, "group", 0, 0, tiled=True)
-    total, rounded = call(
+    total, rounded, edge = call(
         correct_mixed_body,
-        [((cases, owned), F32), ((cases, owned), BF16)],
-        arrived, field, edge, message, inverse_rows, basis, total,
+        [((cases, owned), F32), ((cases, owned), BF16), ((cases, LANES), BF16)],
+        arrived, total, *far, basis,
     )
     residual, solution_out = call(
-        lambda *refs: residual_body(True, *refs),
+        finish_body,
         [((cases, owned), F32)] * 2,
-        rounded, *member_around(rounded, rounded), *group_around(rounded), picks, stiff_rows, own_load, total,
+        rounded, *member_around(rounded, rounded), edge, picks, stiff_rows, own_load, total,
     )
     return (solution_out[None], residual[None])
 

time: 128 us -> 127 us (level)
  starting transfers between devices: 53.8 us -> 48.7 us
  blocking collectives: 57.1 us -> 60.3 us
    ppermute x14 -> x12, starting transfers between devices: 53.8 us -> 48.7 us  [exchanged(): return lax.ppermute(shard, axis, pairs)]
    all_to_all x2, blocking collectives: 28.4 us -> 31.7 us  [local(): arrived = lax.all_to_all(share, 'group', 0, 0, tiled=True)]
    ppermute x14 -> x12, waiting for transfers between devices: 8.63 us -> 9.14 us  [exchanged(): return lax.ppermute(shard, axis, pairs)]
  transfers between devices with their start and end apart: 14 -> 12, of which waited for: 6 -> 5; matrix products, arithmetic and copies ran while one was open for 0% -> 0% of each run, Pallas kernels for 0% -> 0%
where the time goes in v7:
time: 127 us; the launch traced here: 126 us
  blocking collectives  60.3 us (47%)
  starting transfers between devices  48.7 us (38%)
  waiting for transfers between devices  9.14 us (7%)
  Pallas kernels  7.26 us (6%)
    ppermute x12, starting transfers between devices, exchanged(): return lax.ppermute(shard, axis, pairs)  48.7 us
    all_to_all x2, blocking collectives, local(): arrived = lax.all_to_all(share, 'group', 0, 0, tiled=True)  31.7 us
    all_to_all x1, blocking collectives, local(): message = lax.all_to_all(message, 'member', 0, 0, tiled=True)  15.1 us
    all_to_all x1, blocking collectives, local(): gathered = lax.all_to_all(coef, 'member', 0, 0, tiled=True)  13.5 us
    ppermute x12, waiting for transfers between devices, exchanged(): return lax.ppermute(shard, axis, pairs)  9.14 us
    pallas_call x9, Pallas kernels, call(): pl.pallas_call(body, out_shape=[jax.ShapeDtypeStruct(shape, dtype) for sh...  7.26 us
  transfers between devices with their start and end apart: 12, of which 5 were waited for; matrix products, arithmetic and copies ran while one was open for 0% of the time, Pallas kernels for 0%

profile of v7, /device:TPU:1, one launch (start us, length us, event | category | flops | bytes accessed | tf_op | source)
XLA Modules:
  0.0 126.3 jit_solution(3619932757615974802)
XLA Ops:
  0.6 0.0 copy-start
  0.6 1.5 %shard_map.77 = (bf16[16,768]{1,0:T(8,128)(2,1)S(1)}, bf16[768,256]{1,0:T(8,128)(2,1)S(1)}, bf16[32,1024]{1,0:T(8,128)(2,1)S(1)}, bf16[16,768]{1,0:T(8,128)(2,1)...) custom-call(f32[16,768]{1,0:T(8,128)} %bitcast.10, ...), custom_call_target="tpu_custom_call" | custom-call | tf_op jit(solution)/shard_map/pallas_call | solution.py:25
  2.1 14.7 %collective-permute-start.3 = (bf16[16,768]{1,0:T(8,128)(2,1)S(1)}, bf16[16,768]{1,0:T(8,128)(2,1)S(1)}, u32[]{:S(2)}, u32[]{:S(2)}) collective-permute-start(bf16[16,768]{1,0:T(8,128)(2,1)S(1)} %get-tuple-element.29.v), channel_id=1, source_target_pairs={{8,16},{16,8},{24,32},{32,24},{40,48},{48,40},{56,64},{64,56},{72,... | collective-permute-start | bytes 73736 | tf_op jit(solution)/shard_map/ppermute | solution.py:21
  16.8 1.9 %collective-permute-start.2 = (bf16[16,768]{1,0:T(8,128)(2,1)S(1)}, bf16[16,768]{1,0:T(8,128)(2,1)S(1)}, u32[]{:S(2)}, u32[]{:S(2)}) collective-permute-start(bf16[16,768]{1,0:T(8,128)(2,1)S(1)} %get-tuple-element.29.v), channel_id=1, source_target_pairs={{0,8},{8,0},{16,24},{24,16},{32,40},{40,32},{48,56},{56,48},{64,72... | collective-permute-start | bytes 73736 | tf_op jit(solution)/shard_map/ppermute | solution.py:21
  18.7 5.1 %collective-permute-start.1 = (bf16[16,768]{1,0:T(8,128)(2,1)S(1)}, bf16[16,768]{1,0:T(8,128)(2,1)S(1)}, u32[]{:S(2)}, u32[]{:S(2)}) collective-permute-start(bf16[16,768]{1,0:T(8,128)(2,1)S(1)} %get-tuple-element.29.v), channel_id=1, source_target_pairs={{1,2},{2,1},{3,4},{4,3},{5,6},{6,5},{7,0},{0,7},{9,10},{10,9},{11,... | collective-permute-start | bytes 73736 | tf_op jit(solution)/shard_map/ppermute | solution.py:21
  23.8 2.2 %collective-permute-start = (bf16[16,768]{1,0:T(8,128)(2,1)S(1)}, bf16[16,768]{1,0:T(8,128)(2,1)S(1)}, u32[]{:S(2)}, u32[]{:S(2)}) collective-permute-start(bf16[16,768]{1,0:T(8,128)(2,1)S(1)} %get-tuple-element.29.v), channel_id=1, source_target_pairs={{0,1},{1,0},{2,3},{3,2},{4,5},{5,4},{6,7},{7,6},{8,9},{9,8},{10,11... | collective-permute-start | bytes 73736 | tf_op jit(solution)/shard_map/ppermute | solution.py:21
  26.0 0.0 collective-permute-done.3.next_
  26.0 0.0 collective-permute-done.2.near
  26.1 0.0 collective-permute-done.1.other
  26.1 0.8 collective-permute-done.pair
  26.9 0.4 shard_map.78
  27.3 13.5 %all_to_all.20.coef = bf16[8,32,128]{2,1,0:T(8,128)(2,1)S(1)} all-to-all(bf16[8,32,128]{2,1,0:T(8,128)(2,1)S(1)} %get-tuple-element.32), channel_id=1, replica_groups=mesh['group'=64,'member'=8] {'member'}, dimensions={0} | all-to-all | bytes 131072 | tf_op jit(solution)/shard_map/all_to_all | solution.py:331
  40.8 0.0 copy-start.1
  40.8 0.0 copy-start.2
  40.8 0.5 shard_map.79
  41.3 14.7 %all_to_all.21.arrived = f32[64,4,128]{2,1,0:T(4,128)S(1)} all-to-all(f32[64,4,128]{2,1,0:T(4,128)S(1)} %shard_map.79), channel_id=1, replica_groups=mesh['group'=64,'member'=8] {'group'}, dimensions={0} | all-to-all | bytes 262144 | tf_op jit(solution)/shard_map/all_to_all | solution.py:334
  56.0 0.0 copy-done
  56.0 0.7 shard_map.80
  56.7 4.2 %collective-permute-start.4 = (bf16[32,768]{1,0:T(8,128)(2,1)S(1)}, bf16[32,768]{1,0:T(8,128)(2,1)S(1)}, u32[]{:S(2)}, u32[]{:S(2)}) collective-permute-start(bf16[32,768]{1,0:T(8,128)(2,1)S(1)} %get-tuple-element.39), channel_id=1, source_target_pairs={{0,1},{1,0},{2,3},{3,2},{4,5},{5,4},{6,7},{7,6},{8,9},{9,8},{10,11... | collective-permute-start | bytes 147464 | tf_op jit(solution)/shard_map/ppermute | solution.py:21
  60.9 2.0 %collective-permute-start.5 = (bf16[32,768]{1,0:T(8,128)(2,1)S(1)}, bf16[32,768]{1,0:T(8,128)(2,1)S(1)}, u32[]{:S(2)}, u32[]{:S(2)}) collective-permute-start(bf16[32,768]{1,0:T(8,128)(2,1)S(1)} %get-tuple-element.40), channel_id=1, source_target_pairs={{1,2},{2,1},{3,4},{4,3},{5,6},{6,5},{7,0},{0,7},{9,10},{10,9},{11,... | collective-permute-start | bytes 147464 | tf_op jit(solution)/shard_map/ppermute | solution.py:21
  62.9 3.1 %collective-permute-start.7 = (bf16[32,768]{1,0:T(8,128)(2,1)S(1)}, bf16[32,768]{1,0:T(8,128)(2,1)S(1)}, u32[]{:S(2)}, u32[]{:S(2)}) collective-permute-start(bf16[32,768]{1,0:T(8,128)(2,1)S(1)} %get-tuple-element.41), channel_id=1, source_target_pairs={{8,16},{16,8},{24,32},{32,24},{40,48},{48,40},{56,64},{64,56},{72,... | collective-permute-start | bytes 147464 | tf_op jit(solution)/shard_map/ppermute | solution.py:21
  66.1 1.9 %collective-permute-start.6 = (bf16[32,768]{1,0:T(8,128)(2,1)S(1)}, bf16[32,768]{1,0:T(8,128)(2,1)S(1)}, u32[]{:S(2)}, u32[]{:S(2)}) collective-permute-start(bf16[32,768]{1,0:T(8,128)(2,1)S(1)} %get-tuple-element.41), channel_id=1, source_target_pairs={{0,8},{8,0},{16,24},{24,16},{32,40},{40,32},{48,56},{56,48},{64,72... | collective-permute-start | bytes 147464 | tf_op jit(solution)/shard_map/ppermute | solution.py:21
  68.0 0.0 collective-permute-done.4.pair
  68.0 0.0 collective-permute-done.5.other
  68.0 4.0 %collective-permute-done.7.next_ = bf16[32,768]{1,0:T(8,128)(2,1)S(1)} collective-permute-done((bf16[32,768]{1,0:T(8,128)(2,1)S(1)}, bf16[32,768]{1,0:T(8,128)(2,1)S(1)}, u32[]{:S(2)}, u32[]{:S(2)}) %collective-permute-start.7) | collective-permute-done | bytes 49184 | tf_op jit(solution)/shard_map/ppermute | solution.py:21
  72.0 0.0 collective-permute-done.6.near
  72.0 0.0 copy-done.1
  72.0 0.0 copy-done.2
  72.0 0.7 shard_map.81
  72.7 5.3 %collective-permute-start.9 = (bf16[32,768]{1,0:T(8,128)(2,1)S(1)}, bf16[32,768]{1,0:T(8,128)(2,1)S(1)}, u32[]{:S(2)}, u32[]{:S(2)}) collective-permute-start(bf16[32,768]{1,0:T(8,128)(2,1)S(1)} %get-tuple-element.42.v), channel_id=1, source_target_pairs={{8,16},{16,8},{24,32},{32,24},{40,48},{48,40},{56,64},{64,56},{72,... | collective-permute-start | bytes 147464 | tf_op jit(solution)/shard_map/ppermute | solution.py:21
  78.0 1.9 %collective-permute-start.8 = (bf16[32,768]{1,0:T(8,128)(2,1)S(1)}, bf16[32,768]{1,0:T(8,128)(2,1)S(1)}, u32[]{:S(2)}, u32[]{:S(2)}) collective-permute-start(bf16[32,768]{1,0:T(8,128)(2,1)S(1)} %get-tuple-element.42.v), channel_id=1, source_target_pairs={{0,8},{8,0},{16,24},{24,16},{32,40},{40,32},{48,56},{56,48},{64,72... | collective-permute-start | bytes 147464 | tf_op jit(solution)/shard_map/ppermute | solution.py:21
  79.9 1.8 %collective-permute-done.9.next_ = bf16[32,768]{1,0:T(8,128)(2,1)S(1)} collective-permute-done((bf16[32,768]{1,0:T(8,128)(2,1)S(1)}, bf16[32,768]{1,0:T(8,128)(2,1)S(1)}, u32[]{:S(2)}, u32[]{:S(2)}) %collective-permute-start.9) | collective-permute-done | bytes 49184 | tf_op jit(solution)/shard_map/ppermute | solution.py:21
  81.7 1.4 %collective-permute-done.8.near = bf16[32,768]{1,0:T(8,128)(2,1)S(1)} collective-permute-done((bf16[32,768]{1,0:T(8,128)(2,1)S(1)}, bf16[32,768]{1,0:T(8,128)(2,1)S(1)}, u32[]{:S(2)}, u32[]{:S(2)}) %collective-permute-start.8) | collective-permute-done | bytes 49184 | tf_op jit(solution)/shard_map/ppermute | solution.py:21
  83.1 0.5 shard_map.82
  83.6 15.1 %all_to_all.22.message = bf16[8,32,128]{2,1,0:T(8,128)(2,1)S(1)} all-to-all(bf16[8,32,128]{2,1,0:T(8,128)(2,1)S(1)} %get-tuple-element.45), channel_id=1, replica_groups=mesh['group'=64,'member'=8] {'member'}, dimensions={0} | all-to-all | bytes 131072 | tf_op jit(solution)/shard_map/all_to_all | solution.py:353
  98.7 1.4 %shard_map.83 = (bf16[64,5,4,128]{3,2,1,0:T(4,128)(2,1)S(1)}, f32[16,768]{1,0:T(8,128)S(1)}) custom-call(bf16[8,32,128]{2,1,0:T(8,128)(2,1)S(1)} %all_to_all.22.message, bf16[32,64,256]{2,1,0:T(8,128)(2,1)S(1)} %get-tuple-element.33.inverse, bf16[32,768]{1,0:T(8,128)(2,1)S(1)} %get-tuple-element.42.v, bf16[16,128]{1,0:T(8,128)(2,1)S(1)} %get-tuple-element.46.edge, ...), custom_call_target="tpu_custom_call" | custom-call | tf_op jit(solution)/shard_map/pallas_call | solution.py:25
  100.1 17.0 %all_to_all.23.arrived = bf16[64,5,4,128]{3,2,1,0:T(4,128)(2,1)S(1)} all-to-all(bf16[64,5,4,128]{3,2,1,0:T(4,128)(2,1)S(1)} %get-tuple-element.49), channel_id=1, replica_groups=mesh['group'=64,'member'=8] {'group'}, dimensions={0} | all-to-all | bytes 655360 | tf_op jit(solution)/shard_map/all_to_all | solution.py:360
  117.1 0.4 shard_map.84
  117.6 4.4 %collective-permute-start.11 = (bf16[16,768]{1,0:T(8,128)(2,1)S(1)}, bf16[16,768]{1,0:T(8,128)(2,1)S(1)}, u32[]{:S(2)}, u32[]{:S(2)}) collective-permute-start(bf16[16,768]{1,0:T(8,128)(2,1)S(1)} %get-tuple-element.51.v), channel_id=1, source_target_pairs={{1,2},{2,1},{3,4},{4,3},{5,6},{6,5},{7,0},{0,7},{9,10},{10,9},{11,... | collective-permute-start | bytes 73736 | tf_op jit(solution)/shard_map/ppermute | solution.py:21
  122.0 1.9 %collective-permute-start.10 = (bf16[16,768]{1,0:T(8,128)(2,1)S(1)}, bf16[16,768]{1,0:T(8,128)(2,1)S(1)}, u32[]{:S(2)}, u32[]{:S(2)}) collective-permute-start(bf16[16,768]{1,0:T(8,128)(2,1)S(1)} %get-tuple-element.51.v), channel_id=1, source_target_pairs={{0,1},{1,0},{2,3},{3,2},{4,5},{5,4},{6,7},{7,6},{8,9},{9,8},{10,11... | collective-permute-start | bytes 73736 | tf_op jit(solution)/shard_map/ppermute | solution.py:21
  123.9 0.0 collective-permute-done.11.other
  123.9 1.2 collective-permute-done.10.pair
  125.1 1.2 shard_map.85
Async XLA Ops:
  0.6 55.4 %copy-start = (bf16[1,768,1024]{2,1,0:T(8,128)(2,1)S(1)}, bf16[1,768,1024]{2,1,0:T(8,128)(2,1)}, u32[]{:S(2)}) copy-start(bf16[1,768,1024]{2,1,0:T(8,128)(2,1)} %param.8) | copy-start | bytes 4718596
  2.1 23.9 %collective-permute-start.3 = (bf16[16,768]{1,0:T(8,128)(2,1)S(1)}, bf16[16,768]{1,0:T(8,128)(2,1)S(1)}, u32[]{:S(2)}, u32[]{:S(2)}) collective-permute-start(bf16[16,768]{1,0:T(8,128)(2,1)S(1)} %get-tuple-element.29.v), channel_id=1, source_target_pairs={{8,16},{16,8},{24,32},{32,24},{40,48},{48,40},{56,64},{64,56},{72,... | collective-permute-start | bytes 73736 | tf_op jit(solution)/shard_map/ppermute | solution.py:21
  16.8 9.2 %collective-permute-start.2 = (bf16[16,768]{1,0:T(8,128)(2,1)S(1)}, bf16[16,768]{1,0:T(8,128)(2,1)S(1)}, u32[]{:S(2)}, u32[]{:S(2)}) collective-permute-start(bf16[16,768]{1,0:T(8,128)(2,1)S(1)} %get-tuple-element.29.v), channel_id=1, source_target_pairs={{0,8},{8,0},{16,24},{24,16},{32,40},{40,32},{48,56},{56,48},{64,72... | collective-permute-start | bytes 73736 | tf_op jit(solution)/shard_map/ppermute | solution.py:21
  18.7 7.3 %collective-permute-start.1 = (bf16[16,768]{1,0:T(8,128)(2,1)S(1)}, bf16[16,768]{1,0:T(8,128)(2,1)S(1)}, u32[]{:S(2)}, u32[]{:S(2)}) collective-permute-start(bf16[16,768]{1,0:T(8,128)(2,1)S(1)} %get-tuple-element.29.v), channel_id=1, source_target_pairs={{1,2},{2,1},{3,4},{4,3},{5,6},{6,5},{7,0},{0,7},{9,10},{10,9},{11,... | collective-permute-start | bytes 73736 | tf_op jit(solution)/shard_map/ppermute | solution.py:21
  23.8 3.1 %collective-permute-start = (bf16[16,768]{1,0:T(8,128)(2,1)S(1)}, bf16[16,768]{1,0:T(8,128)(2,1)S(1)}, u32[]{:S(2)}, u32[]{:S(2)}) collective-permute-start(bf16[16,768]{1,0:T(8,128)(2,1)S(1)} %get-tuple-element.29.v), channel_id=1, source_target_pairs={{0,1},{1,0},{2,3},{3,2},{4,5},{5,4},{6,7},{7,6},{8,9},{9,8},{10,11... | collective-permute-start | bytes 73736 | tf_op jit(solution)/shard_map/ppermute | solution.py:21
  40.8 31.2 %copy-start.1 = (bf16[1,768,1024]{2,1,0:T(8,128)(2,1)S(1)}, bf16[1,768,1024]{2,1,0:T(8,128)(2,1)}, u32[]{:S(2)}) copy-start(bf16[1,768,1024]{2,1,0:T(8,128)(2,1)} %param.7) | copy-start | bytes 4718596
  40.8 31.2 %copy-start.2 = (f32[1,16,768]{2,1,0:T(8,128)S(1)}, f32[1,16,768]{2,1,0:T(8,128)}, u32[]{:S(2)}) copy-start(f32[1,16,768]{2,1,0:T(8,128)} %param.6) | copy-start | bytes 147460
  56.7 11.3 %collective-permute-start.4 = (bf16[32,768]{1,0:T(8,128)(2,1)S(1)}, bf16[32,768]{1,0:T(8,128)(2,1)S(1)}, u32[]{:S(2)}, u32[]{:S(2)}) collective-permute-start(bf16[32,768]{1,0:T(8,128)(2,1)S(1)} %get-tuple-element.39), channel_id=1, source_target_pairs={{0,1},{1,0},{2,3},{3,2},{4,5},{5,4},{6,7},{7,6},{8,9},{9,8},{10,11... | collective-permute-start | bytes 147464 | tf_op jit(solution)/shard_map/ppermute | solution.py:21
  60.9 7.1 %collective-permute-start.5 = (bf16[32,768]{1,0:T(8,128)(2,1)S(1)}, bf16[32,768]{1,0:T(8,128)(2,1)S(1)}, u32[]{:S(2)}, u32[]{:S(2)}) collective-permute-start(bf16[32,768]{1,0:T(8,128)(2,1)S(1)} %get-tuple-element.40), channel_id=1, source_target_pairs={{1,2},{2,1},{3,4},{4,3},{5,6},{6,5},{7,0},{0,7},{9,10},{10,9},{11,... | collective-permute-start | bytes 147464 | tf_op jit(solution)/shard_map/ppermute | solution.py:21
  62.9 9.1 %collective-permute-start.7 = (bf16[32,768]{1,0:T(8,128)(2,1)S(1)}, bf16[32,768]{1,0:T(8,128)(2,1)S(1)}, u32[]{:S(2)}, u32[]{:S(2)}) collective-permute-start(bf16[32,768]{1,0:T(8,128)(2,1)S(1)} %get-tuple-element.41), channel_id=1, source_target_pairs={{8,16},{16,8},{24,32},{32,24},{40,48},{48,40},{56,64},{64,56},{72,... | collective-permute-start | bytes 147464 | tf_op jit(solution)/shard_map/ppermute | solution.py:21
  66.1 5.9 %collective-permute-start.6 = (bf16[32,768]{1,0:T(8,128)(2,1)S(1)}, bf16[32,768]{1,0:T(8,128)(2,1)S(1)}, u32[]{:S(2)}, u32[]{:S(2)}) collective-permute-start(bf16[32,768]{1,0:T(8,128)(2,1)S(1)} %get-tuple-element.41), channel_id=1, source_target_pairs={{0,8},{8,0},{16,24},{24,16},{32,40},{40,32},{48,56},{56,48},{64,72... | collective-permute-start | bytes 147464 | tf_op jit(solution)/shard_map/ppermute | solution.py:21
  72.7 9.1 %collective-permute-start.9 = (bf16[32,768]{1,0:T(8,128)(2,1)S(1)}, bf16[32,768]{1,0:T(8,128)(2,1)S(1)}, u32[]{:S(2)}, u32[]{:S(2)}) collective-permute-start(bf16[32,768]{1,0:T(8,128)(2,1)S(1)} %get-tuple-element.42.v), channel_id=1, source_target_pairs={{8,16},{16,8},{24,32},{32,24},{40,48},{48,40},{56,64},{64,56},{72,... | collective-permute-start | bytes 147464 | tf_op jit(solution)/shard_map/ppermute | solution.py:21
  78.0 5.1 %collective-permute-start.8 = (bf16[32,768]{1,0:T(8,128)(2,1)S(1)}, bf16[32,768]{1,0:T(8,128)(2,1)S(1)}, u32[]{:S(2)}, u32[]{:S(2)}) collective-permute-start(bf16[32,768]{1,0:T(8,128)(2,1)S(1)} %get-tuple-element.42.v), channel_id=1, source_target_pairs={{0,8},{8,0},{16,24},{24,16},{32,40},{40,32},{48,56},{56,48},{64,72... | collective-permute-start | bytes 147464 | tf_op jit(solution)/shard_map/ppermute | solution.py:21
  117.6 6.4 %collective-permute-start.11 = (bf16[16,768]{1,0:T(8,128)(2,1)S(1)}, bf16[16,768]{1,0:T(8,128)(2,1)S(1)}, u32[]{:S(2)}, u32[]{:S(2)}) collective-permute-start(bf16[16,768]{1,0:T(8,128)(2,1)S(1)} %get-tuple-element.51.v), channel_id=1, source_target_pairs={{1,2},{2,1},{3,4},{4,3},{5,6},{6,5},{7,0},{0,7},{9,10},{10,9},{11,... | collective-permute-start | bytes 73736 | tf_op jit(solution)/shard_map/ppermute | solution.py:21
  122.0 3.1 %collective-permute-start.10 = (bf16[16,768]{1,0:T(8,128)(2,1)S(1)}, bf16[16,768]{1,0:T(8,128)(2,1)S(1)}, u32[]{:S(2)}, u32[]{:S(2)}) collective-permute-start(bf16[16,768]{1,0:T(8,128)(2,1)S(1)} %get-tuple-element.51.v), channel_id=1, source_target_pairs={{0,1},{1,0},{2,3},{3,2},{4,5},{5,4},{6,7},{7,6},{8,9},{9,8},{10,11... | collective-permute-start | bytes 73736 | tf_op jit(solution)/shard_map/ppermute | solution.py:21

commit v8 on v7

--- a/solution.py
+++ b/solution.py
@@ -125,8 +125,8 @@
 
 
 def restrict_body(v, pair, other, near, next_, picks, basis, block, coef):
-    edge = margins(near[...], next_[...], pair[...], other[...], picks[...])
-    whole = jnp.concatenate([v[...], edge], axis=1)
+    fields = [ref[...].astype(BF16) for ref in (near, next_, pair, other)]
+    whole = jnp.concatenate([v[...], margins(*fields, picks[...])], axis=1)
     block[...] = whole
     part = dot_nt(basis[...], tall(whole)).astype(BF16)
     for m in range(coef.shape[0]):
@@ -321,8 +321,8 @@
         space=pltpu.HBM,
         scratch=(VMEM((cases, owned), F32), VMEM(margin_rows.shape, jnp.int32), pltpu.SemaphoreType.DMA((4,))),
     )
-    near = member_around(field, field)
-    far = group_around(field)
+    near = member_around(own_load, own_load)
+    far = group_around(own_load)
     block, coef = call(
         restrict_body,
         [((cases, nb), BF16), ((members, kdef, LANES), BF16)],

time: 127 us -> 126 us (level)
  transfers between devices with their start and end apart: 12 -> 12, of which waited for: 5 -> 4; matrix products, arithmetic and copies ran while one was open for 0% -> 0% of each run, Pallas kernels for 0% -> 1%
where the time goes in v8:
time: 126 us; the launch traced here: 125 us
  blocking collectives  60.4 us (48%)
  starting transfers between devices  48.6 us (39%)
  waiting for transfers between devices  8.32 us (7%)
  Pallas kernels  7.27 us (6%)
    ppermute x12, starting transfers between devices, exchanged(): return lax.ppermute(shard, axis, pairs)  48.6 us
    all_to_all x2, blocking collectives, local(): arrived = lax.all_to_all(share, 'group', 0, 0, tiled=True)  32 us
    all_to_all x1, blocking collectives, local(): message = lax.all_to_all(message, 'member', 0, 0, tiled=True)  15.1 us
    all_to_all x1, blocking collectives, local(): gathered = lax.all_to_all(coef, 'member', 0, 0, tiled=True)  13.3 us
    ppermute x12, waiting for transfers between devices, exchanged(): return lax.ppermute(shard, axis, pairs)  8.32 us
    pallas_call x9, Pallas kernels, call(): pl.pallas_call(body, out_shape=[jax.ShapeDtypeStruct(shape, dtype) for sh...  7.27 us
  transfers between devices with their start and end apart: 12, of which 4 were waited for; matrix products, arithmetic and copies ran while one was open for 0% of the time, Pallas kernels for 1%

profile of v8, /device:TPU:1, one launch (start us, length us, event | category | flops | bytes accessed | tf_op | source)
XLA Modules:
  0.0 125.4 jit_solution(18089495457681591203)
XLA Ops:
  0.6 14.7 %collective-permute-start.3 = (f32[16,768]{1,0:T(8,128)}, f32[16,768]{1,0:T(8,128)S(1)}, u32[]{:S(2)}, u32[]{:S(2)}) collective-permute-start(f32[16,768]{1,0:T(8,128)} %bitcast.10), channel_id=1, source_target_pairs={{8,16},{16,8},{24,32},{32,24},{40,48},{48,40},{56,64},{64,56},{72,... | collective-permute-start | bytes 147464 | tf_op jit(solution)/shard_map/ppermute | solution.py:21
  15.3 1.9 %collective-permute-start.2 = (f32[16,768]{1,0:T(8,128)}, f32[16,768]{1,0:T(8,128)S(1)}, u32[]{:S(2)}, u32[]{:S(2)}) collective-permute-start(f32[16,768]{1,0:T(8,128)} %bitcast.11), channel_id=1, source_target_pairs={{0,8},{8,0},{16,24},{24,16},{32,40},{40,32},{48,56},{56,48},{64,72... | collective-permute-start | bytes 147464 | tf_op jit(solution)/shard_map/ppermute | solution.py:21
  17.3 5.1 %collective-permute-start.1 = (f32[16,768]{1,0:T(8,128)}, f32[16,768]{1,0:T(8,128)S(1)}, u32[]{:S(2)}, u32[]{:S(2)}) collective-permute-start(f32[16,768]{1,0:T(8,128)} %bitcast.12), channel_id=1, source_target_pairs={{1,2},{2,1},{3,4},{4,3},{5,6},{6,5},{7,0},{0,7},{9,10},{10,9},{11,... | collective-permute-start | bytes 147464 | tf_op jit(solution)/shard_map/ppermute | solution.py:21
  22.3 2.2 %collective-permute-start = (f32[16,768]{1,0:T(8,128)}, f32[16,768]{1,0:T(8,128)S(1)}, u32[]{:S(2)}, u32[]{:S(2)}) collective-permute-start(f32[16,768]{1,0:T(8,128)} %bitcast.13), channel_id=1, source_target_pairs={{0,1},{1,0},{2,3},{3,2},{4,5},{5,4},{6,7},{7,6},{8,9},{9,8},{10,11... | collective-permute-start | bytes 147464 | tf_op jit(solution)/shard_map/ppermute | solution.py:21
  24.6 0.0 copy-start
  24.6 1.5 %shard_map.77 = (bf16[16,768]{1,0:T(8,128)(2,1)S(1)}, bf16[768,256]{1,0:T(8,128)(2,1)S(1)}, bf16[32,1024]{1,0:T(8,128)(2,1)S(1)}, bf16[16,768]{1,0:T(8,128)(2,1)...) custom-call(f32[16,768]{1,0:T(8,128)} %bitcast.14, ...), custom_call_target="tpu_custom_call" | custom-call | tf_op jit(solution)/shard_map/pallas_call | solution.py:25
  26.0 0.0 collective-permute-done.3.next_
  26.1 0.0 collective-permute-done.2.near
  26.1 0.0 collective-permute-done.1.other
  26.1 0.0 collective-permute-done.pair
  26.1 0.4 shard_map.78
  26.5 13.3 %all_to_all.20.coef = bf16[8,32,128]{2,1,0:T(8,128)(2,1)S(1)} all-to-all(bf16[8,32,128]{2,1,0:T(8,128)(2,1)S(1)} %get-tuple-element.32), channel_id=1, replica_groups=mesh['group'=64,'member'=8] {'member'}, dimensions={0} | all-to-all | bytes 131072 | tf_op jit(solution)/shard_map/all_to_all | solution.py:331
  39.8 0.0 copy-start.1
  39.8 0.0 copy-start.2
  39.8 0.5 shard_map.79
  40.3 15.0 %all_to_all.21.arrived = f32[64,4,128]{2,1,0:T(4,128)S(1)} all-to-all(f32[64,4,128]{2,1,0:T(4,128)S(1)} %shard_map.79), channel_id=1, replica_groups=mesh['group'=64,'member'=8] {'group'}, dimensions={0} | all-to-all | bytes 262144 | tf_op jit(solution)/shard_map/all_to_all | solution.py:334
  55.3 0.0 copy-done
  55.3 0.7 shard_map.80
  56.0 4.1 %collective-permute-start.4 = (bf16[32,768]{1,0:T(8,128)(2,1)S(1)}, bf16[32,768]{1,0:T(8,128)(2,1)S(1)}, u32[]{:S(2)}, u32[]{:S(2)}) collective-permute-start(bf16[32,768]{1,0:T(8,128)(2,1)S(1)} %get-tuple-element.39), channel_id=1, source_target_pairs={{0,1},{1,0},{2,3},{3,2},{4,5},{5,4},{6,7},{7,6},{8,9},{9,8},{10,11... | collective-permute-start | bytes 147464 | tf_op jit(solution)/shard_map/ppermute | solution.py:21
  60.1 2.0 %collective-permute-start.5 = (bf16[32,768]{1,0:T(8,128)(2,1)S(1)}, bf16[32,768]{1,0:T(8,128)(2,1)S(1)}, u32[]{:S(2)}, u32[]{:S(2)}) collective-permute-start(bf16[32,768]{1,0:T(8,128)(2,1)S(1)} %get-tuple-element.40), channel_id=1, source_target_pairs={{1,2},{2,1},{3,4},{4,3},{5,6},{6,5},{7,0},{0,7},{9,10},{10,9},{11,... | collective-permute-start | bytes 147464 | tf_op jit(solution)/shard_map/ppermute | solution.py:21
  62.1 3.1 %collective-permute-start.7 = (bf16[32,768]{1,0:T(8,128)(2,1)S(1)}, bf16[32,768]{1,0:T(8,128)(2,1)S(1)}, u32[]{:S(2)}, u32[]{:S(2)}) collective-permute-start(bf16[32,768]{1,0:T(8,128)(2,1)S(1)} %get-tuple-element.41), channel_id=1, source_target_pairs={{8,16},{16,8},{24,32},{32,24},{40,48},{48,40},{56,64},{64,56},{72,... | collective-permute-start | bytes 147464 | tf_op jit(solution)/shard_map/ppermute | solution.py:21
  65.3 1.9 %collective-permute-start.6 = (bf16[32,768]{1,0:T(8,128)(2,1)S(1)}, bf16[32,768]{1,0:T(8,128)(2,1)S(1)}, u32[]{:S(2)}, u32[]{:S(2)}) collective-permute-start(bf16[32,768]{1,0:T(8,128)(2,1)S(1)} %get-tuple-element.41), channel_id=1, source_target_pairs={{0,8},{8,0},{16,24},{24,16},{32,40},{40,32},{48,56},{56,48},{64,72... | collective-permute-start | bytes 147464 | tf_op jit(solution)/shard_map/ppermute | solution.py:21
  67.2 0.0 collective-permute-done.4.pair
  67.2 0.0 collective-permute-done.5.other
  67.2 4.0 %collective-permute-done.7.next_ = bf16[32,768]{1,0:T(8,128)(2,1)S(1)} collective-permute-done((bf16[32,768]{1,0:T(8,128)(2,1)S(1)}, bf16[32,768]{1,0:T(8,128)(2,1)S(1)}, u32[]{:S(2)}, u32[]{:S(2)}) %collective-permute-start.7) | collective-permute-done | bytes 49184 | tf_op jit(solution)/shard_map/ppermute | solution.py:21
  71.2 0.0 collective-permute-done.6.near
  71.2 0.0 copy-done.1
  71.2 0.0 copy-done.2
  71.2 0.7 shard_map.81
  71.8 5.3 %collective-permute-start.9 = (bf16[32,768]{1,0:T(8,128)(2,1)S(1)}, bf16[32,768]{1,0:T(8,128)(2,1)S(1)}, u32[]{:S(2)}, u32[]{:S(2)}) collective-permute-start(bf16[32,768]{1,0:T(8,128)(2,1)S(1)} %get-tuple-element.42.v), channel_id=1, source_target_pairs={{8,16},{16,8},{24,32},{32,24},{40,48},{48,40},{56,64},{64,56},{72,... | collective-permute-start | bytes 147464 | tf_op jit(solution)/shard_map/ppermute | solution.py:21
  77.1 1.9 %collective-permute-start.8 = (bf16[32,768]{1,0:T(8,128)(2,1)S(1)}, bf16[32,768]{1,0:T(8,128)(2,1)S(1)}, u32[]{:S(2)}, u32[]{:S(2)}) collective-permute-start(bf16[32,768]{1,0:T(8,128)(2,1)S(1)} %get-tuple-element.42.v), channel_id=1, source_target_pairs={{0,8},{8,0},{16,24},{24,16},{32,40},{40,32},{48,56},{56,48},{64,72... | collective-permute-start | bytes 147464 | tf_op jit(solution)/shard_map/ppermute | solution.py:21
  79.1 1.8 %collective-permute-done.9.next_ = bf16[32,768]{1,0:T(8,128)(2,1)S(1)} collective-permute-done((bf16[32,768]{1,0:T(8,128)(2,1)S(1)}, bf16[32,768]{1,0:T(8,128)(2,1)S(1)}, u32[]{:S(2)}, u32[]{:S(2)}) %collective-permute-start.9) | collective-permute-done | bytes 49184 | tf_op jit(solution)/shard_map/ppermute | solution.py:21
  80.9 1.4 %collective-permute-done.8.near = bf16[32,768]{1,0:T(8,128)(2,1)S(1)} collective-permute-done((bf16[32,768]{1,0:T(8,128)(2,1)S(1)}, bf16[32,768]{1,0:T(8,128)(2,1)S(1)}, u32[]{:S(2)}, u32[]{:S(2)}) %collective-permute-start.8) | collective-permute-done | bytes 49184 | tf_op jit(solution)/shard_map/ppermute | solution.py:21
  82.3 0.5 shard_map.82
  82.8 15.1 %all_to_all.22.message = bf16[8,32,128]{2,1,0:T(8,128)(2,1)S(1)} all-to-all(bf16[8,32,128]{2,1,0:T(8,128)(2,1)S(1)} %get-tuple-element.45), channel_id=1, replica_groups=mesh['group'=64,'member'=8] {'member'}, dimensions={0} | all-to-all | bytes 131072 | tf_op jit(solution)/shard_map/all_to_all | solution.py:353
  97.9 1.4 %shard_map.83 = (bf16[64,5,4,128]{3,2,1,0:T(4,128)(2,1)S(1)}, f32[16,768]{1,0:T(8,128)S(1)}) custom-call(bf16[8,32,128]{2,1,0:T(8,128)(2,1)S(1)} %all_to_all.22.message, bf16[32,64,256]{2,1,0:T(8,128)(2,1)S(1)} %get-tuple-element.33.inverse, bf16[32,768]{1,0:T(8,128)(2,1)S(1)} %get-tuple-element.42.v, bf16[16,128]{1,0:T(8,128)(2,1)S(1)} %get-tuple-element.46.edge, ...), custom_call_target="tpu_custom_call" | custom-call | tf_op jit(solution)/shard_map/pallas_call | solution.py:25
  99.3 17.0 %all_to_all.23.arrived = bf16[64,5,4,128]{3,2,1,0:T(4,128)(2,1)S(1)} all-to-all(bf16[64,5,4,128]{3,2,1,0:T(4,128)(2,1)S(1)} %get-tuple-element.49), channel_id=1, replica_groups=mesh['group'=64,'member'=8] {'group'}, dimensions={0} | all-to-all | bytes 655360 | tf_op jit(solution)/shard_map/all_to_all | solution.py:360
  116.3 0.4 shard_map.84
  116.7 4.4 %collective-permute-start.11 = (bf16[16,768]{1,0:T(8,128)(2,1)S(1)}, bf16[16,768]{1,0:T(8,128)(2,1)S(1)}, u32[]{:S(2)}, u32[]{:S(2)}) collective-permute-start(bf16[16,768]{1,0:T(8,128)(2,1)S(1)} %get-tuple-element.51.v), channel_id=1, source_target_pairs={{1,2},{2,1},{3,4},{4,3},{5,6},{6,5},{7,0},{0,7},{9,10},{10,9},{11,... | collective-permute-start | bytes 73736 | tf_op jit(solution)/shard_map/ppermute | solution.py:21
  121.2 1.9 %collective-permute-start.10 = (bf16[16,768]{1,0:T(8,128)(2,1)S(1)}, bf16[16,768]{1,0:T(8,128)(2,1)S(1)}, u32[]{:S(2)}, u32[]{:S(2)}) collective-permute-start(bf16[16,768]{1,0:T(8,128)(2,1)S(1)} %get-tuple-element.51.v), channel_id=1, source_target_pairs={{0,1},{1,0},{2,3},{3,2},{4,5},{5,4},{6,7},{7,6},{8,9},{9,8},{10,11... | collective-permute-start | bytes 73736 | tf_op jit(solution)/shard_map/ppermute | solution.py:21
  123.1 0.0 collective-permute-done.11.other
  123.1 1.2 collective-permute-done.10.pair
  124.2 1.2 shard_map.85
Async XLA Ops:
  0.6 25.4 %collective-permute-start.3 = (f32[16,768]{1,0:T(8,128)}, f32[16,768]{1,0:T(8,128)S(1)}, u32[]{:S(2)}, u32[]{:S(2)}) collective-permute-start(f32[16,768]{1,0:T(8,128)} %bitcast.10), channel_id=1, source_target_pairs={{8,16},{16,8},{24,32},{32,24},{40,48},{48,40},{56,64},{64,56},{72,... | collective-permute-start | bytes 147464 | tf_op jit(solution)/shard_map/ppermute | solution.py:21
  15.3 10.7 %collective-permute-start.2 = (f32[16,768]{1,0:T(8,128)}, f32[16,768]{1,0:T(8,128)S(1)}, u32[]{:S(2)}, u32[]{:S(2)}) collective-permute-start(f32[16,768]{1,0:T(8,128)} %bitcast.11), channel_id=1, source_target_pairs={{0,8},{8,0},{16,24},{24,16},{32,40},{40,32},{48,56},{56,48},{64,72... | collective-permute-start | bytes 147464 | tf_op jit(solution)/shard_map/ppermute | solution.py:21
  17.3 8.8 %collective-permute-start.1 = (f32[16,768]{1,0:T(8,128)}, f32[16,768]{1,0:T(8,128)S(1)}, u32[]{:S(2)}, u32[]{:S(2)}) collective-permute-start(f32[16,768]{1,0:T(8,128)} %bitcast.12), channel_id=1, source_target_pairs={{1,2},{2,1},{3,4},{4,3},{5,6},{6,5},{7,0},{0,7},{9,10},{10,9},{11,... | collective-permute-start | bytes 147464 | tf_op jit(solution)/shard_map/ppermute | solution.py:21
  22.3 3.7 %collective-permute-start = (f32[16,768]{1,0:T(8,128)}, f32[16,768]{1,0:T(8,128)S(1)}, u32[]{:S(2)}, u32[]{:S(2)}) collective-permute-start(f32[16,768]{1,0:T(8,128)} %bitcast.13), channel_id=1, source_target_pairs={{0,1},{1,0},{2,3},{3,2},{4,5},{5,4},{6,7},{7,6},{8,9},{9,8},{10,11... | collective-permute-start | bytes 147464 | tf_op jit(solution)/shard_map/ppermute | solution.py:21
  24.6 30.7 %copy-start = (bf16[1,768,1024]{2,1,0:T(8,128)(2,1)S(1)}, bf16[1,768,1024]{2,1,0:T(8,128)(2,1)}, u32[]{:S(2)}) copy-start(bf16[1,768,1024]{2,1,0:T(8,128)(2,1)} %param.8) | copy-start | bytes 4718596
  39.8 31.4 %copy-start.1 = (bf16[1,768,1024]{2,1,0:T(8,128)(2,1)S(1)}, bf16[1,768,1024]{2,1,0:T(8,128)(2,1)}, u32[]{:S(2)}) copy-start(bf16[1,768,1024]{2,1,0:T(8,128)(2,1)} %param.7) | copy-start | bytes 4718596
  39.8 31.4 %copy-start.2 = (f32[1,16,768]{2,1,0:T(8,128)S(1)}, f32[1,16,768]{2,1,0:T(8,128)}, u32[]{:S(2)}) copy-start(f32[1,16,768]{2,1,0:T(8,128)} %param.6) | copy-start | bytes 147460
  56.0 11.2 %collective-permute-start.4 = (bf16[32,768]{1,0:T(8,128)(2,1)S(1)}, bf16[32,768]{1,0:T(8,128)(2,1)S(1)}, u32[]{:S(2)}, u32[]{:S(2)}) collective-permute-start(bf16[32,768]{1,0:T(8,128)(2,1)S(1)} %get-tuple-element.39), channel_id=1, source_target_pairs={{0,1},{1,0},{2,3},{3,2},{4,5},{5,4},{6,7},{7,6},{8,9},{9,8},{10,11... | collective-permute-start | bytes 147464 | tf_op jit(solution)/shard_map/ppermute | solution.py:21
  60.1 7.1 %collective-permute-start.5 = (bf16[32,768]{1,0:T(8,128)(2,1)S(1)}, bf16[32,768]{1,0:T(8,128)(2,1)S(1)}, u32[]{:S(2)}, u32[]{:S(2)}) collective-permute-start(bf16[32,768]{1,0:T(8,128)(2,1)S(1)} %get-tuple-element.40), channel_id=1, source_target_pairs={{1,2},{2,1},{3,4},{4,3},{5,6},{6,5},{7,0},{0,7},{9,10},{10,9},{11,... | collective-permute-start | bytes 147464 | tf_op jit(solution)/shard_map/ppermute | solution.py:21
  62.1 9.1 %collective-permute-start.7 = (bf16[32,768]{1,0:T(8,128)(2,1)S(1)}, bf16[32,768]{1,0:T(8,128)(2,1)S(1)}, u32[]{:S(2)}, u32[]{:S(2)}) collective-permute-start(bf16[32,768]{1,0:T(8,128)(2,1)S(1)} %get-tuple-element.41), channel_id=1, source_target_pairs={{8,16},{16,8},{24,32},{32,24},{40,48},{48,40},{56,64},{64,56},{72,... | collective-permute-start | bytes 147464 | tf_op jit(solution)/shard_map/ppermute | solution.py:21
  65.3 5.9 %collective-permute-start.6 = (bf16[32,768]{1,0:T(8,128)(2,1)S(1)}, bf16[32,768]{1,0:T(8,128)(2,1)S(1)}, u32[]{:S(2)}, u32[]{:S(2)}) collective-permute-start(bf16[32,768]{1,0:T(8,128)(2,1)S(1)} %get-tuple-element.41), channel_id=1, source_target_pairs={{0,8},{8,0},{16,24},{24,16},{32,40},{40,32},{48,56},{56,48},{64,72... | collective-permute-start | bytes 147464 | tf_op jit(solution)/shard_map/ppermute | solution.py:21
  71.8 9.1 %collective-permute-start.9 = (bf16[32,768]{1,0:T(8,128)(2,1)S(1)}, bf16[32,768]{1,0:T(8,128)(2,1)S(1)}, u32[]{:S(2)}, u32[]{:S(2)}) collective-permute-start(bf16[32,768]{1,0:T(8,128)(2,1)S(1)} %get-tuple-element.42.v), channel_id=1, source_target_pairs={{8,16},{16,8},{24,32},{32,24},{40,48},{48,40},{56,64},{64,56},{72,... | collective-permute-start | bytes 147464 | tf_op jit(solution)/shard_map/ppermute | solution.py:21
  77.1 5.1 %collective-permute-start.8 = (bf16[32,768]{1,0:T(8,128)(2,1)S(1)}, bf16[32,768]{1,0:T(8,128)(2,1)S(1)}, u32[]{:S(2)}, u32[]{:S(2)}) collective-permute-start(bf16[32,768]{1,0:T(8,128)(2,1)S(1)} %get-tuple-element.42.v), channel_id=1, source_target_pairs={{0,8},{8,0},{16,24},{24,16},{32,40},{40,32},{48,56},{56,48},{64,72... | collective-permute-start | bytes 147464 | tf_op jit(solution)/shard_map/ppermute | solution.py:21
  116.7 6.4 %collective-permute-start.11 = (bf16[16,768]{1,0:T(8,128)(2,1)S(1)}, bf16[16,768]{1,0:T(8,128)(2,1)S(1)}, u32[]{:S(2)}, u32[]{:S(2)}) collective-permute-start(bf16[16,768]{1,0:T(8,128)(2,1)S(1)} %get-tuple-element.51.v), channel_id=1, source_target_pairs={{1,2},{2,1},{3,4},{4,3},{5,6},{6,5},{7,0},{0,7},{9,10},{10,9},{11,... | collective-permute-start | bytes 73736 | tf_op jit(solution)/shard_map/ppermute | solution.py:21
  121.2 3.1 %collective-permute-start.10 = (bf16[16,768]{1,0:T(8,128)(2,1)S(1)}, bf16[16,768]{1,0:T(8,128)(2,1)S(1)}, u32[]{:S(2)}, u32[]{:S(2)}) collective-permute-start(bf16[16,768]{1,0:T(8,128)(2,1)S(1)} %get-tuple-element.51.v), channel_id=1, source_target_pairs={{0,1},{1,0},{2,3},{3,2},{4,5},{5,4},{6,7},{7,6},{8,9},{9,8},{10,11... | collective-permute-start | bytes 73736 | tf_op jit(solution)/shard_map/ppermute | solution.py:21

commit v9 on v8

--- a/solution.py
+++ b/solution.py
@@ -176,7 +176,7 @@
     shares_of(coef[...].reshape(-1, LANES), inverse, share)
 
 
-def coarse_mixed_body(message, inverse, v, edge, inverse_rows, before, choice, out, total, share):
+def coarse_mixed_body(message, inverse, v, edge, inverse_rows, before, choice, basis, out, total, share):
     peers, kdef, _ = message.shape
     source = lax.broadcasted_iota(jnp.int32, (LANES, 3 * LANES), 0)
     target = lanes((LANES, 3 * LANES))
@@ -209,20 +209,29 @@
     out[:1, 1] = short[-1:]
     out[:-1, 2] = short[1:]
     out[-1:, 2] = short[:1]
-    out[:, 3:] = jnp.zeros((groups, 2) + short.shape[1:], BF16)
-    chosen = dot_nn(value.astype(BF16), choice[...])
+    out[:, 3:] = jnp.zeros((groups, 1) + short.shape[1:], BF16)
+    mine = spread_of(share[lax.axis_index("group")], kdef)
+    shown = value + dot_nn(mine, basis[:, : value.shape[1]])
+    chosen = dot_nn(shown.astype(BF16), choice[...])
     top, low = chosen[: CASES // 2], pltpu.roll(chosen, HALF, 1)[CASES // 2 :]
     side = lanes(top.shape) < HALF
     near, next_ = partners("group", groups)
     rows = short.shape[1]
-    for target, kept in ((near, jnp.where(side, low, top)), (next_, jnp.where(side, top, low))):
+    slot = jnp.where(even("group"), 1, 2)
+    for target, at, kept in (
+        (near, slot, jnp.where(side, low, top)),
+        (next_, 3 - slot, jnp.where(side, top, low)),
+    ):
         kept = kept.astype(BF16)
-        out[target, 3] = kept[:rows]
-        out[target, 4] = kept[rows:]
+        out[target, at] = kept[:rows]
+        out[target, 3] = kept[rows:]
 
 
 def prolong_of(arrived, kdef):
-    total = jnp.sum(arrived, axis=0)
+    return spread_of(jnp.sum(arrived, axis=0), kdef)
+
+
+def spread_of(total, kdef):
     tiles = total.shape[0]
     row = lax.broadcasted_iota(jnp.int32, (CASES, LANES), 0)
     lane = lanes((CASES, LANES))
@@ -252,15 +261,23 @@
     kdef = basis.shape[0]
     upward = even("group")
     first, second = partners("group", arrived.shape[0])
-    take = lambda k: jnp.concatenate([arrived[k, 3], arrived[k, 4]], axis=0).astype(F32)
+    slot = jnp.where(upward, 1, 2)
+    take = lambda k, at: jnp.concatenate([arrived[k, at], arrived[k, 3]], axis=0).astype(F32)
     widen = lambda part: jnp.concatenate([part, pltpu.roll(part, HALF, 1)], axis=0)
     left = lanes((CASES, LANES)) < HALF
-    known = jnp.where(left, widen(take(second)), widen(take(first)))
+    known = jnp.where(left, widen(take(second, slot)), widen(take(first, 3 - slot)))
     known = jnp.where(upward, known, pltpu.roll(known, HALF, 1))
     unfold = lambda ref: jnp.concatenate([ref[CASES:, :LANES], ref[CASES:, LANES : 2 * LANES]], axis=0)
     vectors = jnp.where(lanes((kdef, LANES)) < HALF, unfold(next_).astype(F32), unfold(near).astype(F32))
     vectors = jnp.where(upward, vectors, pltpu.roll(vectors, HALF, 1)).astype(BF16)
-    prolong = [prolong_of(arrived[:, k].astype(F32), kdef) for k in range(3)]
+    me = lax.axis_index("group")
+    groups = arrived.shape[0]
+    source = lax.broadcasted_iota(jnp.int32, (groups,) + arrived.shape[2:], 0)
+    lower, upper = lax.rem(me + groups - 1, groups), lax.rem(me + 1, groups)
+    shares = [arrived[:, k].astype(F32) for k in range(3)]
+    shares[1] = jnp.where(source == lower, 0.0, shares[1])
+    shares[2] = jnp.where(source == upper, 0.0, shares[2])
+    prolong = [prolong_of(share, kdef) for share in shares]
     added = jnp.where(left, dot_nn(prolong[1], vectors), dot_nn(prolong[2], vectors))
     edge[...] = (known + added).astype(BF16)
     value = before[...] + dot_nn(prolong[0], basis[:, : total.shape[1]])
@@ -353,8 +370,8 @@
     message = lax.all_to_all(message, "member", 0, 0, tiled=True)
     share, total = call(
         coarse_mixed_body,
-        [((groups, 5, tiles, LANES), BF16), ((cases, owned), F32)],
-        message, inverse_coarse, field, edge, inverse_rows, total, choice,
+        [((groups, 4, tiles, LANES), BF16), ((cases, owned), F32)],
+        message, inverse_coarse, field, edge, inverse_rows, total, choice, basis,
         scratch=(VMEM((groups, tiles, LANES), F32),),
     )
     arrived = lax.all_to_all(share, "group", 0, 0, tiled=True)

time: 126 us -> 125 us (level)
  blocking collectives: 60.4 us -> 58.6 us
    all_to_all x2, blocking collectives: 32 us -> 30.2 us  [local(): arrived = lax.all_to_all(share, 'group', 0, 0, tiled=True)]
where the time goes in v9:
time: 125 us; the launch traced here: 124 us
  blocking collectives  58.6 us (47%)
  starting transfers between devices  49.1 us (39%)
  waiting for transfers between devices  8.32 us (7%)
  Pallas kernels  7.33 us (6%)
    ppermute x12, starting transfers between devices, exchanged(): return lax.ppermute(shard, axis, pairs)  49.1 us
    all_to_all x2, blocking collectives, local(): arrived = lax.all_to_all(share, 'group', 0, 0, tiled=True)  30.2 us
    all_to_all x1, blocking collectives, local(): message = lax.all_to_all(message, 'member', 0, 0, tiled=True)  15.1 us
    all_to_all x1, blocking collectives, local(): gathered = lax.all_to_all(coef, 'member', 0, 0, tiled=True)  13.3 us
    ppermute x12, waiting for transfers between devices, exchanged(): return lax.ppermute(shard, axis, pairs)  8.32 us
    pallas_call x9, Pallas kernels, call(): pl.pallas_call(body, out_shape=[jax.ShapeDtypeStruct(shape, dtype) for sh...  7.33 us
  transfers between devices with their start and end apart: 12, of which 4 were waited for; matrix products, arithmetic and copies ran while one was open for 0% of the time, Pallas kernels for 1%

profile of v9, /device:TPU:1, one launch (start us, length us, event | category | flops | bytes accessed | tf_op | source)
XLA Modules:
  0.0 124.2 jit_solution(1181654345977168139)
XLA Ops:
  0.6 14.7 %collective-permute-start.3 = (f32[16,768]{1,0:T(8,128)}, f32[16,768]{1,0:T(8,128)S(1)}, u32[]{:S(2)}, u32[]{:S(2)}) collective-permute-start(f32[16,768]{1,0:T(8,128)} %bitcast.10), channel_id=1, source_target_pairs={{8,16},{16,8},{24,32},{32,24},{40,48},{48,40},{56,64},{64,56},{72,... | collective-permute-start | bytes 147464 | tf_op jit(solution)/shard_map/ppermute | solution.py:21
  15.3 1.9 %collective-permute-start.2 = (f32[16,768]{1,0:T(8,128)}, f32[16,768]{1,0:T(8,128)S(1)}, u32[]{:S(2)}, u32[]{:S(2)}) collective-permute-start(f32[16,768]{1,0:T(8,128)} %bitcast.11), channel_id=1, source_target_pairs={{0,8},{8,0},{16,24},{24,16},{32,40},{40,32},{48,56},{56,48},{64,72... | collective-permute-start | bytes 147464 | tf_op jit(solution)/shard_map/ppermute | solution.py:21
  17.3 5.1 %collective-permute-start.1 = (f32[16,768]{1,0:T(8,128)}, f32[16,768]{1,0:T(8,128)S(1)}, u32[]{:S(2)}, u32[]{:S(2)}) collective-permute-start(f32[16,768]{1,0:T(8,128)} %bitcast.12), channel_id=1, source_target_pairs={{1,2},{2,1},{3,4},{4,3},{5,6},{6,5},{7,0},{0,7},{9,10},{10,9},{11,... | collective-permute-start | bytes 147464 | tf_op jit(solution)/shard_map/ppermute | solution.py:21
  22.3 2.2 %collective-permute-start = (f32[16,768]{1,0:T(8,128)}, f32[16,768]{1,0:T(8,128)S(1)}, u32[]{:S(2)}, u32[]{:S(2)}) collective-permute-start(f32[16,768]{1,0:T(8,128)} %bitcast.13), channel_id=1, source_target_pairs={{0,1},{1,0},{2,3},{3,2},{4,5},{5,4},{6,7},{7,6},{8,9},{9,8},{10,11... | collective-permute-start | bytes 147464 | tf_op jit(solution)/shard_map/ppermute | solution.py:21
  24.6 0.0 copy-start
  24.6 1.5 %shard_map.77 = (bf16[16,768]{1,0:T(8,128)(2,1)S(1)}, bf16[768,256]{1,0:T(8,128)(2,1)S(1)}, bf16[32,1024]{1,0:T(8,128)(2,1)S(1)}, bf16[16,768]{1,0:T(8,128)(2,1)...) custom-call(f32[16,768]{1,0:T(8,128)} %bitcast.14, ...), custom_call_target="tpu_custom_call" | custom-call | tf_op jit(solution)/shard_map/pallas_call | solution.py:25
  26.0 0.0 collective-permute-done.3.next_
  26.1 0.0 collective-permute-done.2.near
  26.1 0.0 collective-permute-done.1.other
  26.1 0.0 collective-permute-done.pair
  26.1 0.4 shard_map.78
  26.5 13.3 %all_to_all.20.coef = bf16[8,32,128]{2,1,0:T(8,128)(2,1)S(1)} all-to-all(bf16[8,32,128]{2,1,0:T(8,128)(2,1)S(1)} %get-tuple-element.32), channel_id=1, replica_groups=mesh['group'=64,'member'=8] {'member'}, dimensions={0} | all-to-all | bytes 131072 | tf_op jit(solution)/shard_map/all_to_all | solution.py:348
  39.8 0.0 copy-start.1
  39.8 0.0 copy-start.2
  39.8 0.5 shard_map.79
  40.3 15.0 %all_to_all.21.arrived = f32[64,4,128]{2,1,0:T(4,128)S(1)} all-to-all(f32[64,4,128]{2,1,0:T(4,128)S(1)} %shard_map.79), channel_id=1, replica_groups=mesh['group'=64,'member'=8] {'group'}, dimensions={0} | all-to-all | bytes 262144 | tf_op jit(solution)/shard_map/all_to_all | solution.py:351
  55.3 0.0 copy-done
  55.3 0.7 shard_map.80
  56.0 4.1 %collective-permute-start.4 = (bf16[32,768]{1,0:T(8,128)(2,1)S(1)}, bf16[32,768]{1,0:T(8,128)(2,1)S(1)}, u32[]{:S(2)}, u32[]{:S(2)}) collective-permute-start(bf16[32,768]{1,0:T(8,128)(2,1)S(1)} %get-tuple-element.39), channel_id=1, source_target_pairs={{0,1},{1,0},{2,3},{3,2},{4,5},{5,4},{6,7},{7,6},{8,9},{9,8},{10,11... | collective-permute-start | bytes 147464 | tf_op jit(solution)/shard_map/ppermute | solution.py:21
  60.1 2.0 %collective-permute-start.5 = (bf16[32,768]{1,0:T(8,128)(2,1)S(1)}, bf16[32,768]{1,0:T(8,128)(2,1)S(1)}, u32[]{:S(2)}, u32[]{:S(2)}) collective-permute-start(bf16[32,768]{1,0:T(8,128)(2,1)S(1)} %get-tuple-element.40), channel_id=1, source_target_pairs={{1,2},{2,1},{3,4},{4,3},{5,6},{6,5},{7,0},{0,7},{9,10},{10,9},{11,... | collective-permute-start | bytes 147464 | tf_op jit(solution)/shard_map/ppermute | solution.py:21
  62.1 3.1 %collective-permute-start.7 = (bf16[32,768]{1,0:T(8,128)(2,1)S(1)}, bf16[32,768]{1,0:T(8,128)(2,1)S(1)}, u32[]{:S(2)}, u32[]{:S(2)}) collective-permute-start(bf16[32,768]{1,0:T(8,128)(2,1)S(1)} %get-tuple-element.41), channel_id=1, source_target_pairs={{8,16},{16,8},{24,32},{32,24},{40,48},{48,40},{56,64},{64,56},{72,... | collective-permute-start | bytes 147464 | tf_op jit(solution)/shard_map/ppermute | solution.py:21
  65.3 1.9 %collective-permute-start.6 = (bf16[32,768]{1,0:T(8,128)(2,1)S(1)}, bf16[32,768]{1,0:T(8,128)(2,1)S(1)}, u32[]{:S(2)}, u32[]{:S(2)}) collective-permute-start(bf16[32,768]{1,0:T(8,128)(2,1)S(1)} %get-tuple-element.41), channel_id=1, source_target_pairs={{0,8},{8,0},{16,24},{24,16},{32,40},{40,32},{48,56},{56,48},{64,72... | collective-permute-start | bytes 147464 | tf_op jit(solution)/shard_map/ppermute | solution.py:21
  67.2 0.0 collective-permute-done.4.pair
  67.2 0.0 collective-permute-done.5.other
  67.2 4.0 %collective-permute-done.7.next_ = bf16[32,768]{1,0:T(8,128)(2,1)S(1)} collective-permute-done((bf16[32,768]{1,0:T(8,128)(2,1)S(1)}, bf16[32,768]{1,0:T(8,128)(2,1)S(1)}, u32[]{:S(2)}, u32[]{:S(2)}) %collective-permute-start.7) | collective-permute-done | bytes 49184 | tf_op jit(solution)/shard_map/ppermute | solution.py:21
  71.2 0.0 collective-permute-done.6.near
  71.2 0.0 copy-done.1
  71.2 0.0 copy-done.2
  71.2 0.7 shard_map.81
  71.8 5.3 %collective-permute-start.9 = (bf16[32,768]{1,0:T(8,128)(2,1)S(1)}, bf16[32,768]{1,0:T(8,128)(2,1)S(1)}, u32[]{:S(2)}, u32[]{:S(2)}) collective-permute-start(bf16[32,768]{1,0:T(8,128)(2,1)S(1)} %get-tuple-element.42.v), channel_id=1, source_target_pairs={{8,16},{16,8},{24,32},{32,24},{40,48},{48,40},{56,64},{64,56},{72,... | collective-permute-start | bytes 147464 | tf_op jit(solution)/shard_map/ppermute | solution.py:21
  77.1 1.9 %collective-permute-start.8 = (bf16[32,768]{1,0:T(8,128)(2,1)S(1)}, bf16[32,768]{1,0:T(8,128)(2,1)S(1)}, u32[]{:S(2)}, u32[]{:S(2)}) collective-permute-start(bf16[32,768]{1,0:T(8,128)(2,1)S(1)} %get-tuple-element.42.v), channel_id=1, source_target_pairs={{0,8},{8,0},{16,24},{24,16},{32,40},{40,32},{48,56},{56,48},{64,72... | collective-permute-start | bytes 147464 | tf_op jit(solution)/shard_map/ppermute | solution.py:21
  79.0 1.8 %collective-permute-done.9.next_ = bf16[32,768]{1,0:T(8,128)(2,1)S(1)} collective-permute-done((bf16[32,768]{1,0:T(8,128)(2,1)S(1)}, bf16[32,768]{1,0:T(8,128)(2,1)S(1)}, u32[]{:S(2)}, u32[]{:S(2)}) %collective-permute-start.9) | collective-permute-done | bytes 49184 | tf_op jit(solution)/shard_map/ppermute | solution.py:21
  80.9 1.4 %collective-permute-done.8.near = bf16[32,768]{1,0:T(8,128)(2,1)S(1)} collective-permute-done((bf16[32,768]{1,0:T(8,128)(2,1)S(1)}, bf16[32,768]{1,0:T(8,128)(2,1)S(1)}, u32[]{:S(2)}, u32[]{:S(2)}) %collective-permute-start.8) | collective-permute-done | bytes 49184 | tf_op jit(solution)/shard_map/ppermute | solution.py:21
  82.3 0.5 shard_map.82
  82.8 15.1 %all_to_all.22.message = bf16[8,32,128]{2,1,0:T(8,128)(2,1)S(1)} all-to-all(bf16[8,32,128]{2,1,0:T(8,128)(2,1)S(1)} %get-tuple-element.45), channel_id=1, replica_groups=mesh['group'=64,'member'=8] {'member'}, dimensions={0} | all-to-all | bytes 131072 | tf_op jit(solution)/shard_map/all_to_all | solution.py:370
  97.9 1.4 %shard_map.83 = (bf16[64,4,4,128]{3,2,1,0:T(4,128)(2,1)S(1)}, f32[16,768]{1,0:T(8,128)S(1)}) custom-call(bf16[8,32,128]{2,1,0:T(8,128)(2,1)S(1)} %all_to_all.22.message, bf16[32,64,256]{2,1,0:T(8,128)(2,1)S(1)} %get-tuple-element.33.inverse, bf16[32,768]{1,0:T(8,128)(2,1)S(1)} %get-tuple-element.42.v, bf16[16,128]{1,0:T(8,128)(2,1)S(1)} %get-tuple-element.46.edge, ...), custom_call_target="tpu_custom_call" | custom-call | tf_op jit(solution)/shard_map/pallas_call | solution.py:25
  99.3 15.2 %all_to_all.23.arrived = bf16[64,4,4,128]{3,2,1,0:T(4,128)(2,1)S(1)} all-to-all(bf16[64,4,4,128]{3,2,1,0:T(4,128)(2,1)S(1)} %get-tuple-element.49), channel_id=1, replica_groups=mesh['group'=64,'member'=8] {'group'}, dimensions={0} | all-to-all | bytes 524288 | tf_op jit(solution)/shard_map/all_to_all | solution.py:377
  114.5 0.5 shard_map.84
  115.0 4.9 %collective-permute-start.11 = (bf16[16,768]{1,0:T(8,128)(2,1)S(1)}, bf16[16,768]{1,0:T(8,128)(2,1)S(1)}, u32[]{:S(2)}, u32[]{:S(2)}) collective-permute-start(bf16[16,768]{1,0:T(8,128)(2,1)S(1)} %get-tuple-element.51.v), channel_id=1, source_target_pairs={{1,2},{2,1},{3,4},{4,3},{5,6},{6,5},{7,0},{0,7},{9,10},{10,9},{11,... | collective-permute-start | bytes 73736 | tf_op jit(solution)/shard_map/ppermute | solution.py:21
  119.9 1.9 %collective-permute-start.10 = (bf16[16,768]{1,0:T(8,128)(2,1)S(1)}, bf16[16,768]{1,0:T(8,128)(2,1)S(1)}, u32[]{:S(2)}, u32[]{:S(2)}) collective-permute-start(bf16[16,768]{1,0:T(8,128)(2,1)S(1)} %get-tuple-element.51.v), channel_id=1, source_target_pairs={{0,1},{1,0},{2,3},{3,2},{4,5},{5,4},{6,7},{7,6},{8,9},{9,8},{10,11... | collective-permute-start | bytes 73736 | tf_op jit(solution)/shard_map/ppermute | solution.py:21
  121.9 0.0 collective-permute-done.11.other
  121.9 1.2 collective-permute-done.10.pair
  123.0 1.2 shard_map.85
Async XLA Ops:
  0.6 25.4 %collective-permute-start.3 = (f32[16,768]{1,0:T(8,128)}, f32[16,768]{1,0:T(8,128)S(1)}, u32[]{:S(2)}, u32[]{:S(2)}) collective-permute-start(f32[16,768]{1,0:T(8,128)} %bitcast.10), channel_id=1, source_target_pairs={{8,16},{16,8},{24,32},{32,24},{40,48},{48,40},{56,64},{64,56},{72,... | collective-permute-start | bytes 147464 | tf_op jit(solution)/shard_map/ppermute | solution.py:21
  15.3 10.7 %collective-permute-start.2 = (f32[16,768]{1,0:T(8,128)}, f32[16,768]{1,0:T(8,128)S(1)}, u32[]{:S(2)}, u32[]{:S(2)}) collective-permute-start(f32[16,768]{1,0:T(8,128)} %bitcast.11), channel_id=1, source_target_pairs={{0,8},{8,0},{16,24},{24,16},{32,40},{40,32},{48,56},{56,48},{64,72... | collective-permute-start | bytes 147464 | tf_op jit(solution)/shard_map/ppermute | solution.py:21
  17.3 8.8 %collective-permute-start.1 = (f32[16,768]{1,0:T(8,128)}, f32[16,768]{1,0:T(8,128)S(1)}, u32[]{:S(2)}, u32[]{:S(2)}) collective-permute-start(f32[16,768]{1,0:T(8,128)} %bitcast.12), channel_id=1, source_target_pairs={{1,2},{2,1},{3,4},{4,3},{5,6},{6,5},{7,0},{0,7},{9,10},{10,9},{11,... | collective-permute-start | bytes 147464 | tf_op jit(solution)/shard_map/ppermute | solution.py:21
  22.3 3.7 %collective-permute-start = (f32[16,768]{1,0:T(8,128)}, f32[16,768]{1,0:T(8,128)S(1)}, u32[]{:S(2)}, u32[]{:S(2)}) collective-permute-start(f32[16,768]{1,0:T(8,128)} %bitcast.13), channel_id=1, source_target_pairs={{0,1},{1,0},{2,3},{3,2},{4,5},{5,4},{6,7},{7,6},{8,9},{9,8},{10,11... | collective-permute-start | bytes 147464 | tf_op jit(solution)/shard_map/ppermute | solution.py:21
  24.6 30.7 %copy-start = (bf16[1,768,1024]{2,1,0:T(8,128)(2,1)S(1)}, bf16[1,768,1024]{2,1,0:T(8,128)(2,1)}, u32[]{:S(2)}) copy-start(bf16[1,768,1024]{2,1,0:T(8,128)(2,1)} %param.8) | copy-start | bytes 4718596
  39.8 31.4 %copy-start.1 = (bf16[1,768,1024]{2,1,0:T(8,128)(2,1)S(1)}, bf16[1,768,1024]{2,1,0:T(8,128)(2,1)}, u32[]{:S(2)}) copy-start(bf16[1,768,1024]{2,1,0:T(8,128)(2,1)} %param.7) | copy-start | bytes 4718596
  39.8 31.4 %copy-start.2 = (f32[1,16,768]{2,1,0:T(8,128)S(1)}, f32[1,16,768]{2,1,0:T(8,128)}, u32[]{:S(2)}) copy-start(f32[1,16,768]{2,1,0:T(8,128)} %param.6) | copy-start | bytes 147460
  56.0 11.2 %collective-permute-start.4 = (bf16[32,768]{1,0:T(8,128)(2,1)S(1)}, bf16[32,768]{1,0:T(8,128)(2,1)S(1)}, u32[]{:S(2)}, u32[]{:S(2)}) collective-permute-start(bf16[32,768]{1,0:T(8,128)(2,1)S(1)} %get-tuple-element.39), channel_id=1, source_target_pairs={{0,1},{1,0},{2,3},{3,2},{4,5},{5,4},{6,7},{7,6},{8,9},{9,8},{10,11... | collective-permute-start | bytes 147464 | tf_op jit(solution)/shard_map/ppermute | solution.py:21
  60.1 7.1 %collective-permute-start.5 = (bf16[32,768]{1,0:T(8,128)(2,1)S(1)}, bf16[32,768]{1,0:T(8,128)(2,1)S(1)}, u32[]{:S(2)}, u32[]{:S(2)}) collective-permute-start(bf16[32,768]{1,0:T(8,128)(2,1)S(1)} %get-tuple-element.40), channel_id=1, source_target_pairs={{1,2},{2,1},{3,4},{4,3},{5,6},{6,5},{7,0},{0,7},{9,10},{10,9},{11,... | collective-permute-start | bytes 147464 | tf_op jit(solution)/shard_map/ppermute | solution.py:21
  62.1 9.1 %collective-permute-start.7 = (bf16[32,768]{1,0:T(8,128)(2,1)S(1)}, bf16[32,768]{1,0:T(8,128)(2,1)S(1)}, u32[]{:S(2)}, u32[]{:S(2)}) collective-permute-start(bf16[32,768]{1,0:T(8,128)(2,1)S(1)} %get-tuple-element.41), channel_id=1, source_target_pairs={{8,16},{16,8},{24,32},{32,24},{40,48},{48,40},{56,64},{64,56},{72,... | collective-permute-start | bytes 147464 | tf_op jit(solution)/shard_map/ppermute | solution.py:21
  65.3 5.9 %collective-permute-start.6 = (bf16[32,768]{1,0:T(8,128)(2,1)S(1)}, bf16[32,768]{1,0:T(8,128)(2,1)S(1)}, u32[]{:S(2)}, u32[]{:S(2)}) collective-permute-start(bf16[32,768]{1,0:T(8,128)(2,1)S(1)} %get-tuple-element.41), channel_id=1, source_target_pairs={{0,8},{8,0},{16,24},{24,16},{32,40},{40,32},{48,56},{56,48},{64,72... | collective-permute-start | bytes 147464 | tf_op jit(solution)/shard_map/ppermute | solution.py:21
  71.8 9.1 %collective-permute-start.9 = (bf16[32,768]{1,0:T(8,128)(2,1)S(1)}, bf16[32,768]{1,0:T(8,128)(2,1)S(1)}, u32[]{:S(2)}, u32[]{:S(2)}) collective-permute-start(bf16[32,768]{1,0:T(8,128)(2,1)S(1)} %get-tuple-element.42.v), channel_id=1, source_target_pairs={{8,16},{16,8},{24,32},{32,24},{40,48},{48,40},{56,64},{64,56},{72,... | collective-permute-start | bytes 147464 | tf_op jit(solution)/shard_map/ppermute | solution.py:21
  77.1 5.1 %collective-permute-start.8 = (bf16[32,768]{1,0:T(8,128)(2,1)S(1)}, bf16[32,768]{1,0:T(8,128)(2,1)S(1)}, u32[]{:S(2)}, u32[]{:S(2)}) collective-permute-start(bf16[32,768]{1,0:T(8,128)(2,1)S(1)} %get-tuple-element.42.v), channel_id=1, source_target_pairs={{0,8},{8,0},{16,24},{24,16},{32,40},{40,32},{48,56},{56,48},{64,72... | collective-permute-start | bytes 147464 | tf_op jit(solution)/shard_map/ppermute | solution.py:21
  115.0 6.9 %collective-permute-start.11 = (bf16[16,768]{1,0:T(8,128)(2,1)S(1)}, bf16[16,768]{1,0:T(8,128)(2,1)S(1)}, u32[]{:S(2)}, u32[]{:S(2)}) collective-permute-start(bf16[16,768]{1,0:T(8,128)(2,1)S(1)} %get-tuple-element.51.v), channel_id=1, source_target_pairs={{1,2},{2,1},{3,4},{4,3},{5,6},{6,5},{7,0},{0,7},{9,10},{10,9},{11,... | collective-permute-start | bytes 73736 | tf_op jit(solution)/shard_map/ppermute | solution.py:21
  119.9 3.1 %collective-permute-start.10 = (bf16[16,768]{1,0:T(8,128)(2,1)S(1)}, bf16[16,768]{1,0:T(8,128)(2,1)S(1)}, u32[]{:S(2)}, u32[]{:S(2)}) collective-permute-start(bf16[16,768]{1,0:T(8,128)(2,1)S(1)} %get-tuple-element.51.v), channel_id=1, source_target_pairs={{0,1},{1,0},{2,3},{3,2},{4,5},{5,4},{6,7},{7,6},{8,9},{9,8},{10,11... | collective-permute-start | bytes 73736 | tf_op jit(solution)/shard_map/ppermute | solution.py:21
